TPU v7x, 32 devices: a whole 2x2x4 slice. The times are simulated.
32 devices in a mesh: date: 2 (over y), slab: 16 (over z, x, core).
Axes of the slice: x: 2, y: 2, z: 4, core: 2. Of those that a mesh axis runs over, the one named last changes fastest.
Arguments:
- pressure: float32 [16, 12288], P('slab', 'date'), parts along dimension 1, may hold values from -6 to 6
- density: float32 [16, 12288], P('slab', 'date'), parts along dimension 1, may hold values from -6 to 6
- vertical_wind: float32 [16, 12288], P('slab', 'date'), parts along dimension 1, may hold values from -6 to 6
- horizontal_wind: float32 [2, 16, 12288], P(None, 'slab', 'date'), parts along dimension 2, may hold values from -6 to 6
- metric_terms: float32 [2, 6144], replicated, may hold values from 0.25 to 1
- neighbors: int32 [4, 6144], replicated, may hold values from 0 to 6143, as said below
- level_order: int32 [16], replicated, may hold values from 0 to 15, each once
- stiffness: float32 [16], replicated, may hold values from 0.2 to 5
- coupling: float32 [16], replicated, may hold values from 0.2 to 1
- weight_one: bfloat16 [64, 512], P('slab'), may hold values from -0.75 to 0.75
- weight_two: bfloat16 [512, 512], P('slab'), may hold values from -0.25 to 0.25
- weight_three: bfloat16 [512, 16], P('slab'), may hold values from -0.25 to 0.25
- pressure_adjoint: float32 [16, 12288], P('slab', 'date'), parts along dimension 1, may hold values from -6 to 6
- wind_adjoint: float32 [16, 12288], P('slab', 'date'), parts along dimension 1, may hold values from -6 to 6
Outputs:
- pressure_new: float32 [16, 12288], P('slab', 'date'), parts along dimension 1
- wind_new: float32 [16, 12288], P('slab', 'date'), parts along dimension 1
- pressure_grad: float32 [16, 12288], P('slab', 'date'), parts along dimension 1
- first_grad: float32 [128, 512], P(('date', 'slab')), parts along dimension 0
- second_grad: float32 [1024, 512], P(('date', 'slab')), parts along dimension 0
- third_grad: float32 [1024, 16], P(('date', 'slab')), parts along dimension 0
There are 2 independent parts, one for each index of `date`. A program takes and returns all parts, laid end to end along the dimension named above; an argument that names none is the same for every part. Nothing has to cross between parts.
Inputs may be any that keep to these rules, and one draw needn't show every extreme that they name: `neighbors`: the columns are the cells of a 8 x 768 grid stored in some order; rows 0, 1, 2, 3 give the stored positions of a column's east, west, north and south neighbours, and the column itself where the grid's edge lies on that side. `level_order`: each level appears once.
All inputs are finite; a program needn't handle non-finite values.
Results may differ from a plain program's by a relative error of at most 0.0075.
Values may be sent and summed in bfloat16 or wider, within the bound.
No kernel may reach another device: no remote copies, remote signals or barrier semaphores. Data moves between devices by JAX's collectives and lax.ppermute only.
A program may use at most 128 MiB of HBM per device.

v0:
```python
import math

import jax
import jax.numpy as jnp
from jax import lax
from jax.sharding import PartitionSpec as P


def lower_diff(field):
    return jnp.concatenate([field[1:] - field[:-1], -field[-1:]], axis=0)


def upper_diff(field):
    return jnp.concatenate([jnp.zeros_like(field[:1]), field[:-1]], axis=0) - field


def level_inverse(stiffness):
    below = jnp.concatenate([jnp.zeros((1,), jnp.float32), stiffness[:-1]])
    matrix = (
        jnp.diag(1.0 + stiffness + below)
        - jnp.diag(stiffness[:-1], 1)
        - jnp.diag(stiffness[:-1], -1)
    )
    factor = jnp.linalg.cholesky(matrix)
    identity = jnp.eye(stiffness.shape[0], dtype=jnp.float32)
    return jax.scipy.linalg.cho_solve((factor, True), identity)


def apply_inverse(inverse_matrix, rhs):
    return jnp.dot(
        inverse_matrix, rhs, precision=lax.Precision.HIGHEST, preferred_element_type=jnp.float32
    )


def contract_first(left, right):
    return lax.dot_general(
        left, right, (((0,), (0,)), ((), ())), preferred_element_type=jnp.float32
    )


def contract_last(left, right):
    return lax.dot_general(
        left, right, (((1,), (1,)), ((), ())), preferred_element_type=jnp.float32
    )


def body(
    pressure,
    density,
    vertical_wind,
    horizontal_wind,
    metric_terms,
    neighbors,
    level_order,
    stiffness,
    coupling,
    weight_one,
    weight_two,
    weight_three,
    pressure_adjoint,
    wind_adjoint,
):
    east = jnp.take(horizontal_wind[0], neighbors[0], axis=1)
    west = jnp.take(horizontal_wind[0], neighbors[1], axis=1)
    north = jnp.take(horizontal_wind[1], neighbors[2], axis=1)
    south = jnp.take(horizontal_wind[1], neighbors[3], axis=1)
    diverg = metric_terms[0] * (east - west) + metric_terms[1] * (north - south)
    star = pressure - diverg
    inverse = jnp.argsort(level_order)
    scale = 1.0 / math.sqrt(neighbors.shape[1])
    forward_raw = lax.all_to_all(
        jnp.stack([star, density, vertical_wind, diverg]).astype(jnp.bfloat16),
        "slab",
        split_axis=2,
        concat_axis=1,
        tiled=True,
    ).astype(jnp.float32)
    full_one, full_two, full_three = (
        lax.all_gather(weight_one, "slab", axis=0, tiled=True),
        lax.all_gather(weight_two, "slab", axis=0, tiled=True),
        lax.all_gather(weight_three, "slab", axis=0, tiled=True),
    )
    forward_part = jnp.take(forward_raw, inverse, axis=1)
    levels = forward_part.shape[1]
    width = forward_part.shape[2]
    couple = coupling[:, None]
    column_input = forward_part.reshape(4 * levels, width).astype(jnp.bfloat16)
    pre_one = contract_first(full_one, column_input)
    tanh_one = jnp.tanh(pre_one)
    act_one = tanh_one.astype(jnp.bfloat16)
    pre_two = contract_first(full_two, act_one)
    tanh_two = jnp.tanh(pre_two)
    act_two = tanh_two.astype(jnp.bfloat16)
    heating = contract_first(full_three, act_two)
    star_column = forward_part[0]
    rhs = forward_part[2] - couple * lower_diff(star_column) - 0.5 * forward_part[1] + heating
    inverse_matrix = level_inverse(stiffness)
    wind_next = apply_inverse(inverse_matrix, rhs)
    press_next = star_column + upper_diff(couple * wind_next)
    forward_slabs = lax.all_to_all(
        jnp.take(jnp.stack([press_next, wind_next]), level_order, axis=1).astype(jnp.bfloat16),
        "slab",
        split_axis=1,
        concat_axis=2,
        tiled=True,
    ).astype(jnp.float32)
    adjoint_raw = lax.all_to_all(
        jnp.stack([pressure_adjoint, wind_adjoint]), "slab", split_axis=2, concat_axis=1, tiled=True
    )
    adjoint_part = jnp.take(adjoint_raw, inverse, axis=1)
    wind_grad = adjoint_part[1] + couple * lower_diff(adjoint_part[0])
    rhs_grad = apply_inverse(inverse_matrix, wind_grad)
    star_grad = adjoint_part[0] - upper_diff(couple * rhs_grad)
    heat_grad = rhs_grad.astype(jnp.bfloat16)
    local_three = contract_last(act_two, heat_grad) * scale
    back_two = jnp.dot(full_three, heat_grad, preferred_element_type=jnp.float32)
    pre_two_grad = (back_two * (1.0 - tanh_two * tanh_two)).astype(jnp.bfloat16)
    local_two = contract_last(act_one, pre_two_grad) * scale
    back_one = jnp.dot(full_two, pre_two_grad, preferred_element_type=jnp.float32)
    pre_one_grad = (back_one * (1.0 - tanh_one * tanh_one)).astype(jnp.bfloat16)
    local_one = contract_last(column_input, pre_one_grad) * scale
    first_grad, second_grad, third_grad = (
        lax.psum_scatter(local_one, "slab", scatter_dimension=0, tiled=True),
        lax.psum_scatter(local_two, "slab", scatter_dimension=0, tiled=True),
        lax.psum_scatter(local_three, "slab", scatter_dimension=0, tiled=True),
    )
    input_grad = jnp.dot(full_one, pre_one_grad, preferred_element_type=jnp.float32)
    star_grad = star_grad + input_grad[:levels]
    stored_grad = jnp.take(star_grad, level_order, axis=0)
    pressure_new = forward_slabs[0]
    wind_new = forward_slabs[1]
    pressure_grad = lax.all_to_all(
        stored_grad[None].astype(jnp.bfloat16), "slab", split_axis=1, concat_axis=2, tiled=True
    ).astype(jnp.float32)[0]
    return (pressure_new, wind_new, pressure_grad, first_grad, second_grad, third_grad)


def solution(mesh):
    in_specs = (
        P("slab", "date"),
        P("slab", "date"),
        P("slab", "date"),
        P(None, "slab", "date"),
        P(),
        P(),
        P(),
        P(),
        P(),
        P("slab", None),
        P("slab", None),
        P("slab", None),
        P("slab", "date"),
        P("slab", "date"),
    )
    out_specs = (
        P("slab", "date"),
        P("slab", "date"),
        P("slab", "date"),
        P(("date", "slab"), None),
        P(("date", "slab"), None),
        P(("date", "slab"), None),
    )
    return jax.shard_map(body, mesh=mesh, in_specs=in_specs, out_specs=out_specs, check_vma=False)
```

profile of v0, /device:TPU:0, one launch (start us, length us, event | category | flops | bytes accessed | tf_op | source)
XLA Modules:
  0.0 540.4 jit_solution(8033137742579381662)
XLA Ops:
  9.1 34.3 %gather_fusion.4 = f32[6144]{0:T(1024)S(1)} fusion(f32[6144]{0:T(1024)S(1)} %bitcast.140, s32[6144]{0:T(1024)S(1)} %fusion.25), kind=kCustom, calls=%fused_computation.3.clone | custom fusion | bytes 73728 | tf_op jit(solution)/shard_map/jit(_take)/gather | solution.py:65
  43.5 34.3 %gather_fusion.5 = f32[6144]{0:T(1024)S(1)} fusion(f32[6144]{0:T(1024)S(1)} %bitcast.141, s32[6144]{0:T(1024)S(1)} %fusion.26), kind=kCustom, calls=%fused_computation.4.clone | custom fusion | bytes 73728 | tf_op jit(solution)/shard_map/jit(_take)/gather | solution.py:66
  77.8 34.3 %gather_fusion.2 = f32[6144]{0:T(1024)S(1)} fusion(f32[6144]{0:T(1024)S(1)} %bitcast.138, s32[6144]{0:T(1024)S(1)} %fusion.23), kind=kCustom, calls=%fused_computation.clone | custom fusion | bytes 73728 | tf_op jit(solution)/shard_map/jit(_take)/gather | solution.py:63
  112.2 34.3 %gather_fusion.3 = f32[6144]{0:T(1024)S(1)} fusion(f32[6144]{0:T(1024)S(1)} %bitcast.139, s32[6144]{0:T(1024)S(1)} %fusion.24), kind=kCustom, calls=%fused_computation.2.clone | custom fusion | bytes 73728 | tf_op jit(solution)/shard_map/jit(_take)/gather | solution.py:64
  146.9 4.0 copy.50
  151.5 34.5 %reduce.6 = bf16[6144,4]{1,0:T(8,128)(2,1)} reduce(bf16[6144,1,4]{2,1,0:T(2,128)(2,1)S(1)} %bitcast.142, bf16[]{:T(256)} %broadcast.246), dimensions={1}, to_apply=%bitcast.107.reduce_sub_computation | reduce | bytes 98306
  186.0 4.4 reshape.350
  190.4 7.4 %all-to-all-start = ((bf16[16,2,768]{2,1,0:T(2,128)(2,1)}), bf16[16,2,768]{2,1,0:T(2,128)(2,1)S(1)}, u32[]{:S(2)}, u32[]{:S(2)}) async-start(bf16[16,2,768]{2,1,0:T(2,128)(2,1)} %reshape.350), calls=%async_computation | async-start | bytes 98304 | tf_op jit(solution)/shard_map/all_to_all | solution.py:71
  197.8 1.2 sort.17
  199.2 21.9 %all-gather = bf16[16,4,512]{2,1,0:T(4,128)(2,1)S(1)} all-gather(bf16[1,4,512]{2,1,0:T(4,128)(2,1)S(1)} %bitcast.168), channel_id=1, replica_groups=mesh['date'=2,'slab'=16] {'slab'}, dimensions={0}, use_global_device_ids=true | all-gather | bytes 69632 | tf_op jit(solution)/shard_map/all_gather | solution.py:79
  221.1 20.3 %all_gather.10 = bf16[512,512]{1,0:T(8,128)(2,1)} all-gather(bf16[32,512]{1,0:T(8,128)(2,1)S(1)} %copy-done.2), channel_id=1, replica_groups=mesh['date'=2,'slab'=16] {'slab'}, dimensions={0}, use_global_device_ids=true | all-gather | bytes 557056 | tf_op jit(solution)/shard_map/all_gather | solution.py:80
  241.4 19.3 %all-gather.1 = bf16[16,32,16]{1,2,0:T(8,128)(2,1)S(1)} all-gather(bf16[1,32,16]{1,2,0:T(8,128)(2,1)S(1)} %bitcast.169), channel_id=1, replica_groups=mesh['date'=2,'slab'=16] {'slab'}, dimensions={0}, use_global_device_ids=true | all-gather | bytes 17408 | tf_op jit(solution)/shard_map/all_gather | solution.py:81
  261.0 1.4 cholesky.17
  263.8 1.2 custom-call.10
  265.4 3.3 copy.56
  269.2 28.4 %reduce.7 = f32[6144,2]{1,0:T(8,128)} reduce(f32[6144,1,2]{2,1,0:T(1,128)S(1)} %bitcast.143, f32[]{:T(128)} %broadcast.247), dimensions={1}, to_apply=%bitcast.109.reduce_sub_computation | reduce | bytes 98308
  297.6 4.3 reshape.352
  302.0 3.5 all-to-all-start.2
  305.7 4.0 reshape.351
  309.7 2.9 copy.51
  314.2 4.5 reshape.353
  321.0 1.4 convolution_tanh_fusion
  325.8 1.4 convolution_multiply_fusion
  329.7 6.0 %all-to-all-start.3 = ((bf16[16,2,192]{2,1,0:T(2,128)(2,1)}), bf16[16,2,192]{2,1,0:T(2,128)(2,1)S(1)}, u32[]{:S(2)}, u32[]{:S(2)}) async-start(bf16[16,2,192]{2,1,0:T(2,128)(2,1)} %reshape.354), calls=%async_computation.3 | async-start | bytes 32768 | tf_op jit(solution)/shard_map/all_to_all | solution.py:132
  337.0 5.1 all-to-all-done.3
  342.2 3.5 all-to-all-start.1
  347.7 4.5 all-to-all-done.1
  352.8 28.3 %reduce-scatter.7.cloned.1.call-done = f32[32,16]{1,0:T(8,128)} async-done(((f32[512,16]{1,0:T(8,128)}), f32[32,16]{1,0:T(8,128)}) %reduce-scatter.7.cloned.1.call-update) | async-done | bytes 2064
  381.1 1.4 copy.64
  382.5 88.1 %all-reduce.6.cloned.1.call-done = f32[64,512]{1,0:T(8,128)} async-done(((f32[64,512]{1,0:T(8,128)}), f32[64,512]{1,0:T(8,128)}) %all-reduce.6.cloned.1.call-update) | async-done | bytes 131088
  470.6 1.3 constant_dynamic-slice_fusion
  472.0 61.9 %reduce-scatter.5.cloned.1.call-done = f32[32,512]{1,0:T(8,128)} async-done(((f32[512,512]{1,0:T(8,128)}), f32[32,512]{1,0:T(8,128)}) %reduce-scatter.5.cloned.1.call-update) | async-done | bytes 65552 | tf_op jit(solution)/shard_map/reduce_scatter | solution.py:124
  (113 shorter events, 18.7 us)
Async XLA Ops:
  112.1 34.4 %copy-start.4 = (f32[1,6144]{1,0:T(1,128)S(1)}, f32[1,6144]{1,0:T(1,128)}, u32[]{:S(2)}) copy-start(f32[1,6144]{1,0:T(1,128)} %param.19) | copy-start | bytes 73732
  112.1 34.4 %copy-start.1 = (f32[2,6144]{1,0:T(2,128)S(1)}, f32[2,6144]{1,0:T(2,128)}, u32[]{:S(2)}) copy-start(f32[2,6144]{1,0:T(2,128)} %param.22) | copy-start | bytes 147460
  112.1 34.4 %copy-start.3 = (f32[1,6144]{1,0:T(1,128)S(1)}, f32[1,6144]{1,0:T(1,128)}, u32[]{:S(2)}) copy-start(f32[1,6144]{1,0:T(1,128)} %param.18) | copy-start | bytes 73732
  112.1 34.5 %copy-start.5 = (f32[1,6144]{1,0:T(1,128)S(1)}, f32[1,6144]{1,0:T(1,128)}, u32[]{:S(2)}) copy-start(f32[1,6144]{1,0:T(1,128)} %param.20) | copy-start | bytes 73732
  151.4 46.3 %copy-start.13 = (s32[16]{0:T(128)S(1)}, s32[16]{0:T(128)}, u32[]{:S(2)}) copy-start(s32[16]{0:T(128)} %param.24) | copy-start | bytes 196
  151.5 47.7 %copy-start.8 = (bf16[4,512]{1,0:T(4,128)(2,1)S(1)}, bf16[4,512]{1,0:T(4,128)(2,1)}, u32[]{:S(2)}) copy-start(bf16[4,512]{1,0:T(4,128)(2,1)} %param.27) | copy-start | bytes 12292
  151.5 69.6 %copy-start.2 = (bf16[32,512]{1,0:T(8,128)(2,1)S(1)}, bf16[32,512]{1,0:T(8,128)(2,1)}, u32[]{:S(2)}) copy-start(bf16[32,512]{1,0:T(8,128)(2,1)} %param.28) | copy-start | bytes 98308
  151.5 89.9 %copy-start.9 = (bf16[32,16]{0,1:T(8,128)(2,1)S(1)}, bf16[32,16]{0,1:T(8,128)(2,1)}, u32[]{:S(2)}) copy-start(bf16[32,16]{0,1:T(8,128)(2,1)} %param.29) | copy-start | bytes 3076
  151.5 109.3 %copy-start.10 = (f32[16]{0:T(128)S(1)}, f32[16]{0:T(128)}, u32[]{:S(2)}) copy-start(f32[16]{0:T(128)} %param.25) | copy-start | bytes 196
  151.5 109.3 %copy-start.12 = (pred[16]{0:T(512)(128)(4,1)S(1)}, pred[16]{0:T(512)(128)(4,1)}, u32[]{:S(2)}) copy-start(pred[16]{0:T(512)(128)(4,1)} %constant.116.clone.1) | copy-start | bytes 52
  151.5 113.9 %copy-start.6 = (f32[1,6144]{1,0:T(1,128)S(1)}, f32[1,6144]{1,0:T(1,128)}, u32[]{:S(2)}) copy-start(f32[1,6144]{1,0:T(1,128)} %param.31) | copy-start | bytes 73732
  151.5 113.9 %copy-start.7 = (f32[1,6144]{1,0:T(1,128)S(1)}, f32[1,6144]{1,0:T(1,128)}, u32[]{:S(2)}) copy-start(f32[1,6144]{1,0:T(1,128)} %param.30) | copy-start | bytes 73732
  190.4 111.6 %all-to-all-start = ((bf16[16,2,768]{2,1,0:T(2,128)(2,1)}), bf16[16,2,768]{2,1,0:T(2,128)(2,1)S(1)}, u32[]{:S(2)}, u32[]{:S(2)}) async-start(bf16[16,2,768]{2,1,0:T(2,128)(2,1)} %reshape.350), calls=%async_computation | async-start | bytes 98304 | tf_op jit(solution)/shard_map/all_to_all | solution.py:71
  302.0 11.4 %all-to-all-start.2 = ((f32[16,1,768]{2,1,0:T(1,128)}), f32[16,1,768]{2,1,0:T(1,128)S(1)}, u32[]{:S(2)}, u32[]{:S(2)}) async-start(f32[16,1,768]{2,1,0:T(1,128)} %reshape.352), calls=%async_computation.2 | async-start | bytes 98304 | tf_op jit(solution)/shard_map/all_to_all | solution.py:107
  305.5 75.7 %reduce-scatter.7.cloned.1.call-start = ((), (), s32[]{:S(2)}) async-start(), calls=%async_computation.7 | async-start | bytes 278528
  318.7 3.7 copy-start.11
  320.7 3.8 copy-start
  324.4 146.2 %all-reduce.6.cloned.1.call-start = ((), (), s32[]{:S(2)}) async-start(), calls=%async_computation.8 | async-start | bytes 262144
  324.9 20.8 %copy-start.14 = (u32[32]{0:T(128)S(1)}, u32[32]{0:T(128)}, u32[]{:S(2)}) copy-start(u32[32]{0:T(128)} %constant.136) | copy-start | bytes 388
  325.8 208.2 %reduce-scatter.5.cloned.1.call-start = ((), (), s32[]{:S(2)}) async-start(), calls=%async_computation.6 | async-start | bytes 1114112 | tf_op jit(solution)/shard_map/reduce_scatter | solution.py:124
  329.7 12.5 %all-to-all-start.3 = ((bf16[16,2,192]{2,1,0:T(2,128)(2,1)}), bf16[16,2,192]{2,1,0:T(2,128)(2,1)S(1)}, u32[]{:S(2)}, u32[]{:S(2)}) async-start(bf16[16,2,192]{2,1,0:T(2,128)(2,1)} %reshape.354), calls=%async_computation.3 | async-start | bytes 32768 | tf_op jit(solution)/shard_map/all_to_all | solution.py:132
  342.2 10.0 %all-to-all-start.1 = ((bf16[2,16,384]{2,0,1:T(2,128)(2,1)}), bf16[2,16,384]{2,0,1:T(2,128)(2,1)S(1)}, u32[]{:S(2)}, u32[]{:S(2)}) async-start(bf16[2,16,384]{2,0,1:T(2,128)(2,1)} %bitcast_convert_fusion), calls=%async_computation.1 | async-start | bytes 49152 | tf_op jit(solution)/shard_map/all_to_all | solution.py:100
Sparse Core Ops, SparseCore 0:
  324.5 56.5 reduce-scatter.6
  384.6 86.0 all-reduce.5
  474.8 59.0 reduce-scatter.4
where the time goes:
time: 541 us; the launch traced here: 540 us
  waiting for transfers between devices  188 us (35%)
  local copies, waits for them, and re-layouts  177 us (33%)
  other arithmetic  72 us (13%)
  blocking collectives  61.4 us (11%)
  starting transfers between devices  20.7 us (4%)
  between operations  15 us (3%)
  matrix products  6.09 us (1%)
    unnamed x5, waiting for transfers between devices  116 us
    unnamed x3, other arithmetic  63.6 us
    reduce_scatter x1, waiting for transfers between devices, body(): lax.psum_scatter(local_two, 'slab', scatter_dimension=0, tiled=True)  61.9 us
    gather x1, local copies, waits for them, and re-layouts, body(): south = jnp.take(horizontal_wind[1], neighbors[3], axis=1)  34.3 us
    gather x1, local copies, waits for them, and re-layouts, body(): east = jnp.take(horizontal_wind[0], neighbors[0], axis=1)  34.3 us
    gather x1, local copies, waits for them, and re-layouts, body(): west = jnp.take(horizontal_wind[0], neighbors[1], axis=1)  34.3 us
    gather x1, local copies, waits for them, and re-layouts, body(): north = jnp.take(horizontal_wind[1], neighbors[2], axis=1)  34.3 us
    unnamed x44, local copies, waits for them, and re-layouts  23.4 us
  transfers between devices with their start and end apart: 7, of which 5 were waited for; matrix products, arithmetic and copies ran while one was open for 11% of the time, Pallas kernels for 0%

commit v1 on v0

--- a/solution.py
+++ b/solution.py
@@ -1,8 +1,11 @@
+import functools
 import math
 
 import jax
 import jax.numpy as jnp
 from jax import lax
+from jax.experimental import pallas as pl
+from jax.experimental.pallas import tpu as pltpu
 from jax.sharding import PartitionSpec as P
 
 
@@ -135,6 +138,344 @@
     return (pressure_new, wind_new, pressure_grad, first_grad, second_grad, third_grad)
 
 
+LANE = 128
+SUB = 8
+
+
+def spec():
+    return pl.BlockSpec(memory_space=pltpu.VMEM)
+
+
+def call(kernel, outs, n_in, scratch=(), name=None):
+    return pl.pallas_call(
+        kernel,
+        out_shape=outs,
+        in_specs=[spec() for _ in range(n_in)],
+        out_specs=jax.tree.map(lambda _: spec(), outs),
+        scratch_shapes=list(scratch),
+        compiler_params=pltpu.CompilerParams(vmem_limit_bytes=48 << 20),
+        name=name,
+    )
+
+
+def shape(dims, kind):
+    return jax.ShapeDtypeStruct(dims, kind)
+
+
+def pack_weights_kernel(one_ref, two_ref, three_ref, out_ref, part_ref):
+    group = lax.axis_index("slab") % 4
+    devices = out_ref.shape[0]
+    rows, lanes = lax.broadcasted_iota(jnp.int32, (32, LANE), 0), lax.broadcasted_iota(jnp.int32, (32, LANE), 1)
+    place = (lanes == rows + 32 * group).astype(jnp.float32).astype(jnp.bfloat16)
+    three = jnp.dot(three_ref[...], place, preferred_element_type=jnp.float32)
+    one = one_ref[...].astype(jnp.float32)
+    for half in range(2):
+        for c in range(4):
+            part_ref[2 * c : 2 * c + 2, :] = one[2 * half : 2 * half + 2, LANE * c : LANE * (c + 1)]
+        part_ref[8:16, :] = three[8 * half : 8 * half + 8, :]
+        part = part_ref[...].astype(jnp.bfloat16)
+        for c in range(4):
+            block = two_ref[16 * half : 16 * half + 16, LANE * c : LANE * (c + 1)]
+            for d in range(half, devices, 2):
+                out_ref[d, 16 * c : 16 * c + 16, :] = block
+        for d in range(half, devices, 2):
+            out_ref[d, 64:80, :] = part
+
+
+def gather_pair(table, first_index, second_index, first_ref, second_ref):
+    rows = table.shape[0]
+    count = first_index.shape[0] // SUB
+    parts = []
+    for index in (first_index, second_index):
+        for v in range(count):
+            block = index[SUB * v : SUB * v + SUB, :]
+            parts.append((block >> 7, block & (LANE - 1)))
+    totals = [jnp.zeros((SUB, LANE), jnp.float32) for _ in parts]
+    for h in range(rows):
+        row = jnp.broadcast_to(table[h : h + 1, :], (SUB, LANE))
+        for i, (high, low) in enumerate(parts):
+            picked = jnp.take_along_axis(row, low, axis=1, mode="promise_in_bounds")
+            totals[i] = jnp.where(high == h, picked, totals[i])
+    return totals[:count], totals[count:]
+
+
+def pack_fields_kernel(p_ref, d_ref, w_ref, u_ref, m_ref, n_ref, pa_ref, wa_ref, out_ref, f_ref):
+    blocks = p_ref.shape[0] // SUB
+    stride = out_ref.shape[1]
+    east, west = gather_pair(u_ref.at[0], n_ref[:, 0, :], n_ref[:, 1, :], None, None)
+    north, south = gather_pair(u_ref.at[1], n_ref[:, 2, :], n_ref[:, 3, :], None, None)
+    for j in range(blocks):
+        rows = slice(SUB * j, SUB * j + SUB)
+        diverg = m_ref[rows, 0, :] * (east[j] - west[j]) + m_ref[rows, 1, :] * (north[j] - south[j])
+        fields = (p_ref[rows, :] - diverg, d_ref[rows, :], w_ref[rows, :], diverg, pa_ref[rows, :], wa_ref[rows, :])
+        for f, field in enumerate(fields):
+            f_ref[pl.ds(blocks * f + j, SUB, stride=stride), :] = field
+    for k in range(6 * blocks, stride):
+        f_ref[pl.ds(k, SUB, stride=stride), :] = jnp.zeros((SUB, LANE), jnp.float32)
+    for c in range(SUB):
+        block = f_ref[stride * c : stride * (c + 1), :].astype(jnp.bfloat16)
+        out_ref[2 * c] = block
+        out_ref[2 * c + 1] = block
+
+
+def unpack_weights_kernel(mine_ref, other_ref, w1t_ref, w1s_ref, w2_ref, w2t_ref, w3t_ref, w3_ref, a_ref, b_ref, one_ref):
+    core = lax.axis_index("slab") % 2
+    devices = mine_ref.shape[0]
+    for s in range(devices):
+        for c in range(4):
+            cols = slice(LANE * c, LANE * (c + 1))
+            w2_ref[pl.ds(pl.multiple_of(32 * s + 16 * core, 16), 16), cols] = mine_ref[s, 16 * c : 16 * c + 16, :]
+            w2_ref[pl.ds(pl.multiple_of(32 * s + 16 * (1 - core), 16), 16), cols] = other_ref[s, 16 * c : 16 * c + 16, :]
+        a_ref[16 * s : 16 * s + 16, :] = mine_ref[s, 64:80, :].astype(jnp.float32)
+        b_ref[16 * s : 16 * s + 16, :] = other_ref[s, 64:80, :].astype(jnp.float32)
+    first = core == 0
+    for c in range(4):
+        for r in range(2):
+            a = a_ref[pl.ds(2 * c + r, devices, stride=16), :]
+            b = b_ref[pl.ds(2 * c + r, devices, stride=16), :]
+            one_ref[pl.ds(4 * devices * c + r, devices, stride=4), :] = jnp.where(first, a, b)
+            one_ref[pl.ds(4 * devices * c + 2 + r, devices, stride=4), :] = jnp.where(first, b, a)
+    three = []
+    for t in range(4):
+        a = sum(a_ref[16 * s + 8 : 16 * s + 16, :] for s in range(4 * t, 4 * t + 4))
+        b = sum(b_ref[16 * s + 8 : 16 * s + 16, :] for s in range(4 * t, 4 * t + 4))
+        three.append(jnp.concatenate([jnp.where(first, a, b), jnp.where(first, b, a)], axis=0))
+    three = jnp.concatenate(three, axis=1)
+    w3t_ref[...] = three.astype(jnp.bfloat16)
+    w3_ref[...] = three.T.astype(jnp.bfloat16)
+    one = jnp.concatenate([one_ref[4 * devices * c : 4 * devices * (c + 1), :] for c in range(4)], axis=1)
+    w1t_ref[...] = one.T.astype(jnp.bfloat16)
+    w1s_ref[...] = one[: w1s_ref.shape[0], :].astype(jnp.bfloat16)
+    w2t_ref[...] = w2_ref[...].T
+
+
+def shifted_up(field, rows):
+    return jnp.where(rows < field.shape[0] - 1, pltpu.roll(field, field.shape[0] - 1, 0), 0.0)
+
+
+def shifted_down(field, rows):
+    return jnp.where(rows > 0, pltpu.roll(field, 1, 0), 0.0)
+
+
+def operator_inverse(stiff, rows):
+    size = stiff.shape[0]
+    below = shifted_down(stiff, rows)
+    lower, diagonal = -below, 1.0 + stiff + below
+    upper = jnp.where(rows < size - 1, -stiff, 0.0)
+    right = (rows == lax.broadcasted_iota(jnp.int32, (size, size), 1)).astype(jnp.float32)
+    distance = 1
+    while distance < size:
+        down = lambda v: pltpu.roll(v, distance, 0)
+        up = lambda v: pltpu.roll(v, size - distance, 0)
+        alpha, gamma = -lower / down(diagonal), -upper / up(diagonal)
+        right = right + alpha * down(right) + gamma * up(right)
+        diagonal = diagonal + alpha * down(upper) + gamma * up(lower)
+        lower, upper = alpha * down(lower), gamma * up(upper)
+        distance *= 2
+    return right / diagonal
+
+
+def column_kernel(
+    f_ref, w1t_ref, w1s_ref, w2_ref, w2t_ref, w3t_ref, w3_ref, order_ref, stiff_ref, couple_ref, out_ref,
+    x_ref, y_ref, one_ref, act_ref, sel_ref,
+):
+    core = lax.axis_index("slab") % 2
+    levels, stride = f_ref.shape[0], f_ref.shape[1]
+    width = act_ref.shape[1]
+    blocks = width // LANE
+    chips = out_ref.shape[0]
+    f32, bf16 = jnp.float32, jnp.bfloat16
+    for s in range(levels):
+        x_ref[stride * s : stride * (s + 1), :] = f_ref[s].astype(f32)
+    raw = jnp.concatenate([x_ref[pl.ds(k, levels, stride=stride), :] for k in range(6 * blocks)], axis=1).astype(bf16)
+    square_rows = lax.broadcasted_iota(jnp.int32, (levels, levels), 0)
+    square_cols = lax.broadcasted_iota(jnp.int32, (levels, levels), 1)
+    place = (order_ref[...] == square_rows).astype(f32).astype(bf16)
+    ordered = jnp.dot(place, raw, preferred_element_type=f32)
+    star, density, vertical, diverg, pressure_adjoint, wind_adjoint = (
+        ordered[:, width * i : width * (i + 1)] for i in range(6)
+    )
+    diagonal = square_rows == square_cols
+    stiff = jnp.sum(jnp.where(diagonal, stiff_ref[...], 0.0), axis=1, keepdims=True)
+    couple = jnp.sum(jnp.where(diagonal, couple_ref[...], 0.0), axis=1, keepdims=True)
+    inverse = operator_inverse(jnp.broadcast_to(stiff, (levels, levels)), square_rows)
+    couple = jnp.broadcast_to(couple, (levels, width))
+    rows = lax.broadcasted_iota(jnp.int32, (levels, width), 0)
+
+    def solve(right):
+        return jnp.dot(inverse, right, precision=lax.Precision.HIGHEST, preferred_element_type=f32)
+
+    def lower(field):
+        return shifted_up(field, rows) - field
+
+    def upper(field):
+        return shifted_down(field, rows) - field
+
+    rhs_grad = solve(wind_adjoint + couple * lower(pressure_adjoint))
+    star_part = pressure_adjoint - upper(couple * rhs_grad)
+    heat_grad = rhs_grad.astype(bf16)
+    column_input = jnp.concatenate([star, density, vertical, diverg], axis=0).astype(bf16)
+    tanh_one = jnp.tanh(jnp.dot(w1t_ref[...], column_input, preferred_element_type=f32))
+    act_one = tanh_one.astype(bf16)
+    act_ref[...] = act_one
+    tanh_two = jnp.tanh(jnp.dot(w2t_ref[...], act_one, preferred_element_type=f32))
+    act_two = tanh_two.astype(bf16)
+    heating = jnp.dot(w3t_ref[...], act_two, preferred_element_type=f32)
+    wind_next = solve(vertical - couple * lower(star) - 0.5 * density + heating)
+    press_next = star + upper(couple * wind_next)
+    back_two = jnp.dot(w3_ref[...], heat_grad, preferred_element_type=f32)
+    pre_two_grad = (back_two * (1.0 - tanh_two * tanh_two)).astype(bf16)
+    back_one = jnp.dot(w2_ref[...], pre_two_grad, preferred_element_type=f32)
+    pre_one_grad = (back_one * (1.0 - tanh_one * tanh_one)).astype(bf16)
+    star_grad = star_part + jnp.dot(w1s_ref[...], pre_one_grad, preferred_element_type=f32)
+    for c in range(chips):
+        sel_ref[32 * c : 32 * c + 32, :] = act_ref[pl.ds(pl.multiple_of(64 * c + 32 * core, 32), 32), :]
+    local_two = contract_last(sel_ref[...], pre_two_grad)
+    local_three = contract_last(heat_grad, act_two)
+    local_one = contract_last(column_input, pre_one_grad)
+    first = core == 0
+    for c in range(chips):
+        mine = jnp.where(first, local_one[8 * c : 8 * c + 4, :], local_one[8 * c + 4 : 8 * c + 8, :])
+        for q in range(4):
+            cols = slice(LANE * q, LANE * (q + 1))
+            out_ref[c, 32 * q : 32 * q + 32, :] = local_two[32 * c : 32 * c + 32, cols].astype(bf16)
+            one_ref[4 * q : 4 * q + 4, :] = mine[:, cols]
+        out_ref[c, 128:144, :] = one_ref[...].astype(bf16)
+        out_ref[c, 144:160, :] = local_three[:, LANE * (c // 2) : LANE * (c // 2 + 1)].astype(bf16)
+    fields = jnp.concatenate([press_next, wind_next, star_grad], axis=1).astype(bf16)
+    stored = lax.dot_general(place, fields, (((0,), (0,)), ((), ())), preferred_element_type=f32)
+    back = y_ref.shape[0] // levels
+    for k in range(3 * blocks):
+        y_ref[pl.ds(k, levels, stride=back), :] = stored[:, LANE * k : LANE * (k + 1)]
+    for k in range(3 * blocks, back):
+        y_ref[pl.ds(k, levels, stride=back), :] = jnp.zeros((levels, LANE), f32)
+    for c in range(chips):
+        out_ref[c, 160 : 160 + back, :] = y_ref[pl.ds(pl.multiple_of(back * (2 * c + core), 8), back), :].astype(bf16)
+
+
+def finish_kernel(scale, r_ref, p_ref, w_ref, g_ref, one_ref, two_ref, three_ref, y_ref):
+    chips = r_ref.shape[0]
+    back = r_ref.shape[1] - 160
+    blocks = p_ref.shape[0] // chips
+    group = lax.axis_index("slab") % 4
+
+    def total(start, stop):
+        return sum(r_ref[c, start:stop, :].astype(jnp.float32) for c in range(chips)) * scale
+
+    for q in range(4):
+        two_ref[:, LANE * q : LANE * (q + 1)] = total(32 * q, 32 * q + 32)
+    one = total(128, 144)
+    for q in range(4):
+        one_ref[:, LANE * q : LANE * (q + 1)] = one[4 * q : 4 * q + 4, :]
+    three = total(144, 160)
+    picked = three[:, 0:32]
+    for q in range(1, 4):
+        picked = jnp.where(group == q, three[:, 32 * q : 32 * q + 32], picked)
+    three_ref[...] = picked
+    for c in range(chips):
+        y_ref[back * c : back * (c + 1), :] = r_ref[c, 160 : 160 + back, :].astype(jnp.float32)
+    for f, ref in enumerate((p_ref, w_ref, g_ref)):
+        for j in range(blocks):
+            ref[chips * j : chips * (j + 1), :] = y_ref[pl.ds(blocks * f + j, chips, stride=back), :]
+
+
+def fast_body(
+    pressure, density, vertical_wind, horizontal_wind, metric_terms, neighbors, level_order, stiffness, coupling,
+    weight_one, weight_two, weight_three, pressure_adjoint, wind_adjoint,
+):
+    devices = level_order.shape[0]
+    columns = neighbors.shape[1]
+    rows = columns // LANE
+    chips = devices // 2
+    blocks = rows // chips
+    width = blocks * LANE
+    hidden = weight_two.shape[1]
+    levels = devices
+    f32, bf16 = jnp.float32, jnp.bfloat16
+
+    def pad(count):
+        return -(-count // SUB) * SUB
+
+    send_weights = call(
+        pack_weights_kernel, shape((devices, 80, LANE), bf16), 3, [pltpu.VMEM((16, LANE), f32)], "pack_weights"
+    )(weight_one, weight_two, weight_three.T)
+    mine = lax.all_to_all(send_weights, "slab", split_axis=0, concat_axis=0, tiled=True)
+    other = lax.ppermute(mine, "slab", [(i, i ^ 1) for i in range(devices)])
+
+    def view(field):
+        return field.reshape(rows, LANE)
+
+    def lanes(table):
+        return table.reshape(table.shape[0], rows, LANE).transpose(1, 0, 2)
+
+    stride = pad(6 * blocks)
+    send_fields = call(
+        pack_fields_kernel, shape((devices, stride, LANE), bf16), 8, [pltpu.VMEM((chips * stride, LANE), f32)], "pack_fields"
+    )(
+        view(pressure), view(density), view(vertical_wind), horizontal_wind.reshape(2, rows, LANE),
+        lanes(metric_terms), lanes(neighbors), view(pressure_adjoint), view(wind_adjoint),
+    )
+    fields = lax.all_to_all(send_fields, "slab", split_axis=0, concat_axis=0, tiled=True)
+    weights = call(
+        unpack_weights_kernel,
+        (
+            shape((hidden, 4 * levels), bf16), shape((levels, hidden), bf16), shape((hidden, hidden), bf16),
+            shape((hidden, hidden), bf16), shape((levels, hidden), bf16), shape((hidden, levels), bf16),
+        ),
+        2,
+        [pltpu.VMEM((devices * 16, LANE), f32), pltpu.VMEM((devices * 16, LANE), f32), pltpu.VMEM((16 * devices, LANE), f32)],
+        "unpack_weights",
+    )(mine, other)
+    back = pad(3 * blocks)
+    send_back = call(
+        column_kernel,
+        shape((chips, 160 + back, LANE), bf16),
+        10,
+        [
+            pltpu.VMEM((devices * stride, LANE), f32), pltpu.VMEM((levels * back, LANE), f32), pltpu.VMEM((16, LANE), f32),
+            pltpu.VMEM((hidden, width), bf16), pltpu.VMEM((hidden // 2, width), bf16),
+        ],
+        "column_step",
+    )(fields, *weights, level_order.reshape(1, levels), stiffness.reshape(1, levels), coupling.reshape(1, levels))
+    received = lax.all_to_all(
+        send_back, "slab", split_axis=0, concat_axis=0, tiled=True,
+        axis_index_groups=[list(range(core, devices, 2)) for core in range(2)],
+    )
+    field_out = shape((rows, LANE), f32)
+    new_pressure, new_wind, grad, first_grad, second_grad, third_grad = call(
+        functools.partial(finish_kernel, 1.0 / math.sqrt(columns)),
+        (
+            field_out, field_out, field_out, shape(weight_one.shape, f32), shape(weight_two.shape, f32),
+            shape(weight_three.shape[::-1], f32),
+        ),
+        1,
+        [pltpu.VMEM((chips * back, LANE), f32)],
+        "finish",
+    )(received)
+    return (
+        new_pressure.reshape(1, columns), new_wind.reshape(1, columns), grad.reshape(1, columns),
+        first_grad, second_grad, third_grad.T,
+    )
+
+
+def fits_tiles(*args):
+    pressure, level_order, neighbors = args[0], args[6], args[5]
+    weight_one, weight_two, weight_three = args[9:12]
+    devices = level_order.shape[0]
+    return (
+        pressure.shape[0] == 1
+        and devices == 2 * SUB
+        and neighbors.shape[1] % (LANE * SUB) == 0
+        and weight_one.shape == (4, 4 * LANE)
+        and weight_two.shape == (32, 4 * LANE)
+        and weight_three.shape == (32, 16)
+    )
+
+
+def any_body(*args):
+    return (fast_body if fits_tiles(*args) else body)(*args)
+
+
 def solution(mesh):
     in_specs = (
         P("slab", "date"),
@@ -160,4 +501,4 @@
         P(("date", "slab"), None),
         P(("date", "slab"), None),
     )
-    return jax.shard_map(body, mesh=mesh, in_specs=in_specs, out_specs=out_specs, check_vma=False)
+    return jax.shard_map(any_body, mesh=mesh, in_specs=in_specs, out_specs=out_specs, check_vma=False)

time: 541 us -> 58.5 us (0.11)
  waiting for transfers between devices: 188 us -> 8.01 us
  local copies, waits for them, and re-layouts: 177 us -> 2.85 us
  other arithmetic: 72 us -> 0 us
  blocking collectives: 61.4 us -> 32.7 us
  starting transfers between devices: 20.7 us -> 3.63 us
  between operations: 15 us -> 0.76 us
  Pallas kernels: 0 us -> 10.1 us
  matrix products: 6.09 us -> 0 us
    gather x9 -> x0, local copies, waits for them, and re-layouts: 140 us -> none  [the longest x1 34.3 us: body(): south = jnp.take(horizontal_wind[1], neighbors[3], axis=1)]
    unnamed x5 -> x0, waiting for transfers between devices: 116 us -> none
    unnamed x3 -> x0, other arithmetic: 63.6 us -> none
    reduce_scatter x1 -> x0, waiting for transfers between devices: 61.9 us -> none  [body(): lax.psum_scatter(local_two, 'slab', scatter_dimension=0, tiled=True)]
    all_gather x3 -> x0, blocking collectives: 61.4 us -> none  [the longest x1 21.9 us: body(): lax.all_gather(weight_one, 'slab', axis=0, tiled=True)]
    all_to_all x0 -> x2, blocking collectives: none -> 32.7 us  [the longest x1 18.4 us: fast_body(): lax.all_to_all(send_weights, 'slab', split_axis=0, concat_axis=0, tiled=T...]
    unnamed x44 -> x28, local copies, waits for them, and re-layouts: 23.4 us -> 2.85 us
    all_to_all x4 -> x1, starting transfers between devices: 20.3 us -> 3.52 us  [fast_body(): lax.all_to_all(send_fields, 'slab', split_axis=0, concat_axis=0, tiled=True)]
  transfers between devices with their start and end apart: 7 -> 2, of which waited for: 5 -> 1; matrix products, arithmetic and copies ran while one was open for 11% -> 0% of each run, Pallas kernels for 0% -> 11%
where the time goes in v1:
time: 58.5 us; the launch traced here: 58 us
  blocking collectives  32.7 us (56%)
  Pallas kernels  10.1 us (17%)
  waiting for transfers between devices  8.01 us (14%)
  starting transfers between devices  3.63 us (6%)
  local copies, waits for them, and re-layouts  2.85 us (5%)
  between operations  0.76 us (1%)
    all_to_all x1, blocking collectives, fast_body(): lax.all_to_all(send_weights, 'slab', split_axis=0, concat_axis=0, tiled=T...  18.4 us
    all_to_all x1, blocking collectives, fast_body(): lax.all_to_all(send_back, 'slab', split_axis=0, concat_axis=0, tiled=True...  14.3 us
    all_to_all x1, waiting for transfers between devices, fast_body(): lax.all_to_all(send_fields, 'slab', split_axis=0, concat_axis=0, tiled=True)  8.01 us
    pallas_call x1, Pallas kernels, fast_body(): call(pack_fields_kernel, shape((devices, stride, LANE), bf16), 8, [pltpu....  5.82 us
    all_to_all x1, starting transfers between devices, fast_body(): lax.all_to_all(send_fields, 'slab', split_axis=0, concat_axis=0, tiled=True)  3.52 us
    pallas_call x1, Pallas kernels, fast_body(): call(column_kernel, shape((chips, 160 + back, LANE), bf16), 10, [pltpu.VM...  2.9 us
    unnamed x28, local copies, waits for them, and re-layouts  2.85 us
  transfers between devices with their start and end apart: 2, of which 1 were waited for; matrix products, arithmetic and copies ran while one was open for 0% of the time, Pallas kernels for 11%

profile of v1, /device:TPU:0, one launch (start us, length us, event | category | flops | bytes accessed | tf_op | source)
XLA Modules:
  0.0 58.0 jit_solution(13002597943364820369)
XLA Ops:
  0.6 0.0 copy-start.3
  0.6 0.7 %copy-done.3 = bf16[32,512]{1,0:T(8,128)(2,1)S(1)} copy-done((bf16[32,512]{1,0:T(8,128)(2,1)S(1)}, bf16[32,512]{1,0:T(8,128)(2,1)}, u32[]{:S(2)}) %copy-start.3) | copy-done | bytes 32792
  1.4 0.7 %copy-done.9 = bf16[4,512]{1,0:T(4,128)(2,1)S(1)} copy-done((bf16[4,512]{1,0:T(4,128)(2,1)S(1)}, bf16[4,512]{1,0:T(4,128)(2,1)}, u32[]{:S(2)}) %copy-start.9) | copy-done | bytes 4120
  2.1 0.7 %copy-done.10 = bf16[32,16]{0,1:T(8,128)(2,1)S(1)} copy-done((bf16[32,16]{0,1:T(8,128)(2,1)S(1)}, bf16[32,16]{0,1:T(8,128)(2,1)}, u32[]{:S(2)}) %copy-start.10) | copy-done | bytes 1048
  2.8 0.1 pack_weights.1
  2.9 0.0 copy-start.2
  2.9 0.0 copy-start.4
  2.9 0.0 copy-start.5
  2.9 0.0 copy-start.6
  3.0 0.0 copy-start.7
  3.0 0.0 copy-start.8
  3.0 18.4 %all_to_all.15.mine_ref = bf16[16,80,128]{2,1,0:T(8,128)(2,1)S(1)} all-to-all(bf16[16,80,128]{2,1,0:T(8,128)(2,1)S(1)} %pack_weights.1), channel_id=1, replica_groups=mesh['date'=2,'slab'=16] {'slab'}, dimensions={0} | all-to-all | bytes 655360 | tf_op jit(solution)/shard_map/all_to_all | solution.py:402
  21.4 0.1 collective-permute-start
  21.5 0.0 copy-done
  21.5 0.0 copy-done.1
  21.5 0.0 copy-done.2
  21.5 0.0 copy-done.4
  21.5 0.0 copy-done.5
  21.5 0.0 copy-done.6
  21.5 0.0 copy-done.7
  21.5 0.0 copy-done.8
  21.5 5.8 %pack_fields.1 = bf16[16,40,128]{2,1,0:T(8,128)(2,1)} custom-call(f32[48,128]{1,0:T(8,128)S(1)} %bitcast.23, f32[48,128]{1,0:T(8,128)S(1)} %bitcast.24, f32[48,128]{1,0:T(8,128)S(1)} %bitcast.25, f32[2,48,128]{2,1,0:T(8,128)S(1)} %bitcast.21, f32[48,2,128]{2,1,0:T(2,128)S(1)} %bitcast.22, s32[48,4,128]{2,1,0:T(4,128)S(1)} %bitcast.20, ...), custom_call_target="tpu_custom_call" | custom-call | tf_op jit(solution)/shard_map/pack_fields/pallas_call | solution.py:412
  27.4 3.5 %all-to-all-start = ((bf16[16,40,128]{2,1,0:T(8,128)(2,1)}), bf16[16,40,128]{2,1,0:T(8,128)(2,1)S(1)}, u32[]{:S(2)}, u32[]{:S(2)}) async-start(bf16[16,40,128]{2,1,0:T(8,128)(2,1)} %pack_fields.1), calls=%async_computation | async-start | bytes 327680 | tf_op jit(solution)/shard_map/all_to_all | solution.py:418
  30.9 0.0 collective-permute-done.other_ref
  30.9 0.4 unpack_weights.1
  31.3 8.0 %all-to-all-done.f_ref = bf16[16,40,128]{2,1,0:T(8,128)(2,1)S(1)} async-done(((bf16[16,40,128]{2,1,0:T(8,128)(2,1)}), bf16[16,40,128]{2,1,0:T(8,128)(2,1)S(1)}, u32[]{:S(2)}, u32[]{:S(2)}) %all-to-all-start) | async-done | bytes 163872 | tf_op jit(solution)/shard_map/all_to_all | solution.py:418
  39.3 0.6 %copy-done.11 = s32[16]{0:T(128)S(1)} copy-done((s32[16]{0:T(128)S(1)}, s32[16]{0:T(128)}, u32[]{:S(2)}) %copy-start.11) | copy-done | bytes 88
  40.0 0.0 copy-done.12
  40.0 0.0 copy-done.13
  40.0 2.9 %column_step.1 = bf16[8,184,128]{2,1,0:T(8,128)(2,1)S(1)} custom-call(bf16[16,40,128]{2,1,0:T(8,128)(2,1)S(1)} %all-to-all-done.f_ref, bf16[512,64]{1,0:T(8,128)(2,1)S(1)} %get-tuple-element.18.w1t_ref, bf16[16,512]{1,0:T(8,128)(2,1)S(1)} %get-tuple-element.19.w1s_ref, bf16[512,512]{1,0:T(8,128)(2,1)S(1)} %get-tuple-element.20.w2_ref, ...), custom_call_target="tpu_custom_call" | custom-call | tf_op jit(solution)/shard_map/column_step/pallas_call | solution.py:430
  42.9 14.3 %all_to_all.16.r_ref = bf16[8,184,128]{2,1,0:T(8,128)(2,1)S(1)} all-to-all(bf16[8,184,128]{2,1,0:T(8,128)(2,1)S(1)} %column_step.1), channel_id=1, replica_groups={{0,2,4,6,8,10,12,14},{1,3,5,7,9,11,13,15},{16,18,20,22,24,26,28,30},{17..., dimensions={0} | all-to-all | bytes 753664 | tf_op jit(solution)/shard_map/all_to_all | solution.py:440
  57.2 0.9 %finish.1 = (f32[48,128]{1,0:T(8,128)}, f32[48,128]{1,0:T(8,128)}, f32[48,128]{1,0:T(8,128)}, f32[4,512]{1,0:T(4,128)}, f32[32,512]{1,0:T(8,128)}, /*index=5*/f32[16,32]{1,0:T(8,128)}) custom-call(bf16[8,184,128]{2,1,0:T(8,128)(2,1)S(1)} %all_to_all.16.r_ref), custom_call_target="tpu_custom_call" | custom-call | tf_op jit(solution)/shard_map/finish/pallas_call | solution.py:445
  (7 shorter events, 0.0 us)
Async XLA Ops:
  0.6 0.8 %copy-start.3 = (bf16[32,512]{1,0:T(8,128)(2,1)S(1)}, bf16[32,512]{1,0:T(8,128)(2,1)}, u32[]{:S(2)}) copy-start(bf16[32,512]{1,0:T(8,128)(2,1)} %two_ref.1) | copy-start | bytes 98308
  1.4 0.7 %copy-start.9 = (bf16[4,512]{1,0:T(4,128)(2,1)S(1)}, bf16[4,512]{1,0:T(4,128)(2,1)}, u32[]{:S(2)}) copy-start(bf16[4,512]{1,0:T(4,128)(2,1)} %one_ref.1) | copy-start | bytes 12292
  2.1 0.7 %copy-start.10 = (bf16[32,16]{0,1:T(8,128)(2,1)S(1)}, bf16[32,16]{0,1:T(8,128)(2,1)}, u32[]{:S(2)}) copy-start(bf16[32,16]{0,1:T(8,128)(2,1)} %param.25) | copy-start | bytes 3076
  2.9 18.6 %copy-start = (s32[4,6144]{1,0:T(4,128)S(1)}, s32[4,6144]{1,0:T(4,128)}, u32[]{:S(2)}) copy-start(s32[4,6144]{1,0:T(4,128)} %param.19) | copy-start | bytes 294916
  2.9 18.6 %copy-start.1 = (f32[2,1,6144]{2,1,0:T(1,128)S(1)}, f32[2,1,6144]{2,1,0:T(1,128)}, u32[]{:S(2)}) copy-start(f32[2,1,6144]{2,1,0:T(1,128)} %param.17) | copy-start | bytes 147460
  2.9 18.6 %copy-start.2 = (f32[2,6144]{1,0:T(2,128)S(1)}, f32[2,6144]{1,0:T(2,128)}, u32[]{:S(2)}) copy-start(f32[2,6144]{1,0:T(2,128)} %param.18) | copy-start | bytes 147460
  2.9 18.6 %copy-start.4 = (f32[1,6144]{1,0:T(1,128)S(1)}, f32[1,6144]{1,0:T(1,128)}, u32[]{:S(2)}) copy-start(f32[1,6144]{1,0:T(1,128)} %param.14) | copy-start | bytes 73732
  2.9 18.6 %copy-start.5 = (f32[1,6144]{1,0:T(1,128)S(1)}, f32[1,6144]{1,0:T(1,128)}, u32[]{:S(2)}) copy-start(f32[1,6144]{1,0:T(1,128)} %param.15) | copy-start | bytes 73732
  2.9 18.6 %copy-start.6 = (f32[1,6144]{1,0:T(1,128)S(1)}, f32[1,6144]{1,0:T(1,128)}, u32[]{:S(2)}) copy-start(f32[1,6144]{1,0:T(1,128)} %param.16) | copy-start | bytes 73732
  3.0 18.6 %copy-start.7 = (f32[1,6144]{1,0:T(1,128)S(1)}, f32[1,6144]{1,0:T(1,128)}, u32[]{:S(2)}) copy-start(f32[1,6144]{1,0:T(1,128)} %param.26) | copy-start | bytes 73732
  3.0 18.6 %copy-start.8 = (f32[1,6144]{1,0:T(1,128)S(1)}, f32[1,6144]{1,0:T(1,128)}, u32[]{:S(2)}) copy-start(f32[1,6144]{1,0:T(1,128)} %param.27) | copy-start | bytes 73732
  21.4 9.5 %collective-permute-start = (bf16[16,80,128]{2,1,0:T(8,128)(2,1)S(1)}, bf16[16,80,128]{2,1,0:T(8,128)(2,1)S(1)}, u32[]{:S(2)}, u32[]{:S(2)}) collective-permute-start(bf16[16,80,128]{2,1,0:T(8,128)(2,1)S(1)} %all_to_all.15.mine_ref), channel_id=1, source_target_pairs={{0,1},{1,0},{2,3},{3,2},{4,5},{5,4},{6,7},{7,6},{8,9},{9,8},{10,11... | collective-permute-start | bytes 983048 | tf_op jit(solution)/shard_map/ppermute | solution.py:403
  27.4 11.9 %all-to-all-start = ((bf16[16,40,128]{2,1,0:T(8,128)(2,1)}), bf16[16,40,128]{2,1,0:T(8,128)(2,1)S(1)}, u32[]{:S(2)}, u32[]{:S(2)}) async-start(bf16[16,40,128]{2,1,0:T(8,128)(2,1)} %pack_fields.1), calls=%async_computation | async-start | bytes 327680 | tf_op jit(solution)/shard_map/all_to_all | solution.py:418
  39.3 0.7 %copy-start.11 = (s32[16]{0:T(128)S(1)}, s32[16]{0:T(128)}, u32[]{:S(2)}) copy-start(s32[16]{0:T(128)} %param.20) | copy-start | bytes 196
  39.3 0.7 %copy-start.12 = (f32[16]{0:T(128)S(1)}, f32[16]{0:T(128)}, u32[]{:S(2)}) copy-start(f32[16]{0:T(128)} %param.21) | copy-start | bytes 196
  39.3 0.7 %copy-start.13 = (f32[16]{0:T(128)S(1)}, f32[16]{0:T(128)}, u32[]{:S(2)}) copy-start(f32[16]{0:T(128)} %param.22) | copy-start | bytes 196

commit v2 on v0

--- a/solution.py
+++ b/solution.py
@@ -1,8 +1,11 @@
+import functools
 import math
 
 import jax
 import jax.numpy as jnp
 from jax import lax
+from jax.experimental import pallas as pl
+from jax.experimental.pallas import tpu as pltpu
 from jax.sharding import PartitionSpec as P
 
 
@@ -135,6 +138,350 @@
     return (pressure_new, wind_new, pressure_grad, first_grad, second_grad, third_grad)
 
 
+LANE = 128
+SUB = 8
+PIECE = 32
+HEAD = 4 * PIECE
+TAIL = HEAD + 16
+
+
+def call(kernel, name, outs, n_in, scratch=(), space=pltpu.VMEM):
+    return pl.pallas_call(
+        kernel,
+        out_shape=outs,
+        in_specs=[pl.BlockSpec(memory_space=space) for _ in range(n_in)],
+        out_specs=jax.tree.map(lambda _: pl.BlockSpec(memory_space=pltpu.VMEM), outs),
+        scratch_shapes=list(scratch),
+        compiler_params=pltpu.CompilerParams(vmem_limit_bytes=48 << 20),
+        name=name,
+    )
+
+
+def shape(dims, kind):
+    return jax.ShapeDtypeStruct(dims, kind)
+
+
+def difference(table_ref, first, second):
+    groups = table_ref.shape[0] // SUB
+    sublanes = lax.broadcasted_iota(jnp.int32, (SUB, LANE), 0)
+    out = []
+    for r in range(SUB):
+        kept = []
+        for index in (first, second):
+            high = jnp.broadcast_to(index[r : r + 1, :] >> 7, (SUB, LANE))
+            low = jnp.broadcast_to(index[r : r + 1, :] & (LANE - 1), (SUB, LANE))
+            total = jnp.zeros((SUB, LANE), jnp.float32)
+            for g in range(groups):
+                picked = jnp.take_along_axis(table_ref[SUB * g : SUB * g + SUB, :], low, axis=1, mode="promise_in_bounds")
+                total = jnp.where(high == sublanes + SUB * g, picked, total)
+            kept.append(total)
+        out.append(jnp.sum(kept[0] - kept[1], axis=0, keepdims=True))
+    return jnp.concatenate(out, axis=0)
+
+
+def lane_group(lanes, q):
+    return (lanes >= PIECE * q) & (lanes < PIECE * (q + 1))
+
+
+def pack_kernel(
+    p_hbm, d_hbm, w_hbm, u_hbm, m_hbm, n_hbm, one_hbm, two_hbm, three_hbm, pa_hbm, wa_hbm, out_ref,
+    p_ref, d_ref, w_ref, u_ref, m_ref, n_ref, one_ref, two_ref, three_ref, pa_ref, wa_ref, part_ref, f_ref, sems,
+):
+    pairs = (
+        (n_hbm, n_ref), (u_hbm, u_ref), (m_hbm, m_ref), (p_hbm, p_ref), (d_hbm, d_ref), (w_hbm, w_ref),
+        (pa_hbm, pa_ref), (wa_hbm, wa_ref), (one_hbm, one_ref), (two_hbm, two_ref), (three_hbm, three_ref),
+    )
+    copies = [pltpu.make_async_copy(source, target, sems.at[i]) for i, (source, target) in enumerate(pairs)]
+    for copy in copies:
+        copy.start()
+    f32, bf16 = jnp.float32, jnp.bfloat16
+    chips = out_ref.shape[0]
+    rest = out_ref.shape[1] - TAIL
+    blocks = p_ref.shape[0] // chips
+    for copy in copies:
+        copy.wait()
+
+    def put(f, j, tile):
+        f_ref[pl.ds(4 + blocks * f + j, chips, stride=rest), :] = tile
+
+    for j in range(blocks):
+        rows = slice(SUB * j, SUB * j + SUB)
+        along = difference(u_ref.at[0], n_ref[rows, 0, :], n_ref[rows, 1, :])
+        across = difference(u_ref.at[1], n_ref[rows, 2, :], n_ref[rows, 3, :])
+        diverg = m_ref[rows, 0, :] * along + m_ref[rows, 1, :] * across
+        for f, tile in enumerate((p_ref[rows, :] - diverg, d_ref[rows, :], w_ref[rows, :], diverg, pa_ref[rows, :], wa_ref[rows, :])):
+            put(f, j, tile)
+    lanes = lax.broadcasted_iota(jnp.int32, (PIECE, LANE), 1)
+    spread = (lanes % PIECE == lax.broadcasted_iota(jnp.int32, (PIECE, LANE), 0)).astype(f32).astype(bf16)
+    part_ref[...] = jnp.dot(three_ref[...], spread, preferred_element_type=f32)
+    lanes = lax.broadcasted_iota(jnp.int32, (4, LANE), 1)
+    three = jnp.zeros((4, LANE), f32)
+    for q in range(4):
+        three = jnp.where(lane_group(lanes, q), part_ref[4 * q : 4 * q + 4, :], three)
+    one = one_ref[...].astype(f32)
+    for q in range(4):
+        part_ref[4 * q : 4 * q + 4, :] = one[:, LANE * q : LANE * (q + 1)]
+    one = part_ref[...].astype(bf16)
+    for c in range(chips):
+        for q in range(4):
+            out_ref[c, PIECE * q : PIECE * (q + 1), :] = two_ref[:, LANE * q : LANE * (q + 1)]
+        out_ref[c, HEAD:TAIL, :] = one
+        f_ref[rest * c : rest * c + 4, :] = three
+        if rest > 4 + 6 * blocks:
+            f_ref[rest * c + 4 + 6 * blocks : rest * (c + 1), :] = jnp.zeros((rest - 4 - 6 * blocks, LANE), f32)
+        out_ref[c, TAIL:, :] = f_ref[rest * c : rest * (c + 1), :].astype(bf16)
+
+
+def shifted_up(field, rows):
+    return jnp.where(rows < field.shape[0] - 1, pltpu.roll(field, field.shape[0] - 1, 0), 0.0)
+
+
+def shifted_down(field, rows):
+    return jnp.where(rows > 0, pltpu.roll(field, 1, 0), 0.0)
+
+
+def operator_inverse(stiff, rows):
+    size = stiff.shape[0]
+    below = shifted_down(stiff, rows)
+    lower, diagonal = -below, 1.0 + stiff + below
+    upper = jnp.where(rows < size - 1, -stiff, 0.0)
+    right = (rows == lax.broadcasted_iota(jnp.int32, (size, size), 1)).astype(jnp.float32)
+    distance = 1
+    while distance < size:
+        down = lambda v: pltpu.roll(v, distance, 0)
+        up = lambda v: pltpu.roll(v, size - distance, 0)
+        alpha, gamma = -lower / down(diagonal), -upper / up(diagonal)
+        right = right + alpha * down(right) + gamma * up(right)
+        diagonal = diagonal + alpha * down(upper) + gamma * up(lower)
+        lower, upper = alpha * down(lower), gamma * up(upper)
+        distance *= 2
+    return right / diagonal
+
+
+def operator_kernel(order_ref, stiff_ref, couple_ref, place_ref, inverse_ref, column_ref):
+    levels = inverse_ref.shape[0]
+    rows = lax.broadcasted_iota(jnp.int32, (levels, levels), 0)
+    diagonal = rows == lax.broadcasted_iota(jnp.int32, (levels, levels), 1)
+    place_ref[...] = (order_ref[...] == rows).astype(jnp.float32).astype(jnp.bfloat16)
+    stiff = jnp.sum(jnp.where(diagonal, stiff_ref[...], 0.0), axis=1, keepdims=True)
+    couple = jnp.sum(jnp.where(diagonal, couple_ref[...], 0.0), axis=1, keepdims=True)
+    inverse_ref[...] = operator_inverse(jnp.broadcast_to(stiff, (levels, levels)), rows)
+    column_ref[...] = jnp.broadcast_to(couple, column_ref.shape)
+
+
+def column_kernel(
+    mine_ref, other_ref, place_ref, inverse_ref, column_ref, out_ref,
+    a_ref, one_ref, w2_ref, w3_ref, act_ref, sel_ref, g_ref, y_ref, t_ref,
+):
+    f32, bf16 = jnp.float32, jnp.bfloat16
+    core = lax.axis_index("slab") % 2
+    first = core == 0
+    chips = mine_ref.shape[0]
+    devices = 2 * chips
+    levels = inverse_ref.shape[0]
+    width = act_ref.shape[1]
+    blocks = width // LANE
+    stride = mine_ref.shape[1] - HEAD
+    for ref, which in ((mine_ref, core), (other_ref, 1 - core)):
+        for c in range(chips):
+            for q in range(4):
+                rows = pl.ds(pl.multiple_of(2 * PIECE * c + PIECE * which, PIECE), PIECE)
+                w2_ref[rows, LANE * q : LANE * (q + 1)] = ref[c, PIECE * q : PIECE * (q + 1), :]
+            rows = pl.ds(pl.multiple_of(stride * (2 * c + which), SUB), stride)
+            a_ref[rows, :] = ref[c, HEAD:, :].astype(f32)
+    for q in range(4):
+        for r in range(4):
+            one_ref[pl.ds(4 * devices * q + r, devices, stride=4), :] = a_ref[pl.ds(4 * q + r, devices, stride=stride), :]
+    one = jnp.concatenate([one_ref[4 * devices * q : 4 * devices * (q + 1), :] for q in range(4)], axis=1)
+    lanes = lax.broadcasted_iota(jnp.int32, (4, LANE), 1)
+    for t in range(devices // 4):
+        packed = [a_ref[stride * (4 * t + s) + 16 : stride * (4 * t + s) + 20, :] for s in range(4)]
+        for q in range(4):
+            tile = jnp.zeros((4, LANE), f32)
+            for s in range(4):
+                moved = packed[s] if s == q else pltpu.roll(packed[s], PIECE * ((s - q) % 4), 1)
+                tile = jnp.where(lane_group(lanes, s), moved, tile)
+            w3_ref[4 * q : 4 * q + 4, LANE * t : LANE * (t + 1)] = tile
+    w1t = one.T.astype(bf16)
+    w1s = one[:levels, :].astype(bf16)
+    w2 = w2_ref[...]
+    w3t = w3_ref[...].astype(bf16)
+    w3 = w3_ref[...].T.astype(bf16)
+    place, inverse = place_ref[...], inverse_ref[...]
+    raw = jnp.concatenate([a_ref[pl.ds(20 + k, levels, stride=stride), :] for k in range(6 * blocks)], axis=1)
+    ordered = jnp.dot(place, raw.astype(bf16), preferred_element_type=f32)
+    star, density, vertical, diverg, pressure_adjoint, wind_adjoint = (
+        ordered[:, width * i : width * (i + 1)] for i in range(6)
+    )
+    couple = jnp.concatenate([column_ref[...]] * blocks, axis=1)
+    rows = lax.broadcasted_iota(jnp.int32, (levels, width), 0)
+
+    def solve(right):
+        return jnp.dot(inverse, right, precision=lax.Precision.HIGHEST, preferred_element_type=f32)
+
+    def lower(field):
+        return shifted_up(field, rows) - field
+
+    def upper(field):
+        return shifted_down(field, rows) - field
+
+    column_input = jnp.concatenate([star, density, vertical, diverg], axis=0).astype(bf16)
+    tanh_one = jnp.tanh(jnp.dot(w1t, column_input, preferred_element_type=f32))
+    act_one = tanh_one.astype(bf16)
+    act_ref[...] = act_one
+    rhs_grad = solve(wind_adjoint + couple * lower(pressure_adjoint))
+    star_part = pressure_adjoint - upper(couple * rhs_grad)
+    heat_grad = rhs_grad.astype(bf16)
+    tanh_two = jnp.tanh(contract_first(w2, act_one))
+    act_two = tanh_two.astype(bf16)
+    back_two = jnp.dot(w3, heat_grad, preferred_element_type=f32)
+    pre_two_grad = (back_two * (1.0 - tanh_two * tanh_two)).astype(bf16)
+    back_one = jnp.dot(w2, pre_two_grad, preferred_element_type=f32)
+    pre_one_grad = (back_one * (1.0 - tanh_one * tanh_one)).astype(bf16)
+    heating = jnp.dot(w3t, act_two, preferred_element_type=f32)
+    wind_next = solve(vertical - couple * lower(star) - 0.5 * density + heating)
+    press_next = star + upper(couple * wind_next)
+    star_grad = star_part + jnp.dot(w1s, pre_one_grad, preferred_element_type=f32)
+    for c in range(chips):
+        rows = pl.ds(pl.multiple_of(2 * PIECE * c + PIECE * core, PIECE), PIECE)
+        sel_ref[PIECE * c : PIECE * (c + 1), :] = act_ref[rows, :]
+    local_two = contract_last(sel_ref[...], pre_two_grad)
+    local_three = contract_last(heat_grad, act_two)
+    local_one = contract_last(column_input, pre_one_grad)
+    fields = jnp.concatenate([press_next, wind_next, star_grad], axis=1).astype(bf16)
+    stored = lax.dot_general(place, fields, (((0,), (0,)), ((), ())), preferred_element_type=f32)
+    back = out_ref.shape[1] - TAIL
+    for k in range(3 * blocks):
+        y_ref[pl.ds(4 + k, devices, stride=back), :] = stored[:, LANE * k : LANE * (k + 1)]
+    for k in range(4 + 3 * blocks, back):
+        y_ref[pl.ds(k, devices, stride=back), :] = jnp.zeros((devices, LANE), f32)
+    for t in range(devices // 4):
+        tile = local_three[:, LANE * t : LANE * (t + 1)]
+        t_ref[16 * t : 16 * t + 16, :] = jnp.where(first, tile, pltpu.roll(tile, LANE - PIECE, 1))
+    for c in range(chips):
+        mine = jnp.where(first, local_one[8 * c : 8 * c + 4, :], local_one[8 * c + 4 : 8 * c + 8, :])
+        three = jnp.zeros((4, LANE), f32)
+        for q in range(4):
+            cols = slice(LANE * q, LANE * (q + 1))
+            out_ref[c, PIECE * q : PIECE * (q + 1), :] = local_two[PIECE * c : PIECE * (c + 1), cols].astype(bf16)
+            g_ref[4 * q : 4 * q + 4, :] = mine[:, cols]
+            moved = t_ref[16 * (c // 2) + 4 * q : 16 * (c // 2) + 4 * q + 4, :]
+            if q != 2 * (c % 2):
+                moved = pltpu.roll(moved, PIECE * ((q - 2 * (c % 2)) % 4), 1)
+            three = jnp.where(lane_group(lanes, q), moved, three)
+        out_ref[c, HEAD:TAIL, :] = g_ref[...].astype(bf16)
+        start = pl.multiple_of(back * (2 * c + core), SUB)
+        y_ref[pl.ds(start, 4), :] = three
+        out_ref[c, TAIL:, :] = y_ref[pl.ds(start, back), :].astype(bf16)
+
+
+def finish_kernel(scale, r_ref, p_ref, w_ref, g_ref, one_ref, two_ref, three_ref, y_ref):
+    chips = r_ref.shape[0]
+    back = r_ref.shape[1] - TAIL
+    blocks = p_ref.shape[0] // chips
+
+    def total(start, stop):
+        return sum(r_ref[c, start:stop, :].astype(jnp.float32) for c in range(chips)) * scale
+
+    for q in range(4):
+        two_ref[:, LANE * q : LANE * (q + 1)] = total(PIECE * q, PIECE * (q + 1))
+    one = total(HEAD, TAIL)
+    for q in range(4):
+        one_ref[:, LANE * q : LANE * (q + 1)] = one[4 * q : 4 * q + 4, :]
+    for c in range(chips):
+        y_ref[back * c : back * (c + 1), :] = r_ref[c, TAIL:, :].astype(jnp.float32)
+    three = sum(y_ref[back * c : back * c + 4, :] for c in range(chips)) * scale
+    for q in range(4):
+        three_ref[4 * q : 4 * q + 4, :] = three[:, PIECE * q : PIECE * (q + 1)]
+    for f, ref in enumerate((p_ref, w_ref, g_ref)):
+        for j in range(blocks):
+            ref[chips * j : chips * (j + 1), :] = y_ref[pl.ds(4 + blocks * f + j, chips, stride=back), :]
+
+
+def fast_body(
+    pressure, density, vertical_wind, horizontal_wind, metric_terms, neighbors, level_order, stiffness, coupling,
+    weight_one, weight_two, weight_three, pressure_adjoint, wind_adjoint,
+):
+    levels = devices = level_order.shape[0]
+    columns = neighbors.shape[1]
+    rows = columns // LANE
+    chips = devices // 2
+    blocks = rows // chips
+    width = blocks * LANE
+    hidden = weight_two.shape[1]
+    f32, bf16 = jnp.float32, jnp.bfloat16
+    same_core = [list(range(core, devices, 2)) for core in range(2)]
+
+    def pad(count):
+        return -(-count // SUB) * SUB
+
+    def view(field):
+        return field.reshape(rows, LANE)
+
+    def lanes(table):
+        return table.reshape(table.shape[0], rows, LANE).transpose(1, 0, 2)
+
+    def exchange(blocks_of_chips):
+        return lax.all_to_all(blocks_of_chips, "slab", split_axis=0, concat_axis=0, tiled=True, axis_index_groups=same_core)
+
+    sources = (
+        view(pressure), view(density), view(vertical_wind), horizontal_wind.reshape(2, rows, LANE), lanes(metric_terms),
+        lanes(neighbors), weight_one, weight_two, weight_three.T, view(pressure_adjoint), view(wind_adjoint),
+    )
+    rest, back = pad(4 + 6 * blocks), pad(4 + 3 * blocks)
+    send = call(
+        pack_kernel, "pack", shape((chips, TAIL + rest, LANE), bf16), len(sources),
+        [pltpu.VMEM(source.shape, source.dtype) for source in sources]
+        + [pltpu.VMEM((16, LANE), f32), pltpu.VMEM((chips * rest, LANE), f32), pltpu.SemaphoreType.DMA((len(sources),))],
+        pltpu.HBM,
+    )(*sources)
+    operators = call(
+        operator_kernel, "operators", (shape((levels, levels), bf16), shape((levels, levels), f32), shape((levels, LANE), f32)), 3
+    )(level_order.reshape(1, levels), stiffness.reshape(1, levels), coupling.reshape(1, levels))
+    mine = exchange(send)
+    other = lax.ppermute(mine, "slab", [(i, i ^ 1) for i in range(devices)])
+    send_back = call(
+        column_kernel, "column_step", shape((chips, TAIL + back, LANE), bf16), 5,
+        [
+            pltpu.VMEM((devices * (16 + rest), LANE), f32), pltpu.VMEM((16 * devices, LANE), f32),
+            pltpu.VMEM((hidden, hidden), bf16), pltpu.VMEM((levels, hidden), f32), pltpu.VMEM((hidden, width), bf16),
+            pltpu.VMEM((hidden // 2, width), bf16), pltpu.VMEM((16, LANE), f32), pltpu.VMEM((devices * back, LANE), f32),
+            pltpu.VMEM((4 * devices, LANE), f32),
+        ],
+    )(mine, other, *operators)
+    field_out = shape((rows, LANE), f32)
+    new_pressure, new_wind, grad, first_grad, second_grad, third_grad = call(
+        functools.partial(finish_kernel, 1.0 / math.sqrt(columns)), "finish",
+        (
+            field_out, field_out, field_out, shape(weight_one.shape, f32), shape(weight_two.shape, f32),
+            shape(weight_three.shape[::-1], f32),
+        ),
+        1,
+        [pltpu.VMEM((chips * back, LANE), f32)],
+    )(exchange(send_back))
+    return (
+        new_pressure.reshape(1, columns), new_wind.reshape(1, columns), grad.reshape(1, columns),
+        first_grad, second_grad, third_grad.T,
+    )
+
+
+def fits_tiles(*args):
+    pressure, level_order, neighbors = args[0], args[6], args[5]
+    weight_one, weight_two, weight_three = args[9:12]
+    return (
+        pressure.shape[0] == 1
+        and level_order.shape[0] == 2 * SUB
+        and neighbors.shape[1] % (LANE * SUB) == 0
+        and weight_one.shape == (4, 4 * LANE)
+        and weight_two.shape == (PIECE, 4 * LANE)
+        and weight_three.shape == (PIECE, 2 * SUB)
+    )
+
+
+def any_body(*args):
+    return (fast_body if fits_tiles(*args) else body)(*args)
+
+
 def solution(mesh):
     in_specs = (
         P("slab", "date"),
@@ -160,4 +507,4 @@
         P(("date", "slab"), None),
         P(("date", "slab"), None),
     )
-    return jax.shard_map(body, mesh=mesh, in_specs=in_specs, out_specs=out_specs, check_vma=False)
+    return jax.shard_map(any_body, mesh=mesh, in_specs=in_specs, out_specs=out_specs, check_vma=False)

time: 541 us -> 50.1 us (0.09)
  waiting for transfers between devices: 188 us -> 0.88 us
  local copies, waits for them, and re-layouts: 177 us -> 8.3 us
  other arithmetic: 72 us -> 0 us
  blocking collectives: 61.4 us -> 33.3 us
  starting transfers between devices: 20.7 us -> 0.01 us
  between operations: 15 us -> 0.69 us
  Pallas kernels: 0 us -> 6.16 us
  matrix products: 6.09 us -> 0 us
    gather x9 -> x0, local copies, waits for them, and re-layouts: 140 us -> none  [the longest x1 34.3 us: body(): south = jnp.take(horizontal_wind[1], neighbors[3], axis=1)]
    unnamed x5 -> x0, waiting for transfers between devices: 116 us -> none
    unnamed x3 -> x0, other arithmetic: 63.6 us -> none
    reduce_scatter x1 -> x0, waiting for transfers between devices: 61.9 us -> none  [body(): lax.psum_scatter(local_two, 'slab', scatter_dimension=0, tiled=True)]
    all_gather x3 -> x0, blocking collectives: 61.4 us -> none  [the longest x1 21.9 us: body(): lax.all_gather(weight_one, 'slab', axis=0, tiled=True)]
    all_to_all x0 -> x2, blocking collectives: none -> 33.3 us  [exchange(): lax.all_to_all(blocks_of_chips, 'slab', split_axis=0, concat_axis=0, tile...]
    all_to_all x4 -> x0, starting transfers between devices: 20.3 us -> none  [the longest x1 7.36 us: body(): lax.all_to_all(jnp.stack([star, density, vertical_wind, diverg]).astype(j...]
    unnamed x44 -> x28, local copies, waits for them, and re-layouts: 23.4 us -> 8.3 us
  transfers between devices with their start and end apart: 7 -> 1, of which waited for: 5 -> 1; matrix products, arithmetic and copies ran while one was open for 11% -> 0% of each run, Pallas kernels for 0% -> 0%
where the time goes in v2:
time: 50.1 us; the launch traced here: 49.3 us
  blocking collectives  33.3 us (66%)
  local copies, waits for them, and re-layouts  8.3 us (17%)
  Pallas kernels  6.16 us (12%)
  waiting for transfers between devices  0.88 us (2%)
  between operations  0.69 us (1%)
    all_to_all x2, blocking collectives, exchange(): lax.all_to_all(blocks_of_chips, 'slab', split_axis=0, concat_axis=0, tile...  33.3 us
    unnamed x28, local copies, waits for them, and re-layouts  8.3 us
    pallas_call x1, Pallas kernels, fast_body(): call(column_kernel, 'column_step', shape((chips, TAIL + back, LANE), bf16...  2.86 us
    pallas_call x1, Pallas kernels, fast_body(): call(pack_kernel, 'pack', shape((chips, TAIL + rest, LANE), bf16), len(so...  2.49 us
  transfers between devices with their start and end apart: 1, of which 1 were waited for; matrix products, arithmetic and copies ran while one was open for 0% of the time, Pallas kernels for 0%

profile of v2, /device:TPU:0, one launch (start us, length us, event | category | flops | bytes accessed | tf_op | source)
XLA Modules:
  0.0 49.3 jit_solution(11315918005810640713)
XLA Ops:
  0.6 0.0 copy-start.10
  0.6 0.0 copy-start.9
  0.7 0.7 %copy-done.10 = bf16[32,16]{0,1:T(8,128)(2,1)S(1)} copy-done((bf16[32,16]{0,1:T(8,128)(2,1)S(1)}, bf16[32,16]{0,1:T(8,128)(2,1)}, u32[]{:S(2)}) %copy-start.10) | copy-done | bytes 1048
  1.3 0.0 copy-done.9
  1.3 0.0 copy-start
  1.3 0.9 %copy-done = s32[4,6144]{1,0:T(4,128)S(1)} copy-done((s32[4,6144]{1,0:T(4,128)S(1)}, s32[4,6144]{1,0:T(4,128)}, u32[]{:S(2)}) %copy-start) | copy-done | bytes 98328
  2.2 0.0 copy-start.1
  2.2 0.8 %copy-done.1 = f32[2,1,6144]{2,1,0:T(1,128)S(1)} copy-done((f32[2,1,6144]{2,1,0:T(1,128)S(1)}, f32[2,1,6144]{2,1,0:T(1,128)}, u32[]{:S(2)}) %copy-start.1) | copy-done | bytes 49176
  3.0 0.0 copy-start.2
  3.0 0.8 %copy-done.2 = f32[2,6144]{1,0:T(2,128)S(1)} copy-done((f32[2,6144]{1,0:T(2,128)S(1)}, f32[2,6144]{1,0:T(2,128)}, u32[]{:S(2)}) %copy-start.2) | copy-done | bytes 49176
  3.8 0.0 copy-start.3
  3.8 0.8 %copy-done.3 = bf16[32,512]{1,0:T(8,128)(2,1)S(1)} copy-done((bf16[32,512]{1,0:T(8,128)(2,1)S(1)}, bf16[32,512]{1,0:T(8,128)(2,1)}, u32[]{:S(2)}) %copy-start.3) | copy-done | bytes 32792
  4.6 0.0 copy-start.4
  4.6 0.7 %copy-done.4 = f32[1,6144]{1,0:T(1,128)S(1)} copy-done((f32[1,6144]{1,0:T(1,128)S(1)}, f32[1,6144]{1,0:T(1,128)}, u32[]{:S(2)}) %copy-start.4) | copy-done | bytes 24600
  5.3 0.0 copy-start.5
  5.3 0.7 %copy-done.5 = f32[1,6144]{1,0:T(1,128)S(1)} copy-done((f32[1,6144]{1,0:T(1,128)S(1)}, f32[1,6144]{1,0:T(1,128)}, u32[]{:S(2)}) %copy-start.5) | copy-done | bytes 24600
  6.1 0.7 %copy-done.6 = f32[1,6144]{1,0:T(1,128)S(1)} copy-done((f32[1,6144]{1,0:T(1,128)S(1)}, f32[1,6144]{1,0:T(1,128)}, u32[]{:S(2)}) %copy-start.6) | copy-done | bytes 24600
  6.8 0.0 copy-start.7
  6.8 0.7 %copy-done.7 = f32[1,6144]{1,0:T(1,128)S(1)} copy-done((f32[1,6144]{1,0:T(1,128)S(1)}, f32[1,6144]{1,0:T(1,128)}, u32[]{:S(2)}) %copy-start.7) | copy-done | bytes 24600
  7.5 0.0 copy-start.8
  7.5 0.7 %copy-done.8 = f32[1,6144]{1,0:T(1,128)S(1)} copy-done((f32[1,6144]{1,0:T(1,128)S(1)}, f32[1,6144]{1,0:T(1,128)}, u32[]{:S(2)}) %copy-start.8) | copy-done | bytes 24600
  8.3 2.5 %pack.1 = bf16[8,184,128]{2,1,0:T(8,128)(2,1)S(1)} custom-call(f32[48,128]{1,0:T(8,128)S(1)} %bitcast.23, f32[48,128]{1,0:T(8,128)S(1)} %bitcast.24, f32[48,128]{1,0:T(8,128)S(1)} %bitcast.25, f32[2,48,128]{2,1,0:T(8,128)S(1)} %bitcast.21, f32[48,2,128]{2,1,0:T(2,128)S(1)} %bitcast.22, s32[48,4,128]{2,1,0:T(4,128)S(1)} %bitcast.20, ...), custom_call_target="tpu_custom_call" | custom-call | tf_op jit(solution)/shard_map/pack/pallas_call | solution.py:432
  10.8 18.9 %all_to_all.10.mine_ref = bf16[8,184,128]{2,1,0:T(8,128)(2,1)S(1)} all-to-all(bf16[8,184,128]{2,1,0:T(8,128)(2,1)S(1)} %pack.1), channel_id=1, replica_groups={{0,2,4,6,8,10,12,14},{1,3,5,7,9,11,13,15},{16,18,20,22,24,26,28,30},{17..., dimensions={0} | all-to-all | bytes 753664 | tf_op jit(solution)/shard_map/all_to_all | solution.py:425
  29.6 0.0 collective-permute-start
  29.7 0.6 %copy-done.11 = s32[16]{0:T(128)S(1)} copy-done((s32[16]{0:T(128)S(1)}, s32[16]{0:T(128)}, u32[]{:S(2)}) %copy-start.11) | copy-done | bytes 88
  30.3 0.0 copy-done.12
  30.3 0.0 copy-done.13
  30.3 0.1 operators.1
  30.5 0.9 %collective-permute-done.other_ref = bf16[8,184,128]{2,1,0:T(8,128)(2,1)S(1)} collective-permute-done((bf16[8,184,128]{2,1,0:T(8,128)(2,1)S(1)}, bf16[8,184,128]{2,1,0:T(8,128)(2,1)S(1)}, u32[]{:S(2)}, u32[]{:S(2)}) %collective-permute-start) | collective-permute-done | bytes 376864 | tf_op jit(solution)/shard_map/ppermute | solution.py:442
  31.3 2.9 %column_step.1 = bf16[8,168,128]{2,1,0:T(8,128)(2,1)S(1)} custom-call(bf16[8,184,128]{2,1,0:T(8,128)(2,1)S(1)} %all_to_all.10.mine_ref, bf16[8,184,128]{2,1,0:T(8,128)(2,1)S(1)} %collective-permute-done.other_ref, bf16[16,16]{1,0:T(8,128)(2,1)S(1)} %get-tuple-element.15.place_ref, f32[16,16]{1,0:T(8,128)S(1)} %get-tuple-element.16.inverse_ref, ...), custom_call_target="tpu_custom_call" | custom-call | tf_op jit(solution)/shard_map/column_step/pallas_call | solution.py:443
  34.2 14.5 %all_to_all.11.r_ref = bf16[8,168,128]{2,1,0:T(8,128)(2,1)S(1)} all-to-all(bf16[8,168,128]{2,1,0:T(8,128)(2,1)S(1)} %column_step.1), channel_id=1, replica_groups={{0,2,4,6,8,10,12,14},{1,3,5,7,9,11,13,15},{16,18,20,22,24,26,28,30},{17..., dimensions={0} | all-to-all | bytes 688128 | tf_op jit(solution)/shard_map/all_to_all | solution.py:425
  48.7 0.7 %finish.1 = (f32[48,128]{1,0:T(8,128)}, f32[48,128]{1,0:T(8,128)}, f32[48,128]{1,0:T(8,128)}, f32[4,512]{1,0:T(4,128)}, f32[32,512]{1,0:T(8,128)}, /*index=5*/f32[16,32]{1,0:T(8,128)}) custom-call(bf16[8,168,128]{2,1,0:T(8,128)(2,1)S(1)} %all_to_all.11.r_ref), custom_call_target="tpu_custom_call" | custom-call | tf_op jit(solution)/shard_map/finish/pallas_call | solution.py:453
  (4 shorter events, 0.0 us)
Async XLA Ops:
  0.6 0.7 %copy-start.10 = (bf16[32,16]{0,1:T(8,128)(2,1)S(1)}, bf16[32,16]{0,1:T(8,128)(2,1)}, u32[]{:S(2)}) copy-start(bf16[32,16]{0,1:T(8,128)(2,1)} %param.25) | copy-start | bytes 3076
  0.6 0.7 %copy-start.9 = (bf16[4,512]{1,0:T(4,128)(2,1)S(1)}, bf16[4,512]{1,0:T(4,128)(2,1)}, u32[]{:S(2)}) copy-start(bf16[4,512]{1,0:T(4,128)(2,1)} %one_hbm.1) | copy-start | bytes 12292
  1.3 0.9 %copy-start = (s32[4,6144]{1,0:T(4,128)S(1)}, s32[4,6144]{1,0:T(4,128)}, u32[]{:S(2)}) copy-start(s32[4,6144]{1,0:T(4,128)} %param.19) | copy-start | bytes 294916
  2.2 0.8 %copy-start.1 = (f32[2,1,6144]{2,1,0:T(1,128)S(1)}, f32[2,1,6144]{2,1,0:T(1,128)}, u32[]{:S(2)}) copy-start(f32[2,1,6144]{2,1,0:T(1,128)} %param.17) | copy-start | bytes 147460
  3.0 0.8 %copy-start.2 = (f32[2,6144]{1,0:T(2,128)S(1)}, f32[2,6144]{1,0:T(2,128)}, u32[]{:S(2)}) copy-start(f32[2,6144]{1,0:T(2,128)} %param.18) | copy-start | bytes 147460
  3.8 0.8 %copy-start.3 = (bf16[32,512]{1,0:T(8,128)(2,1)S(1)}, bf16[32,512]{1,0:T(8,128)(2,1)}, u32[]{:S(2)}) copy-start(bf16[32,512]{1,0:T(8,128)(2,1)} %two_hbm.1) | copy-start | bytes 98308
  4.6 0.7 %copy-start.4 = (f32[1,6144]{1,0:T(1,128)S(1)}, f32[1,6144]{1,0:T(1,128)}, u32[]{:S(2)}) copy-start(f32[1,6144]{1,0:T(1,128)} %param.14) | copy-start | bytes 73732
  5.3 0.7 %copy-start.5 = (f32[1,6144]{1,0:T(1,128)S(1)}, f32[1,6144]{1,0:T(1,128)}, u32[]{:S(2)}) copy-start(f32[1,6144]{1,0:T(1,128)} %param.15) | copy-start | bytes 73732
  6.1 0.7 %copy-start.6 = (f32[1,6144]{1,0:T(1,128)S(1)}, f32[1,6144]{1,0:T(1,128)}, u32[]{:S(2)}) copy-start(f32[1,6144]{1,0:T(1,128)} %param.16) | copy-start | bytes 73732
  6.8 0.7 %copy-start.7 = (f32[1,6144]{1,0:T(1,128)S(1)}, f32[1,6144]{1,0:T(1,128)}, u32[]{:S(2)}) copy-start(f32[1,6144]{1,0:T(1,128)} %param.26) | copy-start | bytes 73732
  7.5 0.7 %copy-start.8 = (f32[1,6144]{1,0:T(1,128)S(1)}, f32[1,6144]{1,0:T(1,128)}, u32[]{:S(2)}) copy-start(f32[1,6144]{1,0:T(1,128)} %param.27) | copy-start | bytes 73732
  29.6 1.7 %collective-permute-start = (bf16[8,184,128]{2,1,0:T(8,128)(2,1)S(1)}, bf16[8,184,128]{2,1,0:T(8,128)(2,1)S(1)}, u32[]{:S(2)}, u32[]{:S(2)}) collective-permute-start(bf16[8,184,128]{2,1,0:T(8,128)(2,1)S(1)} %all_to_all.10.mine_ref), channel_id=1, source_target_pairs={{0,1},{1,0},{2,3},{3,2},{4,5},{5,4},{6,7},{7,6},{8,9},{9,8},{10,11... | collective-permute-start | bytes 1130504 | tf_op jit(solution)/shard_map/ppermute | solution.py:442
  29.6 0.7 %copy-start.11 = (s32[16]{0:T(128)S(1)}, s32[16]{0:T(128)}, u32[]{:S(2)}) copy-start(s32[16]{0:T(128)} %param.20) | copy-start | bytes 196
  29.6 0.7 %copy-start.12 = (f32[16]{0:T(128)S(1)}, f32[16]{0:T(128)}, u32[]{:S(2)}) copy-start(f32[16]{0:T(128)} %param.21) | copy-start | bytes 196
  29.6 0.7 %copy-start.13 = (f32[16]{0:T(128)S(1)}, f32[16]{0:T(128)}, u32[]{:S(2)}) copy-start(f32[16]{0:T(128)} %param.22) | copy-start | bytes 196

commit v3 on v2

--- a/solution.py
+++ b/solution.py
@@ -434,7 +434,7 @@
         [pltpu.VMEM(source.shape, source.dtype) for source in sources]
         + [pltpu.VMEM((16, LANE), f32), pltpu.VMEM((chips * rest, LANE), f32), pltpu.SemaphoreType.DMA((len(sources),))],
         pltpu.HBM,
-    )(*sources)
+    )(*(pltpu.with_memory_space_constraint(source, pltpu.HBM) for source in sources))
     operators = call(
         operator_kernel, "operators", (shape((levels, levels), bf16), shape((levels, levels), f32), shape((levels, LANE), f32)), 3
     )(level_order.reshape(1, levels), stiffness.reshape(1, levels), coupling.reshape(1, levels))

time: 50.1 us -> 42.4 us (0.85); the launches traced: 49.3 us -> 42.2 us
  local copies, waits for them, and re-layouts: 8.3 us -> 0.68 us
  Pallas kernels: 6.16 us -> 6.67 us
    unnamed x28 -> x6, local copies, waits for them, and re-layouts: 8.3 us -> 0.68 us
where the time goes in v3:
time: 42.4 us; the launch traced here: 42.2 us
  blocking collectives  33.3 us (79%)
  Pallas kernels  6.67 us (16%)
  waiting for transfers between devices  0.88 us (2%)
  local copies, waits for them, and re-layouts  0.68 us (2%)
  between operations  0.67 us (2%)
    all_to_all x2, blocking collectives, exchange(): lax.all_to_all(blocks_of_chips, 'slab', split_axis=0, concat_axis=0, tile...  33.3 us
    pallas_call x1, Pallas kernels, fast_body(): call(pack_kernel, 'pack', shape((chips, TAIL + rest, LANE), bf16), len(so...  2.99 us
    pallas_call x1, Pallas kernels, fast_body(): call(column_kernel, 'column_step', shape((chips, TAIL + back, LANE), bf16...  2.87 us
    ppermute x1, waiting for transfers between devices, fast_body(): other = lax.ppermute(mine, 'slab', [(i, i ^ 1) for i in range(devices)])  0.88 us
  transfers between devices with their start and end apart: 1, of which 1 were waited for; matrix products, arithmetic and copies ran while one was open for 0% of the time, Pallas kernels for 0%

profile of v3, /device:TPU:0, one launch (start us, length us, event | category | flops | bytes accessed | tf_op | source)
XLA Modules:
  0.0 42.2 jit_solution(16578306572207666613)
XLA Ops:
  0.6 3.0 %pack.1 = bf16[8,184,128]{2,1,0:T(8,128)(2,1)S(1)} custom-call(f32[48,128]{1,0:T(8,128)} %bitcast.26, f32[48,128]{1,0:T(8,128)} %bitcast.27, f32[48,128]{1,0:T(8,128)} %bitcast.28, f32[2,48,128]{2,1,0:T(8,128)} %bitcast.24, f32[48,2,128]{2,1,0:T(2,128)} %bitcast.25, s32[48,4,128]{2,1,0:T(4,128)} %bitcast.23, bf16[4,512]{1,0:T(4,128)(2,1)} %one_hbm.1, ...), custom_call_target="tpu_custom_call" | custom-call | tf_op jit(solution)/shard_map/pack/pallas_call | solution.py:432
  3.6 18.9 %all_to_all.10.mine_ref = bf16[8,184,128]{2,1,0:T(8,128)(2,1)S(1)} all-to-all(bf16[8,184,128]{2,1,0:T(8,128)(2,1)S(1)} %pack.1), channel_id=1, replica_groups={{0,2,4,6,8,10,12,14},{1,3,5,7,9,11,13,15},{16,18,20,22,24,26,28,30},{17..., dimensions={0} | all-to-all | bytes 753664 | tf_op jit(solution)/shard_map/all_to_all | solution.py:425
  22.5 0.0 collective-permute-start
  22.5 0.0 copy-start
  22.5 0.0 copy-start.1
  22.5 0.0 copy-start.2
  22.5 0.6 %copy-done = s32[16]{0:T(128)S(1)} copy-done((s32[16]{0:T(128)S(1)}, s32[16]{0:T(128)}, u32[]{:S(2)}) %copy-start) | copy-done | bytes 88
  23.2 0.0 copy-done.1
  23.2 0.0 copy-done.2
  23.2 0.1 operators.1
  23.3 0.9 %collective-permute-done.other_ref = bf16[8,184,128]{2,1,0:T(8,128)(2,1)S(1)} collective-permute-done((bf16[8,184,128]{2,1,0:T(8,128)(2,1)S(1)}, bf16[8,184,128]{2,1,0:T(8,128)(2,1)S(1)}, u32[]{:S(2)}, u32[]{:S(2)}) %collective-permute-start) | collective-permute-done | bytes 376864 | tf_op jit(solution)/shard_map/ppermute | solution.py:442
  24.2 2.9 %column_step.1 = bf16[8,168,128]{2,1,0:T(8,128)(2,1)S(1)} custom-call(bf16[8,184,128]{2,1,0:T(8,128)(2,1)S(1)} %all_to_all.10.mine_ref, bf16[8,184,128]{2,1,0:T(8,128)(2,1)S(1)} %collective-permute-done.other_ref, bf16[16,16]{1,0:T(8,128)(2,1)S(1)} %get-tuple-element.15.place_ref, f32[16,16]{1,0:T(8,128)S(1)} %get-tuple-element.16.inverse_ref, ...), custom_call_target="tpu_custom_call" | custom-call | tf_op jit(solution)/shard_map/column_step/pallas_call | solution.py:443
  27.1 14.4 %all_to_all.11.r_ref = bf16[8,168,128]{2,1,0:T(8,128)(2,1)S(1)} all-to-all(bf16[8,168,128]{2,1,0:T(8,128)(2,1)S(1)} %column_step.1), channel_id=1, replica_groups={{0,2,4,6,8,10,12,14},{1,3,5,7,9,11,13,15},{16,18,20,22,24,26,28,30},{17..., dimensions={0} | all-to-all | bytes 688128 | tf_op jit(solution)/shard_map/all_to_all | solution.py:425
  41.5 0.7 %finish.1 = (f32[48,128]{1,0:T(8,128)}, f32[48,128]{1,0:T(8,128)}, f32[48,128]{1,0:T(8,128)}, f32[4,512]{1,0:T(4,128)}, f32[32,512]{1,0:T(8,128)}, /*index=5*/f32[16,32]{1,0:T(8,128)}) custom-call(bf16[8,168,128]{2,1,0:T(8,128)(2,1)S(1)} %all_to_all.11.r_ref), custom_call_target="tpu_custom_call" | custom-call | tf_op jit(solution)/shard_map/finish/pallas_call | solution.py:453
Async XLA Ops:
  22.5 1.7 %collective-permute-start = (bf16[8,184,128]{2,1,0:T(8,128)(2,1)S(1)}, bf16[8,184,128]{2,1,0:T(8,128)(2,1)S(1)}, u32[]{:S(2)}, u32[]{:S(2)}) collective-permute-start(bf16[8,184,128]{2,1,0:T(8,128)(2,1)S(1)} %all_to_all.10.mine_ref), channel_id=1, source_target_pairs={{0,1},{1,0},{2,3},{3,2},{4,5},{5,4},{6,7},{7,6},{8,9},{9,8},{10,11... | collective-permute-start | bytes 1130504 | tf_op jit(solution)/shard_map/ppermute | solution.py:442
  22.5 0.7 %copy-start = (s32[16]{0:T(128)S(1)}, s32[16]{0:T(128)}, u32[]{:S(2)}) copy-start(s32[16]{0:T(128)} %param.20) | copy-start | bytes 196
  22.5 0.7 %copy-start.1 = (f32[16]{0:T(128)S(1)}, f32[16]{0:T(128)}, u32[]{:S(2)}) copy-start(f32[16]{0:T(128)} %param.21) | copy-start | bytes 196
  22.5 0.7 %copy-start.2 = (f32[16]{0:T(128)S(1)}, f32[16]{0:T(128)}, u32[]{:S(2)}) copy-start(f32[16]{0:T(128)} %param.22) | copy-start | bytes 196

commit v4 on v3

--- a/solution.py
+++ b/solution.py
@@ -140,6 +140,7 @@
 
 LANE = 128
 SUB = 8
+GROUPS = 4
 PIECE = 32
 HEAD = 4 * PIECE
 TAIL = HEAD + 16
@@ -196,13 +197,13 @@
         copy.start()
     f32, bf16 = jnp.float32, jnp.bfloat16
     chips = out_ref.shape[0]
-    rest = out_ref.shape[1] - TAIL
-    blocks = p_ref.shape[0] // chips
+    piece = f_ref.shape[0] // SUB
+    blocks = p_ref.shape[0] // SUB
     for copy in copies:
         copy.wait()
 
     def put(f, j, tile):
-        f_ref[pl.ds(4 + blocks * f + j, chips, stride=rest), :] = tile
+        f_ref[pl.ds(blocks * f + j, SUB, stride=piece), :] = tile
 
     for j in range(blocks):
         rows = slice(SUB * j, SUB * j + SUB)
@@ -226,10 +227,13 @@
         for q in range(4):
             out_ref[c, PIECE * q : PIECE * (q + 1), :] = two_ref[:, LANE * q : LANE * (q + 1)]
         out_ref[c, HEAD:TAIL, :] = one
-        f_ref[rest * c : rest * c + 4, :] = three
-        if rest > 4 + 6 * blocks:
-            f_ref[rest * c + 4 + 6 * blocks : rest * (c + 1), :] = jnp.zeros((rest - 4 - 6 * blocks, LANE), f32)
-        out_ref[c, TAIL:, :] = f_ref[rest * c : rest * (c + 1), :].astype(bf16)
+        f_ref[piece * c + 6 * blocks : piece * c + 6 * blocks + 4, :] = three
+        if piece > 6 * blocks + 4:
+            f_ref[piece * c + 6 * blocks + 4 : piece * (c + 1), :] = jnp.zeros((piece - 6 * blocks - 4, LANE), f32)
+    for g in range(GROUPS):
+        both = jnp.concatenate([f_ref[piece * c : piece * (c + 1), :] for c in (g, g + GROUPS)], axis=0).astype(bf16)
+        for c in range(g, chips, GROUPS):
+            out_ref[c, TAIL:, :] = both
 
 
 def shifted_up(field, rows):
@@ -270,18 +274,20 @@
 
 
 def column_kernel(
-    mine_ref, other_ref, place_ref, inverse_ref, column_ref, out_ref,
-    a_ref, one_ref, w2_ref, w3_ref, act_ref, sel_ref, g_ref, y_ref, t_ref,
+    mine_ref, other_ref, place_ref, inverse_ref, column_ref, out0_ref, out1_ref, out2_ref, out3_ref,
+    a_ref, one_ref, w2_ref, w3_ref, act_ref, sel_ref, g_ref, h_ref, y_ref, t_ref,
 ):
     f32, bf16 = jnp.float32, jnp.bfloat16
-    core = lax.axis_index("slab") % 2
-    first = core == 0
+    device = lax.axis_index("slab")
+    core = device % 2
     chips = mine_ref.shape[0]
     devices = 2 * chips
     levels = inverse_ref.shape[0]
     width = act_ref.shape[1]
     blocks = width // LANE
     stride = mine_ref.shape[1] - HEAD
+    piece = (stride - 16) // 2
+    half = blocks // 2
     for ref, which in ((mine_ref, core), (other_ref, 1 - core)):
         for c in range(chips):
             for q in range(4):
@@ -295,7 +301,7 @@
     one = jnp.concatenate([one_ref[4 * devices * q : 4 * devices * (q + 1), :] for q in range(4)], axis=1)
     lanes = lax.broadcasted_iota(jnp.int32, (4, LANE), 1)
     for t in range(devices // 4):
-        packed = [a_ref[stride * (4 * t + s) + 16 : stride * (4 * t + s) + 20, :] for s in range(4)]
+        packed = [a_ref[pl.ds(stride * (4 * t + s) + 16 + 6 * half, 4), :] for s in range(4)]
         for q in range(4):
             tile = jnp.zeros((4, LANE), f32)
             for s in range(4):
@@ -308,7 +314,8 @@
     w3t = w3_ref[...].astype(bf16)
     w3 = w3_ref[...].T.astype(bf16)
     place, inverse = place_ref[...], inverse_ref[...]
-    raw = jnp.concatenate([a_ref[pl.ds(20 + k, levels, stride=stride), :] for k in range(6 * blocks)], axis=1)
+    order = [16 + piece * b + half * f + j for f in range(6) for b in range(2) for j in range(half)]
+    raw = jnp.concatenate([a_ref[pl.ds(k, levels, stride=stride), :] for k in order], axis=1)
     ordered = jnp.dot(place, raw.astype(bf16), preferred_element_type=f32)
     star, density, vertical, diverg, pressure_adjoint, wind_adjoint = (
         ordered[:, width * i : width * (i + 1)] for i in range(6)
@@ -342,60 +349,64 @@
     wind_next = solve(vertical - couple * lower(star) - 0.5 * density + heating)
     press_next = star + upper(couple * wind_next)
     star_grad = star_part + jnp.dot(w1s, pre_one_grad, preferred_element_type=f32)
-    for c in range(chips):
-        rows = pl.ds(pl.multiple_of(2 * PIECE * c + PIECE * core, PIECE), PIECE)
-        sel_ref[PIECE * c : PIECE * (c + 1), :] = act_ref[rows, :]
+    outs = (out0_ref, out1_ref, out2_ref, out3_ref)
+    targets = [device ^ (2 * k) for k in range(GROUPS)]
+    for k, target in enumerate(targets):
+        sel_ref[PIECE * k : PIECE * (k + 1), :] = act_ref[pl.ds(pl.multiple_of(PIECE * target, PIECE), PIECE), :]
     local_two = contract_last(sel_ref[...], pre_two_grad)
     local_three = contract_last(heat_grad, act_two)
-    local_one = contract_last(column_input, pre_one_grad)
+    g_ref[...] = contract_last(column_input, pre_one_grad)
     fields = jnp.concatenate([press_next, wind_next, star_grad], axis=1).astype(bf16)
     stored = lax.dot_general(place, fields, (((0,), (0,)), ((), ())), preferred_element_type=f32)
-    back = out_ref.shape[1] - TAIL
+    back = out0_ref.shape[0] - TAIL
     for k in range(3 * blocks):
         y_ref[pl.ds(4 + k, devices, stride=back), :] = stored[:, LANE * k : LANE * (k + 1)]
     for k in range(4 + 3 * blocks, back):
         y_ref[pl.ds(k, devices, stride=back), :] = jnp.zeros((devices, LANE), f32)
     for t in range(devices // 4):
-        tile = local_three[:, LANE * t : LANE * (t + 1)]
-        t_ref[16 * t : 16 * t + 16, :] = jnp.where(first, tile, pltpu.roll(tile, LANE - PIECE, 1))
-    for c in range(chips):
-        mine = jnp.where(first, local_one[8 * c : 8 * c + 4, :], local_one[8 * c + 4 : 8 * c + 8, :])
-        three = jnp.zeros((4, LANE), f32)
+        t_ref[16 * t : 16 * t + 16, :] = local_three[:, LANE * t : LANE * (t + 1)]
+    for k, (target, out_ref) in enumerate(zip(targets, outs)):
+        pair = g_ref[pl.ds(pl.multiple_of(SUB * (target // 2), SUB), SUB), :]
+        one = jnp.where(core == 0, pair[:4, :], pair[4:, :])
+        tile = t_ref[pl.ds(pl.multiple_of(16 * (target // 4), 16), 16), :]
+        tile = pltpu.roll(tile, (LANE - PIECE * (target % 4)) % LANE, 1)
+        three = tile[:4, :]
         for q in range(4):
             cols = slice(LANE * q, LANE * (q + 1))
-            out_ref[c, PIECE * q : PIECE * (q + 1), :] = local_two[PIECE * c : PIECE * (c + 1), cols].astype(bf16)
-            g_ref[4 * q : 4 * q + 4, :] = mine[:, cols]
-            moved = t_ref[16 * (c // 2) + 4 * q : 16 * (c // 2) + 4 * q + 4, :]
-            if q != 2 * (c % 2):
-                moved = pltpu.roll(moved, PIECE * ((q - 2 * (c % 2)) % 4), 1)
-            three = jnp.where(lane_group(lanes, q), moved, three)
-        out_ref[c, HEAD:TAIL, :] = g_ref[...].astype(bf16)
-        start = pl.multiple_of(back * (2 * c + core), SUB)
+            out_ref[PIECE * q : PIECE * (q + 1), :] = local_two[PIECE * k : PIECE * (k + 1), cols].astype(bf16)
+            h_ref[4 * q : 4 * q + 4, :] = one[:, cols]
+            if q > 0:
+                three = jnp.where(lane_group(lanes, q), pltpu.roll(tile[4 * q : 4 * q + 4, :], PIECE * q, 1), three)
+        out_ref[HEAD:TAIL, :] = h_ref[...].astype(bf16)
+        start = pl.multiple_of(back * target, SUB)
         y_ref[pl.ds(start, 4), :] = three
-        out_ref[c, TAIL:, :] = y_ref[pl.ds(start, back), :].astype(bf16)
-
-
-def finish_kernel(scale, r_ref, p_ref, w_ref, g_ref, one_ref, two_ref, three_ref, y_ref):
-    chips = r_ref.shape[0]
-    back = r_ref.shape[1] - TAIL
-    blocks = p_ref.shape[0] // chips
+        out_ref[TAIL:, :] = y_ref[pl.ds(start, back), :].astype(bf16)
+
+
+def finish_kernel(scale, r0_ref, r1_ref, r2_ref, r3_ref, p_ref, w_ref, g_ref, one_ref, two_ref, three_ref, y_ref):
+    received = (r0_ref, r1_ref, r2_ref, r3_ref)
+    back = r0_ref.shape[0] - TAIL
+    half = p_ref.shape[0] // SUB
+    group = lax.axis_index("slab") // 2 % GROUPS
 
     def total(start, stop):
-        return sum(r_ref[c, start:stop, :].astype(jnp.float32) for c in range(chips)) * scale
+        return sum(ref[start:stop, :].astype(jnp.float32) for ref in received) * scale
 
     for q in range(4):
         two_ref[:, LANE * q : LANE * (q + 1)] = total(PIECE * q, PIECE * (q + 1))
     one = total(HEAD, TAIL)
     for q in range(4):
         one_ref[:, LANE * q : LANE * (q + 1)] = one[4 * q : 4 * q + 4, :]
-    for c in range(chips):
-        y_ref[back * c : back * (c + 1), :] = r_ref[c, TAIL:, :].astype(jnp.float32)
-    three = sum(y_ref[back * c : back * c + 4, :] for c in range(chips)) * scale
+    for k, ref in enumerate(received):
+        y_ref[pl.ds(pl.multiple_of(back * (group ^ k), SUB), back), :] = ref[TAIL:, :].astype(jnp.float32)
+    three = sum(y_ref[back * g : back * g + 4, :] for g in range(GROUPS)) * scale
     for q in range(4):
         three_ref[4 * q : 4 * q + 4, :] = three[:, PIECE * q : PIECE * (q + 1)]
     for f, ref in enumerate((p_ref, w_ref, g_ref)):
-        for j in range(blocks):
-            ref[chips * j : chips * (j + 1), :] = y_ref[pl.ds(4 + blocks * f + j, chips, stride=back), :]
+        for j in range(half):
+            for b in range(2):
+                rows = pl.ds(4 + 2 * half * f + half * b + j, GROUPS, stride=back)
+                ref[SUB * j + GROUPS * b : SUB * j + GROUPS * (b + 1), :] = y_ref[rows, :]
 
 
 def fast_body(
@@ -406,7 +417,7 @@
     columns = neighbors.shape[1]
     rows = columns // LANE
     chips = devices // 2
-    blocks = rows // chips
+    blocks = rows // GROUPS
     width = blocks * LANE
     hidden = weight_two.shape[1]
     f32, bf16 = jnp.float32, jnp.bfloat16
@@ -428,11 +439,11 @@
         view(pressure), view(density), view(vertical_wind), horizontal_wind.reshape(2, rows, LANE), lanes(metric_terms),
         lanes(neighbors), weight_one, weight_two, weight_three.T, view(pressure_adjoint), view(wind_adjoint),
     )
-    rest, back = pad(4 + 6 * blocks), pad(4 + 3 * blocks)
+    piece, back = pad(4 + 3 * blocks), pad(4 + 3 * blocks)
     send = call(
-        pack_kernel, "pack", shape((chips, TAIL + rest, LANE), bf16), len(sources),
+        pack_kernel, "pack", shape((chips, TAIL + 2 * piece, LANE), bf16), len(sources),
         [pltpu.VMEM(source.shape, source.dtype) for source in sources]
-        + [pltpu.VMEM((16, LANE), f32), pltpu.VMEM((chips * rest, LANE), f32), pltpu.SemaphoreType.DMA((len(sources),))],
+        + [pltpu.VMEM((16, LANE), f32), pltpu.VMEM((SUB * piece, LANE), f32), pltpu.SemaphoreType.DMA((len(sources),))],
         pltpu.HBM,
     )(*(pltpu.with_memory_space_constraint(source, pltpu.HBM) for source in sources))
     operators = call(
@@ -440,15 +451,19 @@
     )(level_order.reshape(1, levels), stiffness.reshape(1, levels), coupling.reshape(1, levels))
     mine = exchange(send)
     other = lax.ppermute(mine, "slab", [(i, i ^ 1) for i in range(devices)])
+    block = shape((TAIL + back, LANE), bf16)
     send_back = call(
-        column_kernel, "column_step", shape((chips, TAIL + back, LANE), bf16), 5,
+        column_kernel, "column_step", (block,) * GROUPS, 5,
         [
-            pltpu.VMEM((devices * (16 + rest), LANE), f32), pltpu.VMEM((16 * devices, LANE), f32),
+            pltpu.VMEM((devices * (16 + 2 * piece), LANE), f32), pltpu.VMEM((16 * devices, LANE), f32),
             pltpu.VMEM((hidden, hidden), bf16), pltpu.VMEM((levels, hidden), f32), pltpu.VMEM((hidden, width), bf16),
-            pltpu.VMEM((hidden // 2, width), bf16), pltpu.VMEM((16, LANE), f32), pltpu.VMEM((devices * back, LANE), f32),
-            pltpu.VMEM((4 * devices, LANE), f32),
+            pltpu.VMEM((GROUPS * PIECE, width), bf16), pltpu.VMEM((4 * levels, hidden), f32), pltpu.VMEM((16, LANE), f32),
+            pltpu.VMEM((devices * back, LANE), f32), pltpu.VMEM((4 * devices, LANE), f32),
         ],
     )(mine, other, *operators)
+    received = [send_back[0]] + [
+        lax.ppermute(send_back[k], "slab", [(i, i ^ (2 * k)) for i in range(devices)]) for k in range(1, GROUPS)
+    ]
     field_out = shape((rows, LANE), f32)
     new_pressure, new_wind, grad, first_grad, second_grad, third_grad = call(
         functools.partial(finish_kernel, 1.0 / math.sqrt(columns)), "finish",
@@ -456,9 +471,9 @@
             field_out, field_out, field_out, shape(weight_one.shape, f32), shape(weight_two.shape, f32),
             shape(weight_three.shape[::-1], f32),
         ),
-        1,
-        [pltpu.VMEM((chips * back, LANE), f32)],
-    )(exchange(send_back))
+        GROUPS,
+        [pltpu.VMEM((GROUPS * back, LANE), f32)],
+    )(*received)
     return (
         new_pressure.reshape(1, columns), new_wind.reshape(1, columns), grad.reshape(1, columns),
         first_grad, second_grad, third_grad.T,

time: 42.4 us -> 38.6 us (0.910)
  blocking collectives: 33.3 us -> 20.3 us
  starting transfers between devices: 0.01 us -> 3.55 us
  waiting for transfers between devices: 0.88 us -> 3.86 us
  Pallas kernels: 6.67 us -> 9.36 us
    all_to_all x2 -> x1, blocking collectives: 33.3 us -> 20.3 us  [exchange(): lax.all_to_all(blocks_of_chips, 'slab', split_axis=0, concat_axis=0, tile...]
    ppermute x0 -> x3, starting transfers between devices: none -> 3.55 us  [fast_body(): lax.ppermute(send_back[k], 'slab', [(i, i ^ 2 * k) for i in range(devices)])]
    ppermute x0 -> x3, waiting for transfers between devices: none -> 2.87 us  [fast_body(): lax.ppermute(send_back[k], 'slab', [(i, i ^ 2 * k) for i in range(devices)])]
    pallas_call x2, Pallas kernels: 5.85 us -> 8.54 us  [the longest x1 5.55 us: fast_body(): call(column_kernel, 'column_step', (block,) * GROUPS, 5, [pltpu.VMEM((dev...]
  transfers between devices with their start and end apart: 1 -> 4, of which waited for: 1 -> 4; matrix products, arithmetic and copies ran while one was open for 0% -> 0% of each run, Pallas kernels for 0% -> 0%
where the time goes in v4:
time: 38.6 us; the launch traced here: 38.4 us
  blocking collectives  20.3 us (53%)
  Pallas kernels  9.36 us (24%)
  waiting for transfers between devices  3.86 us (10%)
  starting transfers between devices  3.55 us (9%)
  local copies, waits for them, and re-layouts  0.68 us (2%)
  between operations  0.67 us (2%)
    all_to_all x1, blocking collectives, exchange(): lax.all_to_all(blocks_of_chips, 'slab', split_axis=0, concat_axis=0, tile...  20.3 us
    pallas_call x1, Pallas kernels, fast_body(): call(column_kernel, 'column_step', (block,) * GROUPS, 5, [pltpu.VMEM((dev...  5.55 us
    ppermute x3, starting transfers between devices, fast_body(): lax.ppermute(send_back[k], 'slab', [(i, i ^ 2 * k) for i in range(devices)])  3.55 us
    pallas_call x1, Pallas kernels, fast_body(): call(pack_kernel, 'pack', shape((chips, TAIL + 2 * piece, LANE), bf16), l...  2.99 us
    ppermute x3, waiting for transfers between devices, fast_body(): lax.ppermute(send_back[k], 'slab', [(i, i ^ 2 * k) for i in range(devices)])  2.87 us
    ppermute x1, waiting for transfers between devices, fast_body(): other = lax.ppermute(mine, 'slab', [(i, i ^ 1) for i in range(devices)])  0.99 us
  transfers between devices with their start and end apart: 4, of which 4 were waited for; matrix products, arithmetic and copies ran while one was open for 0% of the time, Pallas kernels for 0%

profile of v4, /device:TPU:0, one launch (start us, length us, event | category | flops | bytes accessed | tf_op | source)
XLA Modules:
  0.0 38.4 jit_solution(11342020970305264387)
XLA Ops:
  0.6 3.0 %pack.1 = bf16[8,224,128]{2,1,0:T(8,128)(2,1)S(1)} custom-call(f32[48,128]{1,0:T(8,128)} %bitcast.26, f32[48,128]{1,0:T(8,128)} %bitcast.27, f32[48,128]{1,0:T(8,128)} %bitcast.28, f32[2,48,128]{2,1,0:T(8,128)} %bitcast.24, f32[48,2,128]{2,1,0:T(2,128)} %bitcast.25, s32[48,4,128]{2,1,0:T(4,128)} %bitcast.23, bf16[4,512]{1,0:T(4,128)(2,1)} %one_hbm.1, ...), custom_call_target="tpu_custom_call" | custom-call | tf_op jit(solution)/shard_map/pack/pallas_call | solution.py:443
  3.6 20.3 %all_to_all.5.mine_ref = bf16[8,224,128]{2,1,0:T(8,128)(2,1)S(1)} all-to-all(bf16[8,224,128]{2,1,0:T(8,128)(2,1)S(1)} %pack.1), channel_id=1, replica_groups={{0,2,4,6,8,10,12,14},{1,3,5,7,9,11,13,15},{16,18,20,22,24,26,28,30},{17..., dimensions={0} | all-to-all | bytes 917504 | tf_op jit(solution)/shard_map/all_to_all | solution.py:436
  23.9 0.0 collective-permute-start
  23.9 0.0 copy-start
  23.9 0.0 copy-start.1
  23.9 0.0 copy-start.2
  23.9 0.6 %copy-done = s32[16]{0:T(128)S(1)} copy-done((s32[16]{0:T(128)S(1)}, s32[16]{0:T(128)}, u32[]{:S(2)}) %copy-start) | copy-done | bytes 88
  24.6 0.0 copy-done.1
  24.6 0.0 copy-done.2
  24.6 0.1 operators.1
  24.7 1.0 %collective-permute-done.other_ref = bf16[8,224,128]{2,1,0:T(8,128)(2,1)S(1)} collective-permute-done((bf16[8,224,128]{2,1,0:T(8,128)(2,1)S(1)}, bf16[8,224,128]{2,1,0:T(8,128)(2,1)S(1)}, u32[]{:S(2)}, u32[]{:S(2)}) %collective-permute-start) | collective-permute-done | bytes 458784 | tf_op jit(solution)/shard_map/ppermute | solution.py:453
  25.7 5.5 %column_step.1 = (bf16[184,128]{1,0:T(8,128)(2,1)S(1)}, bf16[184,128]{1,0:T(8,128)(2,1)S(1)}, bf16[184,128]{1,0:T(8,128)(2,1)S(1)}, bf16[184,128]{1,0:T(8,128)(2,1)S(1)}) custom-call(bf16[8,224,128]{2,1,0:T(8,128)(2,1)S(1)} %all_to_all.5.mine_ref, bf16[8,224,128]{2,1,0:T(8,128)(2,1)S(1)} %collective-permute-done.other_ref, ...), custom_call_target="tpu_custom_call" | custom-call | tf_op jit(solution)/shard_map/column_step/pallas_call | solution.py:455
  31.3 1.4 %collective-permute-start.1 = (bf16[184,128]{1,0:T(8,128)(2,1)S(1)}, bf16[184,128]{1,0:T(8,128)(2,1)S(1)}, u32[]{:S(2)}, u32[]{:S(2)}) collective-permute-start(bf16[184,128]{1,0:T(8,128)(2,1)S(1)} %get-tuple-element.23), channel_id=1, source_target_pairs={{0,2},{1,3},{2,0},{3,1},{4,6},{5,7},{6,4},{7,5},{8,10},{9,11},{10,... | collective-permute-start | bytes 141320 | tf_op jit(solution)/shard_map/ppermute | solution.py:465
  32.7 0.0 collective-permute-start.2
  32.7 2.1 %collective-permute-start.3 = (bf16[184,128]{1,0:T(8,128)(2,1)S(1)}, bf16[184,128]{1,0:T(8,128)(2,1)S(1)}, u32[]{:S(2)}, u32[]{:S(2)}) collective-permute-start(bf16[184,128]{1,0:T(8,128)(2,1)S(1)} %get-tuple-element.25), channel_id=1, source_target_pairs={{0,6},{1,7},{2,4},{3,5},{4,2},{5,3},{6,0},{7,1},{8,14},{9,15},{10,... | collective-permute-start | bytes 141320 | tf_op jit(solution)/shard_map/ppermute | solution.py:465
  34.8 0.6 %collective-permute-done.1.r1_ref = bf16[184,128]{1,0:T(8,128)(2,1)S(1)} collective-permute-done((bf16[184,128]{1,0:T(8,128)(2,1)S(1)}, bf16[184,128]{1,0:T(8,128)(2,1)S(1)}, u32[]{:S(2)}, u32[]{:S(2)}) %collective-permute-start.1) | collective-permute-done | bytes 47136 | tf_op jit(solution)/shard_map/ppermute | solution.py:465
  35.4 1.7 %collective-permute-done.2.r2_ref = bf16[184,128]{1,0:T(8,128)(2,1)S(1)} collective-permute-done((bf16[184,128]{1,0:T(8,128)(2,1)S(1)}, bf16[184,128]{1,0:T(8,128)(2,1)S(1)}, u32[]{:S(2)}, u32[]{:S(2)}) %collective-permute-start.2) | collective-permute-done | bytes 47136 | tf_op jit(solution)/shard_map/ppermute | solution.py:465
  37.1 0.6 %collective-permute-done.3.r3_ref = bf16[184,128]{1,0:T(8,128)(2,1)S(1)} collective-permute-done((bf16[184,128]{1,0:T(8,128)(2,1)S(1)}, bf16[184,128]{1,0:T(8,128)(2,1)S(1)}, u32[]{:S(2)}, u32[]{:S(2)}) %collective-permute-start.3) | collective-permute-done | bytes 47136 | tf_op jit(solution)/shard_map/ppermute | solution.py:465
  37.7 0.7 %finish.1 = (f32[48,128]{1,0:T(8,128)}, f32[48,128]{1,0:T(8,128)}, f32[48,128]{1,0:T(8,128)}, f32[4,512]{1,0:T(4,128)}, f32[32,512]{1,0:T(8,128)}, /*index=5*/f32[16,32]{1,0:T(8,128)}) custom-call(bf16[184,128]{1,0:T(8,128)(2,1)S(1)} %get-tuple-element.22.r0_ref, bf16[184,128]{1,0:T(8,128)(2,1)S(1)} %collective-permute-done.1.r1_ref, ...), custom_call_target="tpu_custom_call" | custom-call | tf_op jit(solution)/shard_map/finish/pallas_call | solution.py:468
Async XLA Ops:
  23.9 1.8 %collective-permute-start = (bf16[8,224,128]{2,1,0:T(8,128)(2,1)S(1)}, bf16[8,224,128]{2,1,0:T(8,128)(2,1)S(1)}, u32[]{:S(2)}, u32[]{:S(2)}) collective-permute-start(bf16[8,224,128]{2,1,0:T(8,128)(2,1)S(1)} %all_to_all.5.mine_ref), channel_id=1, source_target_pairs={{0,1},{1,0},{2,3},{3,2},{4,5},{5,4},{6,7},{7,6},{8,9},{9,8},{10,11... | collective-permute-start | bytes 1376264 | tf_op jit(solution)/shard_map/ppermute | solution.py:453
  23.9 0.7 %copy-start = (s32[16]{0:T(128)S(1)}, s32[16]{0:T(128)}, u32[]{:S(2)}) copy-start(s32[16]{0:T(128)} %param.20) | copy-start | bytes 196
  23.9 0.7 %copy-start.1 = (f32[16]{0:T(128)S(1)}, f32[16]{0:T(128)}, u32[]{:S(2)}) copy-start(f32[16]{0:T(128)} %param.21) | copy-start | bytes 196
  23.9 0.7 %copy-start.2 = (f32[16]{0:T(128)S(1)}, f32[16]{0:T(128)}, u32[]{:S(2)}) copy-start(f32[16]{0:T(128)} %param.22) | copy-start | bytes 196
  31.3 4.1 %collective-permute-start.1 = (bf16[184,128]{1,0:T(8,128)(2,1)S(1)}, bf16[184,128]{1,0:T(8,128)(2,1)S(1)}, u32[]{:S(2)}, u32[]{:S(2)}) collective-permute-start(bf16[184,128]{1,0:T(8,128)(2,1)S(1)} %get-tuple-element.23), channel_id=1, source_target_pairs={{0,2},{1,3},{2,0},{3,1},{4,6},{5,7},{6,4},{7,5},{8,10},{9,11},{10,... | collective-permute-start | bytes 141320 | tf_op jit(solution)/shard_map/ppermute | solution.py:465
  32.7 4.4 %collective-permute-start.2 = (bf16[184,128]{1,0:T(8,128)(2,1)S(1)}, bf16[184,128]{1,0:T(8,128)(2,1)S(1)}, u32[]{:S(2)}, u32[]{:S(2)}) collective-permute-start(bf16[184,128]{1,0:T(8,128)(2,1)S(1)} %get-tuple-element.24), channel_id=1, source_target_pairs={{0,4},{1,5},{2,6},{3,7},{4,0},{5,1},{6,2},{7,3},{8,12},{9,13},{10,... | collective-permute-start | bytes 141320 | tf_op jit(solution)/shard_map/ppermute | solution.py:465
  32.7 5.0 %collective-permute-start.3 = (bf16[184,128]{1,0:T(8,128)(2,1)S(1)}, bf16[184,128]{1,0:T(8,128)(2,1)S(1)}, u32[]{:S(2)}, u32[]{:S(2)}) collective-permute-start(bf16[184,128]{1,0:T(8,128)(2,1)S(1)} %get-tuple-element.25), channel_id=1, source_target_pairs={{0,6},{1,7},{2,4},{3,5},{4,2},{5,3},{6,0},{7,1},{8,14},{9,15},{10,... | collective-permute-start | bytes 141320 | tf_op jit(solution)/shard_map/ppermute | solution.py:465

commit v5 on v4

--- a/solution.py
+++ b/solution.py
@@ -144,6 +144,7 @@
 PIECE = 32
 HEAD = 4 * PIECE
 TAIL = HEAD + 16
+FRONT = TAIL + 8
 
 
 def call(kernel, name, outs, n_in, scratch=(), space=pltpu.VMEM):
@@ -185,35 +186,27 @@
 
 
 def pack_kernel(
-    p_hbm, d_hbm, w_hbm, u_hbm, m_hbm, n_hbm, one_hbm, two_hbm, three_hbm, pa_hbm, wa_hbm, out_ref,
-    p_ref, d_ref, w_ref, u_ref, m_ref, n_ref, one_ref, two_ref, three_ref, pa_ref, wa_ref, part_ref, f_ref, sems,
+    d_hbm, w_hbm, one_hbm, two_hbm, three_hbm, pa_hbm, wa_hbm, out_ref,
+    d_ref, w_ref, one_ref, two_ref, three_ref, pa_ref, wa_ref, part_ref, f_ref, sems,
 ):
     pairs = (
-        (n_hbm, n_ref), (u_hbm, u_ref), (m_hbm, m_ref), (p_hbm, p_ref), (d_hbm, d_ref), (w_hbm, w_ref),
-        (pa_hbm, pa_ref), (wa_hbm, wa_ref), (one_hbm, one_ref), (two_hbm, two_ref), (three_hbm, three_ref),
+        (d_hbm, d_ref), (w_hbm, w_ref), (one_hbm, one_ref), (two_hbm, two_ref), (three_hbm, three_ref),
+        (pa_hbm, pa_ref), (wa_hbm, wa_ref),
     )
     copies = [pltpu.make_async_copy(source, target, sems.at[i]) for i, (source, target) in enumerate(pairs)]
     for copy in copies:
         copy.start()
     f32, bf16 = jnp.float32, jnp.bfloat16
     chips = out_ref.shape[0]
-    piece = f_ref.shape[0] // SUB
-    blocks = p_ref.shape[0] // SUB
+    half = d_ref.shape[0] // SUB
+    piece = 4 * half
+    lanes = lax.broadcasted_iota(jnp.int32, (PIECE, LANE), 1)
+    spread = (lanes % PIECE == lax.broadcasted_iota(jnp.int32, (PIECE, LANE), 0)).astype(f32).astype(bf16)
     for copy in copies:
         copy.wait()
-
-    def put(f, j, tile):
-        f_ref[pl.ds(blocks * f + j, SUB, stride=piece), :] = tile
-
-    for j in range(blocks):
-        rows = slice(SUB * j, SUB * j + SUB)
-        along = difference(u_ref.at[0], n_ref[rows, 0, :], n_ref[rows, 1, :])
-        across = difference(u_ref.at[1], n_ref[rows, 2, :], n_ref[rows, 3, :])
-        diverg = m_ref[rows, 0, :] * along + m_ref[rows, 1, :] * across
-        for f, tile in enumerate((p_ref[rows, :] - diverg, d_ref[rows, :], w_ref[rows, :], diverg, pa_ref[rows, :], wa_ref[rows, :])):
-            put(f, j, tile)
-    lanes = lax.broadcasted_iota(jnp.int32, (PIECE, LANE), 1)
-    spread = (lanes % PIECE == lax.broadcasted_iota(jnp.int32, (PIECE, LANE), 0)).astype(f32).astype(bf16)
+    for f, field_ref in enumerate((d_ref, w_ref, pa_ref, wa_ref)):
+        for j in range(half):
+            f_ref[pl.ds(half * f + j, SUB, stride=piece), :] = field_ref[SUB * j : SUB * j + SUB, :]
     part_ref[...] = jnp.dot(three_ref[...], spread, preferred_element_type=f32)
     lanes = lax.broadcasted_iota(jnp.int32, (4, LANE), 1)
     three = jnp.zeros((4, LANE), f32)
@@ -223,17 +216,42 @@
     for q in range(4):
         part_ref[4 * q : 4 * q + 4, :] = one[:, LANE * q : LANE * (q + 1)]
     one = part_ref[...].astype(bf16)
-    for c in range(chips):
-        for q in range(4):
-            out_ref[c, PIECE * q : PIECE * (q + 1), :] = two_ref[:, LANE * q : LANE * (q + 1)]
-        out_ref[c, HEAD:TAIL, :] = one
-        f_ref[piece * c + 6 * blocks : piece * c + 6 * blocks + 4, :] = three
-        if piece > 6 * blocks + 4:
-            f_ref[piece * c + 6 * blocks + 4 : piece * (c + 1), :] = jnp.zeros((piece - 6 * blocks - 4, LANE), f32)
+    part_ref[0:4, :] = three
+    part_ref[4:8, :] = jnp.zeros((4, LANE), f32)
+    three = part_ref[0:8, :].astype(bf16)
     for g in range(GROUPS):
         both = jnp.concatenate([f_ref[piece * c : piece * (c + 1), :] for c in (g, g + GROUPS)], axis=0).astype(bf16)
         for c in range(g, chips, GROUPS):
-            out_ref[c, TAIL:, :] = both
+            for q in range(4):
+                out_ref[c, PIECE * q : PIECE * (q + 1), :] = two_ref[:, LANE * q : LANE * (q + 1)]
+            out_ref[c, HEAD:TAIL, :] = one
+            out_ref[c, TAIL:FRONT, :] = three
+            out_ref[c, FRONT:, :] = both
+
+
+def star_kernel(p_ref, u_ref, m_ref, n_ref, out0_ref, out1_ref, out2_ref, out3_ref, f_ref):
+    half = p_ref.shape[0] // SUB
+    size = out0_ref.shape[0]
+    for j in range(half):
+        rows = slice(SUB * j, SUB * j + SUB)
+        along = difference(u_ref.at[0], n_ref[rows, 0, :], n_ref[rows, 1, :])
+        across = difference(u_ref.at[1], n_ref[rows, 2, :], n_ref[rows, 3, :])
+        diverg = m_ref[rows, 0, :] * along + m_ref[rows, 1, :] * across
+        for f, tile in enumerate((p_ref[rows, :] - diverg, diverg)):
+            for b in range(2):
+                place = pl.ds(2 * half * b + half * f + j, GROUPS, stride=size)
+                f_ref[place, :] = tile[GROUPS * b : GROUPS * (b + 1), :]
+    group = lax.axis_index("slab") // 2 % GROUPS
+    for k, out_ref in enumerate((out0_ref, out1_ref, out2_ref, out3_ref)):
+        out_ref[...] = f_ref[pl.ds(pl.multiple_of(size * (group ^ k), SUB), size), :].astype(jnp.bfloat16)
+
+
+def join_kernel(r0_ref, r1_ref, r2_ref, r3_ref, out_ref, f_ref):
+    size = r0_ref.shape[0]
+    group = lax.axis_index("slab") // 2 % GROUPS
+    for k, ref in enumerate((r0_ref, r1_ref, r2_ref, r3_ref)):
+        f_ref[pl.ds(pl.multiple_of(size * (group ^ k), SUB), size), :] = ref[...].astype(jnp.float32)
+    out_ref[...] = f_ref[...].astype(jnp.bfloat16)
 
 
 def shifted_up(field, rows):
@@ -274,8 +292,8 @@
 
 
 def column_kernel(
-    mine_ref, other_ref, place_ref, inverse_ref, column_ref, out0_ref, out1_ref, out2_ref, out3_ref,
-    a_ref, one_ref, w2_ref, w3_ref, act_ref, sel_ref, g_ref, h_ref, y_ref, t_ref,
+    mine_ref, other_ref, near_ref, far_ref, near_other_ref, far_other_ref, place_ref, inverse_ref, column_ref,
+    out0_ref, out1_ref, out2_ref, out3_ref, x_ref, a_ref, one_ref, w2_ref, w3_ref, act_ref, sel_ref, g_ref, h_ref, y_ref, t_ref, act2_ref, sel2_ref,
 ):
     f32, bf16 = jnp.float32, jnp.bfloat16
     device = lax.axis_index("slab")
@@ -286,8 +304,8 @@
     width = act_ref.shape[1]
     blocks = width // LANE
     stride = mine_ref.shape[1] - HEAD
-    piece = (stride - 16) // 2
     half = blocks // 2
+    upper_half = device // SUB
     for ref, which in ((mine_ref, core), (other_ref, 1 - core)):
         for c in range(chips):
             for q in range(4):
@@ -301,7 +319,7 @@
     one = jnp.concatenate([one_ref[4 * devices * q : 4 * devices * (q + 1), :] for q in range(4)], axis=1)
     lanes = lax.broadcasted_iota(jnp.int32, (4, LANE), 1)
     for t in range(devices // 4):
-        packed = [a_ref[pl.ds(stride * (4 * t + s) + 16 + 6 * half, 4), :] for s in range(4)]
+        packed = [a_ref[stride * (4 * t + s) + 16 : stride * (4 * t + s) + 20, :] for s in range(4)]
         for q in range(4):
             tile = jnp.zeros((4, LANE), f32)
             for s in range(4):
@@ -314,8 +332,23 @@
     w3t = w3_ref[...].astype(bf16)
     w3 = w3_ref[...].T.astype(bf16)
     place, inverse = place_ref[...], inverse_ref[...]
-    order = [16 + piece * b + half * f + j for f in range(6) for b in range(2) for j in range(half)]
-    raw = jnp.concatenate([a_ref[pl.ds(k, levels, stride=stride), :] for k in order], axis=1)
+    size = near_ref.shape[0] // GROUPS
+    for ref, side, which in (
+        (near_ref, upper_half, core), (far_ref, 1 - upper_half, core),
+        (near_other_ref, upper_half, 1 - core), (far_other_ref, 1 - upper_half, 1 - core),
+    ):
+        for g in range(GROUPS):
+            start = pl.multiple_of(size * (SUB * side + 2 * g + which), SUB)
+            x_ref[pl.ds(start, size), :] = ref[size * g : size * (g + 1), :].astype(f32)
+
+    def late(f):
+        return [x_ref[pl.ds(2 * half * b + half * f + j, levels, stride=size), :] for b in range(2) for j in range(half)]
+
+    def early(f):
+        start = 24 + half * f
+        return [a_ref[pl.ds(start + 4 * half * b + j, levels, stride=stride), :] for b in range(2) for j in range(half)]
+
+    raw = jnp.concatenate(late(0) + early(0) + early(1) + late(1) + early(2) + early(3), axis=1)
     ordered = jnp.dot(place, raw.astype(bf16), preferred_element_type=f32)
     star, density, vertical, diverg, pressure_adjoint, wind_adjoint = (
         ordered[:, width * i : width * (i + 1)] for i in range(6)
@@ -341,6 +374,7 @@
     heat_grad = rhs_grad.astype(bf16)
     tanh_two = jnp.tanh(contract_first(w2, act_one))
     act_two = tanh_two.astype(bf16)
+    act2_ref[...] = act_two
     back_two = jnp.dot(w3, heat_grad, preferred_element_type=f32)
     pre_two_grad = (back_two * (1.0 - tanh_two * tanh_two)).astype(bf16)
     back_one = jnp.dot(w2, pre_two_grad, preferred_element_type=f32)
@@ -352,9 +386,11 @@
     outs = (out0_ref, out1_ref, out2_ref, out3_ref)
     targets = [device ^ (2 * k) for k in range(GROUPS)]
     for k, target in enumerate(targets):
-        sel_ref[PIECE * k : PIECE * (k + 1), :] = act_ref[pl.ds(pl.multiple_of(PIECE * target, PIECE), PIECE), :]
+        hid = pl.ds(pl.multiple_of(PIECE * target, PIECE), PIECE)
+        sel_ref[PIECE * k : PIECE * (k + 1), :] = act_ref[hid, :]
+        sel2_ref[PIECE * k : PIECE * (k + 1), :] = act2_ref[hid, :]
     local_two = contract_last(sel_ref[...], pre_two_grad)
-    local_three = contract_last(heat_grad, act_two)
+    local_three = contract_last(heat_grad, sel2_ref[...])
     g_ref[...] = contract_last(column_input, pre_one_grad)
     fields = jnp.concatenate([press_next, wind_next, star_grad], axis=1).astype(bf16)
     stored = lax.dot_general(place, fields, (((0,), (0,)), ((), ())), preferred_element_type=f32)
@@ -363,13 +399,11 @@
         y_ref[pl.ds(4 + k, devices, stride=back), :] = stored[:, LANE * k : LANE * (k + 1)]
     for k in range(4 + 3 * blocks, back):
         y_ref[pl.ds(k, devices, stride=back), :] = jnp.zeros((devices, LANE), f32)
-    for t in range(devices // 4):
-        t_ref[16 * t : 16 * t + 16, :] = local_three[:, LANE * t : LANE * (t + 1)]
+    t_ref[...] = local_three
     for k, (target, out_ref) in enumerate(zip(targets, outs)):
         pair = g_ref[pl.ds(pl.multiple_of(SUB * (target // 2), SUB), SUB), :]
         one = jnp.where(core == 0, pair[:4, :], pair[4:, :])
-        tile = t_ref[pl.ds(pl.multiple_of(16 * (target // 4), 16), 16), :]
-        tile = pltpu.roll(tile, (LANE - PIECE * (target % 4)) % LANE, 1)
+        tile = t_ref[...] if k == 0 else pltpu.roll(t_ref[...], LANE - PIECE * k, 1)
         three = tile[:4, :]
         for q in range(4):
             cols = slice(LANE * q, LANE * (q + 1))
@@ -435,35 +469,47 @@
     def exchange(blocks_of_chips):
         return lax.all_to_all(blocks_of_chips, "slab", split_axis=0, concat_axis=0, tiled=True, axis_index_groups=same_core)
 
+    def swap(array, bits):
+        return lax.ppermute(array, "slab", [(i, i ^ bits) for i in range(devices)])
+
+    def among_groups(outgoing):
+        return [outgoing[0]] + [swap(outgoing[k], 2 * k) for k in range(1, GROUPS)]
+
     sources = (
-        view(pressure), view(density), view(vertical_wind), horizontal_wind.reshape(2, rows, LANE), lanes(metric_terms),
-        lanes(neighbors), weight_one, weight_two, weight_three.T, view(pressure_adjoint), view(wind_adjoint),
-    )
-    piece, back = pad(4 + 3 * blocks), pad(4 + 3 * blocks)
+        view(density), view(vertical_wind), weight_one, weight_two, weight_three.T, view(pressure_adjoint), view(wind_adjoint),
+    )
+    half = rows // SUB
+    back = pad(4 + 3 * blocks)
     send = call(
-        pack_kernel, "pack", shape((chips, TAIL + 2 * piece, LANE), bf16), len(sources),
+        pack_kernel, "pack", shape((chips, FRONT + 8 * half, LANE), bf16), len(sources),
         [pltpu.VMEM(source.shape, source.dtype) for source in sources]
-        + [pltpu.VMEM((16, LANE), f32), pltpu.VMEM((SUB * piece, LANE), f32), pltpu.SemaphoreType.DMA((len(sources),))],
+        + [pltpu.VMEM((16, LANE), f32), pltpu.VMEM((SUB * 4 * half, LANE), f32), pltpu.SemaphoreType.DMA((len(sources),))],
         pltpu.HBM,
     )(*(pltpu.with_memory_space_constraint(source, pltpu.HBM) for source in sources))
+    star_block, join_scratch = shape((4 * half, LANE), bf16), pltpu.VMEM((GROUPS * 4 * half, LANE), f32)
+    star_send = call(star_kernel, "star", (star_block,) * GROUPS, 4, [join_scratch])(
+        view(pressure), horizontal_wind.reshape(2, rows, LANE), lanes(metric_terms), lanes(neighbors)
+    )
+    mine = exchange(send)
+    near = call(join_kernel, "join", shape((GROUPS * 4 * half, LANE), bf16), GROUPS, [join_scratch])(*among_groups(star_send))
+    far = swap(near, SUB)
+    mine, far = lax.optimization_barrier((mine, far))
+    other, near_other, far_other = swap(mine, 1), swap(near, 1), swap(far, 1)
     operators = call(
         operator_kernel, "operators", (shape((levels, levels), bf16), shape((levels, levels), f32), shape((levels, LANE), f32)), 3
     )(level_order.reshape(1, levels), stiffness.reshape(1, levels), coupling.reshape(1, levels))
-    mine = exchange(send)
-    other = lax.ppermute(mine, "slab", [(i, i ^ 1) for i in range(devices)])
     block = shape((TAIL + back, LANE), bf16)
     send_back = call(
-        column_kernel, "column_step", (block,) * GROUPS, 5,
+        column_kernel, "column_step", (block,) * GROUPS, 9,
         [
-            pltpu.VMEM((devices * (16 + 2 * piece), LANE), f32), pltpu.VMEM((16 * devices, LANE), f32),
+            pltpu.VMEM((devices * 4 * half, LANE), f32), pltpu.VMEM((devices * (FRONT - HEAD + 8 * half), LANE), f32), pltpu.VMEM((16 * devices, LANE), f32),
             pltpu.VMEM((hidden, hidden), bf16), pltpu.VMEM((levels, hidden), f32), pltpu.VMEM((hidden, width), bf16),
             pltpu.VMEM((GROUPS * PIECE, width), bf16), pltpu.VMEM((4 * levels, hidden), f32), pltpu.VMEM((16, LANE), f32),
-            pltpu.VMEM((devices * back, LANE), f32), pltpu.VMEM((4 * devices, LANE), f32),
+            pltpu.VMEM((devices * back, LANE), f32), pltpu.VMEM((levels, LANE), f32),
+            pltpu.VMEM((hidden, width), bf16), pltpu.VMEM((GROUPS * PIECE, width), bf16),
         ],
-    )(mine, other, *operators)
-    received = [send_back[0]] + [
-        lax.ppermute(send_back[k], "slab", [(i, i ^ (2 * k)) for i in range(devices)]) for k in range(1, GROUPS)
-    ]
+    )(mine, other, near, far, near_other, far_other, *operators)
+    received = among_groups(send_back)
     field_out = shape((rows, LANE), f32)
     new_pressure, new_wind, grad, first_grad, second_grad, third_grad = call(
         functools.partial(finish_kernel, 1.0 / math.sqrt(columns)), "finish",

time: 38.6 us -> 38.8 us (level)
  blocking collectives: 20.3 us -> 0 us
  starting transfers between devices: 3.55 us -> 17.6 us
  waiting for transfers between devices: 3.86 us -> 10 us
    all_to_all x1 -> x0, blocking collectives: 20.3 us -> none  [exchange(): lax.all_to_all(blocks_of_chips, 'slab', split_axis=0, concat_axis=0, tile...]
    all_to_all x0 -> x1, starting transfers between devices: none -> 7.4 us  [exchange(): lax.all_to_all(blocks_of_chips, 'slab', split_axis=0, concat_axis=0, tile...]
    ppermute x4 -> x10, starting transfers between devices: 3.55 us -> 10.2 us  [swap(): return lax.ppermute(array, 'slab', [(i, i ^ bits) for i in range(devices)])]
    ppermute x4 -> x10, waiting for transfers between devices: 3.86 us -> 10 us  [swap(): return lax.ppermute(array, 'slab', [(i, i ^ bits) for i in range(devices)])]
    pallas_call x2 -> x4, Pallas kernels: 8.54 us -> 8.62 us  [the longest x1 4.88 us: fast_body(): call(column_kernel, 'column_step', (block,) * GROUPS, 9, [pltpu.VMEM((dev...]
  transfers between devices with their start and end apart: 4 -> 11, of which waited for: 4 -> 8; matrix products, arithmetic and copies ran while one was open for 0% -> 0% of each run, Pallas kernels for 0% -> 5%
where the time goes in v5:
time: 38.8 us; the launch traced here: 38.5 us
  starting transfers between devices  17.6 us (45%)
  waiting for transfers between devices  10 us (26%)
  Pallas kernels  9.44 us (24%)
  between operations  0.73 us (2%)
  local copies, waits for them, and re-layouts  0.7 us (2%)
    ppermute x10, starting transfers between devices, swap(): return lax.ppermute(array, 'slab', [(i, i ^ bits) for i in range(devices)])  10.2 us
    ppermute x10, waiting for transfers between devices, swap(): return lax.ppermute(array, 'slab', [(i, i ^ bits) for i in range(devices)])  10 us
    all_to_all x1, starting transfers between devices, exchange(): lax.all_to_all(blocks_of_chips, 'slab', split_axis=0, concat_axis=0, tile...  7.4 us
    pallas_call x1, Pallas kernels, fast_body(): call(column_kernel, 'column_step', (block,) * GROUPS, 9, [pltpu.VMEM((dev...  4.88 us
    pallas_call x1, Pallas kernels, fast_body(): call(star_kernel, 'star', (star_block,) * GROUPS, 4, [join_scratch])  1.94 us
    pallas_call x1, Pallas kernels, fast_body(): call(pack_kernel, 'pack', shape((chips, FRONT + 8 * half, LANE), bf16), l...  1.79 us
  transfers between devices with their start and end apart: 11, of which 8 were waited for; matrix products, arithmetic and copies ran while one was open for 0% of the time, Pallas kernels for 5%

profile of v5, /device:TPU:0, one launch (start us, length us, event | category | flops | bytes accessed | tf_op | source)
XLA Modules:
  0.0 38.5 jit_solution(5936956516261510063)
XLA Ops:
  0.6 1.8 %pack.1 = bf16[8,200,128]{2,1,0:T(8,128)(2,1)} custom-call(f32[48,128]{1,0:T(8,128)} %bitcast.27, f32[48,128]{1,0:T(8,128)} %bitcast.28, bf16[4,512]{1,0:T(4,128)(2,1)} %one_hbm.1, bf16[32,512]{1,0:T(8,128)(2,1)} %two_hbm.1, bf16[16,32]{1,0:T(8,128)(2,1)} %bitcast.31, f32[48,128]{1,0:T(8,128)} %bitcast.29, f32[48,128]{1,0:T(8,128)} %bitcast.30), custom_call_target="tpu_custom_call" | custom-call | tf_op jit(solution)/shard_map/pack/pallas_call | solution.py:483
  2.4 0.0 copy-start
  2.4 0.0 copy-start.1
  2.5 0.0 copy-start.2
  2.5 0.0 copy-start.3
  2.5 7.4 %all-to-all-start = ((bf16[8,200,128]{2,1,0:T(8,128)(2,1)}), bf16[8,200,128]{2,1,0:T(8,128)(2,1)S(1)}, u32[]{:S(2)}, u32[]{:S(2)}) async-start(bf16[8,200,128]{2,1,0:T(8,128)(2,1)} %pack.1), calls=%async_computation | async-start | bytes 819200 | tf_op jit(solution)/shard_map/all_to_all | solution.py:470
  9.9 1.9 %star.1 = (bf16[24,128]{1,0:T(8,128)(2,1)S(1)}, bf16[24,128]{1,0:T(8,128)(2,1)S(1)}, bf16[24,128]{1,0:T(8,128)(2,1)S(1)}, bf16[24,128]{1,0:T(8,128)(2,1)S(1)}) custom-call(f32[48,128]{1,0:T(8,128)S(1)} %bitcast.23, f32[2,48,128]{2,1,0:T(8,128)S(1)} %bitcast.21, f32[48,2,128]{2,1,0:T(2,128)S(1)} %bitcast.22, s32[48,4,128]{2,1,0:T(4,128)S(1)} %bitcast.20), custom_call_target="tpu_custom_call" | custom-call | tf_op jit(solution)/shard_map/star/pallas_call | solution.py:490
  11.8 2.1 %collective-permute-start = (bf16[24,128]{1,0:T(8,128)(2,1)S(1)}, bf16[24,128]{1,0:T(8,128)(2,1)S(1)}, u32[]{:S(2)}, u32[]{:S(2)}) collective-permute-start(bf16[24,128]{1,0:T(8,128)(2,1)S(1)} %get-tuple-element.26), channel_id=1, source_target_pairs={{0,2},{1,3},{2,0},{3,1},{4,6},{5,7},{6,4},{7,5},{8,10},{9,11},{10,... | collective-permute-start | bytes 18440 | tf_op jit(solution)/shard_map/ppermute | solution.py:473
  13.9 1.5 %collective-permute-start.1 = (bf16[24,128]{1,0:T(8,128)(2,1)S(1)}, bf16[24,128]{1,0:T(8,128)(2,1)S(1)}, u32[]{:S(2)}, u32[]{:S(2)}) collective-permute-start(bf16[24,128]{1,0:T(8,128)(2,1)S(1)} %get-tuple-element.27), channel_id=1, source_target_pairs={{0,4},{1,5},{2,6},{3,7},{4,0},{5,1},{6,2},{7,3},{8,12},{9,13},{10,... | collective-permute-start | bytes 18440 | tf_op jit(solution)/shard_map/ppermute | solution.py:473
  15.4 0.1 collective-permute-start.2
  15.5 0.7 %collective-permute-done.r1_ref = bf16[24,128]{1,0:T(8,128)(2,1)S(1)} collective-permute-done((bf16[24,128]{1,0:T(8,128)(2,1)S(1)}, bf16[24,128]{1,0:T(8,128)(2,1)S(1)}, u32[]{:S(2)}, u32[]{:S(2)}) %collective-permute-start) | collective-permute-done | bytes 6176 | tf_op jit(solution)/shard_map/ppermute | solution.py:473
  16.1 1.5 %collective-permute-done.1.r2_ref = bf16[24,128]{1,0:T(8,128)(2,1)S(1)} collective-permute-done((bf16[24,128]{1,0:T(8,128)(2,1)S(1)}, bf16[24,128]{1,0:T(8,128)(2,1)S(1)}, u32[]{:S(2)}, u32[]{:S(2)}) %collective-permute-start.1) | collective-permute-done | bytes 6176 | tf_op jit(solution)/shard_map/ppermute | solution.py:473
  17.6 2.3 %collective-permute-done.2.r3_ref = bf16[24,128]{1,0:T(8,128)(2,1)S(1)} collective-permute-done((bf16[24,128]{1,0:T(8,128)(2,1)S(1)}, bf16[24,128]{1,0:T(8,128)(2,1)S(1)}, u32[]{:S(2)}, u32[]{:S(2)}) %collective-permute-start.2) | collective-permute-done | bytes 6176 | tf_op jit(solution)/shard_map/ppermute | solution.py:473
  20.0 2.5 %collective-permute-start.3 = (bf16[96,128]{1,0:T(8,128)(2,1)S(1)}, bf16[96,128]{1,0:T(8,128)(2,1)S(1)}, u32[]{:S(2)}, u32[]{:S(2)}) collective-permute-start(bf16[96,128]{1,0:T(8,128)(2,1)S(1)} %join.1.near_ref), channel_id=1, source_target_pairs={{0,8},{1,9},{2,10},{3,11},{4,12},{5,13},{6,14},{7,15},{8,0},{9,1},... | collective-permute-start | bytes 73736 | tf_op jit(solution)/shard_map/ppermute | solution.py:473
  22.5 2.5 %collective-permute-done.3.far_ref = bf16[96,128]{1,0:T(8,128)(2,1)S(1)} collective-permute-done((bf16[96,128]{1,0:T(8,128)(2,1)S(1)}, bf16[96,128]{1,0:T(8,128)(2,1)S(1)}, u32[]{:S(2)}, u32[]{:S(2)}) %collective-permute-start.3) | collective-permute-done | bytes 24608 | tf_op jit(solution)/shard_map/ppermute | solution.py:473
  25.0 0.0 all-to-all-done.mine_ref
  25.0 0.5 %collective-permute-start.5 = (bf16[96,128]{1,0:T(8,128)(2,1)S(1)}, bf16[96,128]{1,0:T(8,128)(2,1)S(1)}, u32[]{:S(2)}, u32[]{:S(2)}) collective-permute-start(bf16[96,128]{1,0:T(8,128)(2,1)S(1)} %join.1.near_ref), channel_id=1, source_target_pairs={{0,1},{1,0},{2,3},{3,2},{4,5},{5,4},{6,7},{7,6},{8,9},{9,8},{10,11... | collective-permute-start | bytes 73736 | tf_op jit(solution)/shard_map/ppermute | solution.py:473
  25.5 0.0 collective-permute-start.6
  25.5 0.6 %copy-done.4 = s32[16]{0:T(128)S(1)} copy-done((s32[16]{0:T(128)S(1)}, s32[16]{0:T(128)}, u32[]{:S(2)}) %copy-start.4) | copy-done | bytes 88
  26.2 0.0 copy-done.5
  26.2 0.0 copy-done.6
  26.2 0.1 operators.1
  26.3 0.4 %collective-permute-done.5.near_other_ref = bf16[96,128]{1,0:T(8,128)(2,1)S(1)} collective-permute-done((bf16[96,128]{1,0:T(8,128)(2,1)S(1)}, bf16[96,128]{1,0:T(8,128)(2,1)S(1)}, u32[]{:S(2)}, u32[]{:S(2)}) %collective-permute-start.5) | collective-permute-done | bytes 24608 | tf_op jit(solution)/shard_map/ppermute | solution.py:473
  26.8 0.0 collective-permute-done.6.far_other_ref
  26.8 4.9 %column_step.1 = (bf16[184,128]{1,0:T(8,128)(2,1)S(1)}, bf16[184,128]{1,0:T(8,128)(2,1)S(1)}, bf16[184,128]{1,0:T(8,128)(2,1)S(1)}, bf16[184,128]{1,0:T(8,128)(2,1)S(1)}) custom-call(bf16[8,200,128]{2,1,0:T(8,128)(2,1)S(1)} %all-to-all-done.mine_ref, bf16[8,200,128]{2,1,0:T(8,128)(2,1)S(1)} %collective-permute-done.4.other_ref, ...), custom_call_target="tpu_custom_call" | custom-call | tf_op jit(solution)/shard_map/column_step/pallas_call | solution.py:502
  31.7 0.6 %collective-permute-start.7 = (bf16[184,128]{1,0:T(8,128)(2,1)S(1)}, bf16[184,128]{1,0:T(8,128)(2,1)S(1)}, u32[]{:S(2)}, u32[]{:S(2)}) collective-permute-start(bf16[184,128]{1,0:T(8,128)(2,1)S(1)} %get-tuple-element.35), channel_id=1, source_target_pairs={{0,2},{1,3},{2,0},{3,1},{4,6},{5,7},{6,4},{7,5},{8,10},{9,11},{10,... | collective-permute-start | bytes 141320 | tf_op jit(solution)/shard_map/ppermute | solution.py:473
  32.3 0.3 collective-permute-start.8
  32.6 2.6 %collective-permute-start.9 = (bf16[184,128]{1,0:T(8,128)(2,1)S(1)}, bf16[184,128]{1,0:T(8,128)(2,1)S(1)}, u32[]{:S(2)}, u32[]{:S(2)}) collective-permute-start(bf16[184,128]{1,0:T(8,128)(2,1)S(1)} %get-tuple-element.37), channel_id=1, source_target_pairs={{0,6},{1,7},{2,4},{3,5},{4,2},{5,3},{6,0},{7,1},{8,14},{9,15},{10,... | collective-permute-start | bytes 141320 | tf_op jit(solution)/shard_map/ppermute | solution.py:473
  35.3 0.6 %collective-permute-done.7.r1_ref = bf16[184,128]{1,0:T(8,128)(2,1)S(1)} collective-permute-done((bf16[184,128]{1,0:T(8,128)(2,1)S(1)}, bf16[184,128]{1,0:T(8,128)(2,1)S(1)}, u32[]{:S(2)}, u32[]{:S(2)}) %collective-permute-start.7) | collective-permute-done | bytes 47136 | tf_op jit(solution)/shard_map/ppermute | solution.py:473
  35.8 1.0 %collective-permute-done.8.r2_ref = bf16[184,128]{1,0:T(8,128)(2,1)S(1)} collective-permute-done((bf16[184,128]{1,0:T(8,128)(2,1)S(1)}, bf16[184,128]{1,0:T(8,128)(2,1)S(1)}, u32[]{:S(2)}, u32[]{:S(2)}) %collective-permute-start.8) | collective-permute-done | bytes 47136 | tf_op jit(solution)/shard_map/ppermute | solution.py:473
  36.9 1.0 %collective-permute-done.9.r3_ref = bf16[184,128]{1,0:T(8,128)(2,1)S(1)} collective-permute-done((bf16[184,128]{1,0:T(8,128)(2,1)S(1)}, bf16[184,128]{1,0:T(8,128)(2,1)S(1)}, u32[]{:S(2)}, u32[]{:S(2)}) %collective-permute-start.9) | collective-permute-done | bytes 47136 | tf_op jit(solution)/shard_map/ppermute | solution.py:473
  37.8 0.7 %finish.1 = (f32[48,128]{1,0:T(8,128)}, f32[48,128]{1,0:T(8,128)}, f32[48,128]{1,0:T(8,128)}, f32[4,512]{1,0:T(4,128)}, f32[32,512]{1,0:T(8,128)}, /*index=5*/f32[16,32]{1,0:T(8,128)}) custom-call(bf16[184,128]{1,0:T(8,128)(2,1)S(1)} %get-tuple-element.34.r0_ref, bf16[184,128]{1,0:T(8,128)(2,1)S(1)} %collective-permute-done.7.r1_ref, ...), custom_call_target="tpu_custom_call" | custom-call | tf_op jit(solution)/shard_map/finish/pallas_call | solution.py:514
  (10 shorter events, 0.0 us)
Async XLA Ops:
  2.4 7.4 %copy-start = (s32[4,6144]{1,0:T(4,128)S(1)}, s32[4,6144]{1,0:T(4,128)}, u32[]{:S(2)}) copy-start(s32[4,6144]{1,0:T(4,128)} %param.19) | copy-start | bytes 294916
  2.4 7.4 %copy-start.1 = (f32[2,1,6144]{2,1,0:T(1,128)S(1)}, f32[2,1,6144]{2,1,0:T(1,128)}, u32[]{:S(2)}) copy-start(f32[2,1,6144]{2,1,0:T(1,128)} %param.17) | copy-start | bytes 147460
  2.5 7.4 %copy-start.2 = (f32[2,6144]{1,0:T(2,128)S(1)}, f32[2,6144]{1,0:T(2,128)}, u32[]{:S(2)}) copy-start(f32[2,6144]{1,0:T(2,128)} %param.18) | copy-start | bytes 147460
  2.5 7.4 %copy-start.3 = (f32[1,6144]{1,0:T(1,128)S(1)}, f32[1,6144]{1,0:T(1,128)}, u32[]{:S(2)}) copy-start(f32[1,6144]{1,0:T(1,128)} %param.14) | copy-start | bytes 73732
  2.5 22.5 %all-to-all-start = ((bf16[8,200,128]{2,1,0:T(8,128)(2,1)}), bf16[8,200,128]{2,1,0:T(8,128)(2,1)S(1)}, u32[]{:S(2)}, u32[]{:S(2)}) async-start(bf16[8,200,128]{2,1,0:T(8,128)(2,1)} %pack.1), calls=%async_computation | async-start | bytes 819200 | tf_op jit(solution)/shard_map/all_to_all | solution.py:470
  11.8 4.3 %collective-permute-start = (bf16[24,128]{1,0:T(8,128)(2,1)S(1)}, bf16[24,128]{1,0:T(8,128)(2,1)S(1)}, u32[]{:S(2)}, u32[]{:S(2)}) collective-permute-start(bf16[24,128]{1,0:T(8,128)(2,1)S(1)} %get-tuple-element.26), channel_id=1, source_target_pairs={{0,2},{1,3},{2,0},{3,1},{4,6},{5,7},{6,4},{7,5},{8,10},{9,11},{10,... | collective-permute-start | bytes 18440 | tf_op jit(solution)/shard_map/ppermute | solution.py:473
  13.9 3.7 %collective-permute-start.1 = (bf16[24,128]{1,0:T(8,128)(2,1)S(1)}, bf16[24,128]{1,0:T(8,128)(2,1)S(1)}, u32[]{:S(2)}, u32[]{:S(2)}) collective-permute-start(bf16[24,128]{1,0:T(8,128)(2,1)S(1)} %get-tuple-element.27), channel_id=1, source_target_pairs={{0,4},{1,5},{2,6},{3,7},{4,0},{5,1},{6,2},{7,3},{8,12},{9,13},{10,... | collective-permute-start | bytes 18440 | tf_op jit(solution)/shard_map/ppermute | solution.py:473
  15.4 4.5 %collective-permute-start.2 = (bf16[24,128]{1,0:T(8,128)(2,1)S(1)}, bf16[24,128]{1,0:T(8,128)(2,1)S(1)}, u32[]{:S(2)}, u32[]{:S(2)}) collective-permute-start(bf16[24,128]{1,0:T(8,128)(2,1)S(1)} %get-tuple-element.28), channel_id=1, source_target_pairs={{0,6},{1,7},{2,4},{3,5},{4,2},{5,3},{6,0},{7,1},{8,14},{9,15},{10,... | collective-permute-start | bytes 18440 | tf_op jit(solution)/shard_map/ppermute | solution.py:473
  20.0 5.1 %collective-permute-start.3 = (bf16[96,128]{1,0:T(8,128)(2,1)S(1)}, bf16[96,128]{1,0:T(8,128)(2,1)S(1)}, u32[]{:S(2)}, u32[]{:S(2)}) collective-permute-start(bf16[96,128]{1,0:T(8,128)(2,1)S(1)} %join.1.near_ref), channel_id=1, source_target_pairs={{0,8},{1,9},{2,10},{3,11},{4,12},{5,13},{6,14},{7,15},{8,0},{9,1},... | collective-permute-start | bytes 73736 | tf_op jit(solution)/shard_map/ppermute | solution.py:473
  25.0 1.8 %collective-permute-start.4 = (bf16[8,200,128]{2,1,0:T(8,128)(2,1)S(1)}, bf16[8,200,128]{2,1,0:T(8,128)(2,1)S(1)}, u32[]{:S(2)}, u32[]{:S(2)}) collective-permute-start(bf16[8,200,128]{2,1,0:T(8,128)(2,1)S(1)} %all-to-all-done.mine_ref), channel_id=1, source_target_pairs={{0,1},{1,0},{2,3},{3,2},{4,5},{5,4},{6,7},{7,6},{8,9},{9,8},{10,11... | collective-permute-start | bytes 1228808 | tf_op jit(solution)/shard_map/ppermute | solution.py:473
  25.0 1.8 %collective-permute-start.5 = (bf16[96,128]{1,0:T(8,128)(2,1)S(1)}, bf16[96,128]{1,0:T(8,128)(2,1)S(1)}, u32[]{:S(2)}, u32[]{:S(2)}) collective-permute-start(bf16[96,128]{1,0:T(8,128)(2,1)S(1)} %join.1.near_ref), channel_id=1, source_target_pairs={{0,1},{1,0},{2,3},{3,2},{4,5},{5,4},{6,7},{7,6},{8,9},{9,8},{10,11... | collective-permute-start | bytes 73736 | tf_op jit(solution)/shard_map/ppermute | solution.py:473
  25.5 1.3 %collective-permute-start.6 = (bf16[96,128]{1,0:T(8,128)(2,1)S(1)}, bf16[96,128]{1,0:T(8,128)(2,1)S(1)}, u32[]{:S(2)}, u32[]{:S(2)}) collective-permute-start(bf16[96,128]{1,0:T(8,128)(2,1)S(1)} %collective-permute-done.3.far_ref), channel_id=1, source_target_pairs={{0,1},{1,0},{2,3},{3,2},{4,5},{5,4},{6,7},{7,6},{8,9},{9,8},{10,11... | collective-permute-start | bytes 73736 | tf_op jit(solution)/shard_map/ppermute | solution.py:473
  25.5 0.7 %copy-start.4 = (s32[16]{0:T(128)S(1)}, s32[16]{0:T(128)}, u32[]{:S(2)}) copy-start(s32[16]{0:T(128)} %param.20) | copy-start | bytes 196
  25.5 0.7 %copy-start.5 = (f32[16]{0:T(128)S(1)}, f32[16]{0:T(128)}, u32[]{:S(2)}) copy-start(f32[16]{0:T(128)} %param.21) | copy-start | bytes 196
  25.5 0.7 %copy-start.6 = (f32[16]{0:T(128)S(1)}, f32[16]{0:T(128)}, u32[]{:S(2)}) copy-start(f32[16]{0:T(128)} %param.22) | copy-start | bytes 196
  31.7 4.1 %collective-permute-start.7 = (bf16[184,128]{1,0:T(8,128)(2,1)S(1)}, bf16[184,128]{1,0:T(8,128)(2,1)S(1)}, u32[]{:S(2)}, u32[]{:S(2)}) collective-permute-start(bf16[184,128]{1,0:T(8,128)(2,1)S(1)} %get-tuple-element.35), channel_id=1, source_target_pairs={{0,2},{1,3},{2,0},{3,1},{4,6},{5,7},{6,4},{7,5},{8,10},{9,11},{10,... | collective-permute-start | bytes 141320 | tf_op jit(solution)/shard_map/ppermute | solution.py:473
  32.3 4.5 %collective-permute-start.8 = (bf16[184,128]{1,0:T(8,128)(2,1)S(1)}, bf16[184,128]{1,0:T(8,128)(2,1)S(1)}, u32[]{:S(2)}, u32[]{:S(2)}) collective-permute-start(bf16[184,128]{1,0:T(8,128)(2,1)S(1)} %get-tuple-element.36), channel_id=1, source_target_pairs={{0,4},{1,5},{2,6},{3,7},{4,0},{5,1},{6,2},{7,3},{8,12},{9,13},{10,... | collective-permute-start | bytes 141320 | tf_op jit(solution)/shard_map/ppermute | solution.py:473
  32.6 5.2 %collective-permute-start.9 = (bf16[184,128]{1,0:T(8,128)(2,1)S(1)}, bf16[184,128]{1,0:T(8,128)(2,1)S(1)}, u32[]{:S(2)}, u32[]{:S(2)}) collective-permute-start(bf16[184,128]{1,0:T(8,128)(2,1)S(1)} %get-tuple-element.37), channel_id=1, source_target_pairs={{0,6},{1,7},{2,4},{3,5},{4,2},{5,3},{6,0},{7,1},{8,14},{9,15},{10,... | collective-permute-start | bytes 141320 | tf_op jit(solution)/shard_map/ppermute | solution.py:473

commit v6 on v4

--- a/solution.py
+++ b/solution.py
@@ -140,6 +140,7 @@
 
 LANE = 128
 SUB = 8
+STRIDE = 104
 GROUPS = 4
 PIECE = 32
 HEAD = 4 * PIECE
@@ -275,7 +276,7 @@
 
 def column_kernel(
     mine_ref, other_ref, place_ref, inverse_ref, column_ref, out0_ref, out1_ref, out2_ref, out3_ref,
-    a_ref, one_ref, w2_ref, w3_ref, act_ref, sel_ref, g_ref, h_ref, y_ref, t_ref,
+    a_ref, one_ref, w2_ref, w3_ref, act_ref, sel_ref, g_ref, h_ref, y_ref, t_ref, act2_ref, sel2_ref,
 ):
     f32, bf16 = jnp.float32, jnp.bfloat16
     device = lax.axis_index("slab")
@@ -285,15 +286,16 @@
     levels = inverse_ref.shape[0]
     width = act_ref.shape[1]
     blocks = width // LANE
-    stride = mine_ref.shape[1] - HEAD
-    piece = (stride - 16) // 2
+    size = mine_ref.shape[1] - HEAD
+    stride = a_ref.shape[0] // devices
+    piece = (size - 16) // 2
     half = blocks // 2
     for ref, which in ((mine_ref, core), (other_ref, 1 - core)):
         for c in range(chips):
             for q in range(4):
                 rows = pl.ds(pl.multiple_of(2 * PIECE * c + PIECE * which, PIECE), PIECE)
                 w2_ref[rows, LANE * q : LANE * (q + 1)] = ref[c, PIECE * q : PIECE * (q + 1), :]
-            rows = pl.ds(pl.multiple_of(stride * (2 * c + which), SUB), stride)
+            rows = pl.ds(pl.multiple_of(stride * (2 * c + which), SUB), size)
             a_ref[rows, :] = ref[c, HEAD:, :].astype(f32)
     for q in range(4):
         for r in range(4):
@@ -341,6 +343,7 @@
     heat_grad = rhs_grad.astype(bf16)
     tanh_two = jnp.tanh(contract_first(w2, act_one))
     act_two = tanh_two.astype(bf16)
+    act2_ref[...] = act_two
     back_two = jnp.dot(w3, heat_grad, preferred_element_type=f32)
     pre_two_grad = (back_two * (1.0 - tanh_two * tanh_two)).astype(bf16)
     back_one = jnp.dot(w2, pre_two_grad, preferred_element_type=f32)
@@ -352,9 +355,11 @@
     outs = (out0_ref, out1_ref, out2_ref, out3_ref)
     targets = [device ^ (2 * k) for k in range(GROUPS)]
     for k, target in enumerate(targets):
-        sel_ref[PIECE * k : PIECE * (k + 1), :] = act_ref[pl.ds(pl.multiple_of(PIECE * target, PIECE), PIECE), :]
+        hid = pl.ds(pl.multiple_of(PIECE * target, PIECE), PIECE)
+        sel_ref[PIECE * k : PIECE * (k + 1), :] = act_ref[hid, :]
+        sel2_ref[PIECE * k : PIECE * (k + 1), :] = act2_ref[hid, :]
     local_two = contract_last(sel_ref[...], pre_two_grad)
-    local_three = contract_last(heat_grad, act_two)
+    local_three = contract_last(heat_grad, sel2_ref[...])
     g_ref[...] = contract_last(column_input, pre_one_grad)
     fields = jnp.concatenate([press_next, wind_next, star_grad], axis=1).astype(bf16)
     stored = lax.dot_general(place, fields, (((0,), (0,)), ((), ())), preferred_element_type=f32)
@@ -363,13 +368,11 @@
         y_ref[pl.ds(4 + k, devices, stride=back), :] = stored[:, LANE * k : LANE * (k + 1)]
     for k in range(4 + 3 * blocks, back):
         y_ref[pl.ds(k, devices, stride=back), :] = jnp.zeros((devices, LANE), f32)
-    for t in range(devices // 4):
-        t_ref[16 * t : 16 * t + 16, :] = local_three[:, LANE * t : LANE * (t + 1)]
+    t_ref[...] = local_three
     for k, (target, out_ref) in enumerate(zip(targets, outs)):
         pair = g_ref[pl.ds(pl.multiple_of(SUB * (target // 2), SUB), SUB), :]
         one = jnp.where(core == 0, pair[:4, :], pair[4:, :])
-        tile = t_ref[pl.ds(pl.multiple_of(16 * (target // 4), 16), 16), :]
-        tile = pltpu.roll(tile, (LANE - PIECE * (target % 4)) % LANE, 1)
+        tile = t_ref[...] if k == 0 else pltpu.roll(t_ref[...], LANE - PIECE * k, 1)
         three = tile[:4, :]
         for q in range(4):
             cols = slice(LANE * q, LANE * (q + 1))
@@ -455,15 +458,16 @@
     send_back = call(
         column_kernel, "column_step", (block,) * GROUPS, 5,
         [
-            pltpu.VMEM((devices * (16 + 2 * piece), LANE), f32), pltpu.VMEM((16 * devices, LANE), f32),
+            pltpu.VMEM((devices * STRIDE, LANE), f32), pltpu.VMEM((16 * devices, LANE), f32),
             pltpu.VMEM((hidden, hidden), bf16), pltpu.VMEM((levels, hidden), f32), pltpu.VMEM((hidden, width), bf16),
             pltpu.VMEM((GROUPS * PIECE, width), bf16), pltpu.VMEM((4 * levels, hidden), f32), pltpu.VMEM((16, LANE), f32),
-            pltpu.VMEM((devices * back, LANE), f32), pltpu.VMEM((4 * devices, LANE), f32),
+            pltpu.VMEM((devices * back, LANE), f32), pltpu.VMEM((levels, LANE), f32),
+            pltpu.VMEM((hidden, width), bf16), pltpu.VMEM((GROUPS * PIECE, width), bf16),
         ],
     )(mine, other, *operators)
-    received = [send_back[0]] + [
-        lax.ppermute(send_back[k], "slab", [(i, i ^ (2 * k)) for i in range(devices)]) for k in range(1, GROUPS)
-    ]
+    received = [send_back[0]] * GROUPS
+    for k in range(GROUPS - 1, 0, -1):
+        received[k] = lax.ppermute(send_back[k], "slab", [(i, i ^ (2 * k)) for i in range(devices)])
     field_out = shape((rows, LANE), f32)
     new_pressure, new_wind, grad, first_grad, second_grad, third_grad = call(
         functools.partial(finish_kernel, 1.0 / math.sqrt(columns)), "finish",

time: 38.6 us -> 38 us (0.984)
  Pallas kernels: 9.36 us -> 8.74 us
    pallas_call x1, Pallas kernels: 5.55 us -> 4.93 us  [fast_body(): call(column_kernel, 'column_step', (block,) * GROUPS, 5, [pltpu.VMEM((dev...]
where the time goes in v6:
time: 38 us; the launch traced here: 37.8 us
  blocking collectives  20.3 us (53%)
  Pallas kernels  8.74 us (23%)
  waiting for transfers between devices  3.86 us (10%)
  starting transfers between devices  3.56 us (9%)
  local copies, waits for them, and re-layouts  0.68 us (2%)
  between operations  0.67 us (2%)
    all_to_all x1, blocking collectives, exchange(): lax.all_to_all(blocks_of_chips, 'slab', split_axis=0, concat_axis=0, tile...  20.3 us
    pallas_call x1, Pallas kernels, fast_body(): call(column_kernel, 'column_step', (block,) * GROUPS, 5, [pltpu.VMEM((dev...  4.93 us
    ppermute x3, starting transfers between devices, fast_body(): lax.ppermute(send_back[k], 'slab', [(i, i ^ 2 * k) for i in range(devices)])  3.55 us
    pallas_call x1, Pallas kernels, fast_body(): call(pack_kernel, 'pack', shape((chips, TAIL + 2 * piece, LANE), bf16), l...  2.99 us
    ppermute x3, waiting for transfers between devices, fast_body(): lax.ppermute(send_back[k], 'slab', [(i, i ^ 2 * k) for i in range(devices)])  2.87 us
    ppermute x1, waiting for transfers between devices, fast_body(): other = lax.ppermute(mine, 'slab', [(i, i ^ 1) for i in range(devices)])  0.99 us
  transfers between devices with their start and end apart: 4, of which 4 were waited for; matrix products, arithmetic and copies ran while one was open for 0% of the time, Pallas kernels for 0%

profile of v6, /device:TPU:0, one launch (start us, length us, event | category | flops | bytes accessed | tf_op | source)
XLA Modules:
  0.0 37.8 jit_solution(6100050549793240605)
XLA Ops:
  0.6 3.0 %pack.1 = bf16[8,224,128]{2,1,0:T(8,128)(2,1)S(1)} custom-call(f32[48,128]{1,0:T(8,128)} %bitcast.26, f32[48,128]{1,0:T(8,128)} %bitcast.27, f32[48,128]{1,0:T(8,128)} %bitcast.28, f32[2,48,128]{2,1,0:T(8,128)} %bitcast.24, f32[48,2,128]{2,1,0:T(2,128)} %bitcast.25, s32[48,4,128]{2,1,0:T(4,128)} %bitcast.23, bf16[4,512]{1,0:T(4,128)(2,1)} %one_hbm.1, ...), custom_call_target="tpu_custom_call" | custom-call | tf_op jit(solution)/shard_map/pack/pallas_call | solution.py:446
  3.6 20.3 %all_to_all.5.mine_ref = bf16[8,224,128]{2,1,0:T(8,128)(2,1)S(1)} all-to-all(bf16[8,224,128]{2,1,0:T(8,128)(2,1)S(1)} %pack.1), channel_id=1, replica_groups={{0,2,4,6,8,10,12,14},{1,3,5,7,9,11,13,15},{16,18,20,22,24,26,28,30},{17..., dimensions={0} | all-to-all | bytes 917504 | tf_op jit(solution)/shard_map/all_to_all | solution.py:439
  23.9 0.0 collective-permute-start
  23.9 0.0 copy-start
  23.9 0.0 copy-start.1
  23.9 0.0 copy-start.2
  23.9 0.6 %copy-done = s32[16]{0:T(128)S(1)} copy-done((s32[16]{0:T(128)S(1)}, s32[16]{0:T(128)}, u32[]{:S(2)}) %copy-start) | copy-done | bytes 88
  24.6 0.0 copy-done.1
  24.6 0.0 copy-done.2
  24.6 0.1 operators.1
  24.7 1.0 %collective-permute-done.other_ref = bf16[8,224,128]{2,1,0:T(8,128)(2,1)S(1)} collective-permute-done((bf16[8,224,128]{2,1,0:T(8,128)(2,1)S(1)}, bf16[8,224,128]{2,1,0:T(8,128)(2,1)S(1)}, u32[]{:S(2)}, u32[]{:S(2)}) %collective-permute-start) | collective-permute-done | bytes 458784 | tf_op jit(solution)/shard_map/ppermute | solution.py:456
  25.7 4.9 %column_step.1 = (bf16[184,128]{1,0:T(8,128)(2,1)S(1)}, bf16[184,128]{1,0:T(8,128)(2,1)S(1)}, bf16[184,128]{1,0:T(8,128)(2,1)S(1)}, bf16[184,128]{1,0:T(8,128)(2,1)S(1)}) custom-call(bf16[8,224,128]{2,1,0:T(8,128)(2,1)S(1)} %all_to_all.5.mine_ref, bf16[8,224,128]{2,1,0:T(8,128)(2,1)S(1)} %collective-permute-done.other_ref, ...), custom_call_target="tpu_custom_call" | custom-call | tf_op jit(solution)/shard_map/column_step/pallas_call | solution.py:458
  30.7 1.4 %collective-permute-start.1 = (bf16[184,128]{1,0:T(8,128)(2,1)S(1)}, bf16[184,128]{1,0:T(8,128)(2,1)S(1)}, u32[]{:S(2)}, u32[]{:S(2)}) collective-permute-start(bf16[184,128]{1,0:T(8,128)(2,1)S(1)} %get-tuple-element.23), channel_id=1, source_target_pairs={{0,2},{1,3},{2,0},{3,1},{4,6},{5,7},{6,4},{7,5},{8,10},{9,11},{10,... | collective-permute-start | bytes 141320 | tf_op jit(solution)/shard_map/ppermute | solution.py:470
  32.1 0.0 collective-permute-start.2
  32.1 2.1 %collective-permute-start.3 = (bf16[184,128]{1,0:T(8,128)(2,1)S(1)}, bf16[184,128]{1,0:T(8,128)(2,1)S(1)}, u32[]{:S(2)}, u32[]{:S(2)}) collective-permute-start(bf16[184,128]{1,0:T(8,128)(2,1)S(1)} %get-tuple-element.25), channel_id=1, source_target_pairs={{0,6},{1,7},{2,4},{3,5},{4,2},{5,3},{6,0},{7,1},{8,14},{9,15},{10,... | collective-permute-start | bytes 141320 | tf_op jit(solution)/shard_map/ppermute | solution.py:470
  34.2 0.6 %collective-permute-done.1.r1_ref = bf16[184,128]{1,0:T(8,128)(2,1)S(1)} collective-permute-done((bf16[184,128]{1,0:T(8,128)(2,1)S(1)}, bf16[184,128]{1,0:T(8,128)(2,1)S(1)}, u32[]{:S(2)}, u32[]{:S(2)}) %collective-permute-start.1) | collective-permute-done | bytes 47136 | tf_op jit(solution)/shard_map/ppermute | solution.py:470
  34.8 1.7 %collective-permute-done.2.r2_ref = bf16[184,128]{1,0:T(8,128)(2,1)S(1)} collective-permute-done((bf16[184,128]{1,0:T(8,128)(2,1)S(1)}, bf16[184,128]{1,0:T(8,128)(2,1)S(1)}, u32[]{:S(2)}, u32[]{:S(2)}) %collective-permute-start.2) | collective-permute-done | bytes 47136 | tf_op jit(solution)/shard_map/ppermute | solution.py:470
  36.5 0.6 %collective-permute-done.3.r3_ref = bf16[184,128]{1,0:T(8,128)(2,1)S(1)} collective-permute-done((bf16[184,128]{1,0:T(8,128)(2,1)S(1)}, bf16[184,128]{1,0:T(8,128)(2,1)S(1)}, u32[]{:S(2)}, u32[]{:S(2)}) %collective-permute-start.3) | collective-permute-done | bytes 47136 | tf_op jit(solution)/shard_map/ppermute | solution.py:470
  37.1 0.7 %finish.1 = (f32[48,128]{1,0:T(8,128)}, f32[48,128]{1,0:T(8,128)}, f32[48,128]{1,0:T(8,128)}, f32[4,512]{1,0:T(4,128)}, f32[32,512]{1,0:T(8,128)}, /*index=5*/f32[16,32]{1,0:T(8,128)}) custom-call(bf16[184,128]{1,0:T(8,128)(2,1)S(1)} %get-tuple-element.22.r0_ref, bf16[184,128]{1,0:T(8,128)(2,1)S(1)} %collective-permute-done.1.r1_ref, ...), custom_call_target="tpu_custom_call" | custom-call | tf_op jit(solution)/shard_map/finish/pallas_call | solution.py:472
Async XLA Ops:
  23.9 1.8 %collective-permute-start = (bf16[8,224,128]{2,1,0:T(8,128)(2,1)S(1)}, bf16[8,224,128]{2,1,0:T(8,128)(2,1)S(1)}, u32[]{:S(2)}, u32[]{:S(2)}) collective-permute-start(bf16[8,224,128]{2,1,0:T(8,128)(2,1)S(1)} %all_to_all.5.mine_ref), channel_id=1, source_target_pairs={{0,1},{1,0},{2,3},{3,2},{4,5},{5,4},{6,7},{7,6},{8,9},{9,8},{10,11... | collective-permute-start | bytes 1376264 | tf_op jit(solution)/shard_map/ppermute | solution.py:456
  23.9 0.7 %copy-start = (s32[16]{0:T(128)S(1)}, s32[16]{0:T(128)}, u32[]{:S(2)}) copy-start(s32[16]{0:T(128)} %param.20) | copy-start | bytes 196
  23.9 0.7 %copy-start.1 = (f32[16]{0:T(128)S(1)}, f32[16]{0:T(128)}, u32[]{:S(2)}) copy-start(f32[16]{0:T(128)} %param.21) | copy-start | bytes 196
  23.9 0.7 %copy-start.2 = (f32[16]{0:T(128)S(1)}, f32[16]{0:T(128)}, u32[]{:S(2)}) copy-start(f32[16]{0:T(128)} %param.22) | copy-start | bytes 196
  30.7 4.1 %collective-permute-start.1 = (bf16[184,128]{1,0:T(8,128)(2,1)S(1)}, bf16[184,128]{1,0:T(8,128)(2,1)S(1)}, u32[]{:S(2)}, u32[]{:S(2)}) collective-permute-start(bf16[184,128]{1,0:T(8,128)(2,1)S(1)} %get-tuple-element.23), channel_id=1, source_target_pairs={{0,2},{1,3},{2,0},{3,1},{4,6},{5,7},{6,4},{7,5},{8,10},{9,11},{10,... | collective-permute-start | bytes 141320 | tf_op jit(solution)/shard_map/ppermute | solution.py:470
  32.1 4.4 %collective-permute-start.2 = (bf16[184,128]{1,0:T(8,128)(2,1)S(1)}, bf16[184,128]{1,0:T(8,128)(2,1)S(1)}, u32[]{:S(2)}, u32[]{:S(2)}) collective-permute-start(bf16[184,128]{1,0:T(8,128)(2,1)S(1)} %get-tuple-element.24), channel_id=1, source_target_pairs={{0,4},{1,5},{2,6},{3,7},{4,0},{5,1},{6,2},{7,3},{8,12},{9,13},{10,... | collective-permute-start | bytes 141320 | tf_op jit(solution)/shard_map/ppermute | solution.py:470
  32.1 5.0 %collective-permute-start.3 = (bf16[184,128]{1,0:T(8,128)(2,1)S(1)}, bf16[184,128]{1,0:T(8,128)(2,1)S(1)}, u32[]{:S(2)}, u32[]{:S(2)}) collective-permute-start(bf16[184,128]{1,0:T(8,128)(2,1)S(1)} %get-tuple-element.25), channel_id=1, source_target_pairs={{0,6},{1,7},{2,4},{3,5},{4,2},{5,3},{6,0},{7,1},{8,14},{9,15},{10,... | collective-permute-start | bytes 141320 | tf_op jit(solution)/shard_map/ppermute | solution.py:470

commit v7 on v6

--- a/solution.py
+++ b/solution.py
@@ -163,21 +163,31 @@
     return jax.ShapeDtypeStruct(dims, kind)
 
 
-def difference(table_ref, first, second):
-    groups = table_ref.shape[0] // SUB
+def pair_up(table):
+    half = table.shape[0] // 2
+    largest = jnp.max(jnp.max(jnp.abs(table), axis=0, keepdims=True), axis=1, keepdims=True)
+    scale = jnp.where(largest > 0.0, 32767.0 / jnp.maximum(largest, 1e-30), 0.0)
+    steps = jnp.floor(table * scale + 0.5).astype(jnp.int32)
+    return (steps[half:] << 16) | (steps[:half] & 0xFFFF), largest * (1.0 / 32767.0)
+
+
+def difference(words, first, second):
+    half = words.shape[0]
     sublanes = lax.broadcasted_iota(jnp.int32, (SUB, LANE), 0)
     out = []
     for r in range(SUB):
         kept = []
         for index in (first, second):
-            high = jnp.broadcast_to(index[r : r + 1, :] >> 7, (SUB, LANE))
-            low = jnp.broadcast_to(index[r : r + 1, :] & (LANE - 1), (SUB, LANE))
-            total = jnp.zeros((SUB, LANE), jnp.float32)
-            for g in range(groups):
-                picked = jnp.take_along_axis(table_ref[SUB * g : SUB * g + SUB, :], low, axis=1, mode="promise_in_bounds")
+            row = jnp.broadcast_to(index[r : r + 1, :], (SUB, LANE))
+            high, low = row >> 7, row & (LANE - 1)
+            late = high >= half
+            high = jnp.where(late, high - half, high)
+            total = jnp.zeros((SUB, LANE), jnp.int32)
+            for g in range(half // SUB):
+                picked = jnp.take_along_axis(words[SUB * g : SUB * g + SUB, :], low, axis=1, mode="promise_in_bounds")
                 total = jnp.where(high == sublanes + SUB * g, picked, total)
-            kept.append(total)
-        out.append(jnp.sum(kept[0] - kept[1], axis=0, keepdims=True))
+            kept.append(jnp.where(late, total, total << 16) >> 16)
+        out.append(jnp.sum((kept[0] - kept[1]).astype(jnp.float32), axis=0, keepdims=True))
     return jnp.concatenate(out, axis=0)
 
 
@@ -206,10 +216,12 @@
     def put(f, j, tile):
         f_ref[pl.ds(blocks * f + j, SUB, stride=piece), :] = tile
 
+    words_one, step_one = pair_up(u_ref[0])
+    words_two, step_two = pair_up(u_ref[1])
     for j in range(blocks):
         rows = slice(SUB * j, SUB * j + SUB)
-        along = difference(u_ref.at[0], n_ref[rows, 0, :], n_ref[rows, 1, :])
-        across = difference(u_ref.at[1], n_ref[rows, 2, :], n_ref[rows, 3, :])
+        along = difference(words_one, n_ref[rows, 0, :], n_ref[rows, 1, :]) * step_one
+        across = difference(words_two, n_ref[rows, 2, :], n_ref[rows, 3, :]) * step_two
         diverg = m_ref[rows, 0, :] * along + m_ref[rows, 1, :] * across
         for f, tile in enumerate((p_ref[rows, :] - diverg, d_ref[rows, :], w_ref[rows, :], diverg, pa_ref[rows, :], wa_ref[rows, :])):
             put(f, j, tile)
@@ -490,7 +502,7 @@
     return (
         pressure.shape[0] == 1
         and level_order.shape[0] == 2 * SUB
-        and neighbors.shape[1] % (LANE * SUB) == 0
+        and neighbors.shape[1] % (2 * LANE * SUB) == 0
         and weight_one.shape == (4, 4 * LANE)
         and weight_two.shape == (PIECE, 4 * LANE)
         and weight_three.shape == (PIECE, 2 * SUB)

time: 38 us -> 37.5 us (0.987)
  Pallas kernels: 8.74 us -> 8.3 us
    pallas_call x1, Pallas kernels: 2.99 us -> 2.55 us  [fast_body(): call(pack_kernel, 'pack', shape((chips, TAIL + 2 * piece, LANE), bf16), l...]
where the time goes in v7:
time: 37.5 us; the launch traced here: 37.3 us
  blocking collectives  20.3 us (54%)
  Pallas kernels  8.3 us (22%)
  waiting for transfers between devices  3.86 us (10%)
  starting transfers between devices  3.56 us (9%)
  local copies, waits for them, and re-layouts  0.68 us (2%)
  between operations  0.67 us (2%)
    all_to_all x1, blocking collectives, exchange(): lax.all_to_all(blocks_of_chips, 'slab', split_axis=0, concat_axis=0, tile...  20.3 us
    pallas_call x1, Pallas kernels, fast_body(): call(column_kernel, 'column_step', (block,) * GROUPS, 5, [pltpu.VMEM((dev...  4.93 us
    ppermute x3, starting transfers between devices, fast_body(): lax.ppermute(send_back[k], 'slab', [(i, i ^ 2 * k) for i in range(devices)])  3.55 us
    ppermute x3, waiting for transfers between devices, fast_body(): lax.ppermute(send_back[k], 'slab', [(i, i ^ 2 * k) for i in range(devices)])  2.87 us
    pallas_call x1, Pallas kernels, fast_body(): call(pack_kernel, 'pack', shape((chips, TAIL + 2 * piece, LANE), bf16), l...  2.55 us
    ppermute x1, waiting for transfers between devices, fast_body(): other = lax.ppermute(mine, 'slab', [(i, i ^ 1) for i in range(devices)])  0.99 us
  transfers between devices with their start and end apart: 4, of which 4 were waited for; matrix products, arithmetic and copies ran while one was open for 0% of the time, Pallas kernels for 0%

profile of v7, /device:TPU:0, one launch (start us, length us, event | category | flops | bytes accessed | tf_op | source)
XLA Modules:
  0.0 37.3 jit_solution(4575232906216646997)
XLA Ops:
  0.6 2.5 %pack.1 = bf16[8,224,128]{2,1,0:T(8,128)(2,1)S(1)} custom-call(f32[48,128]{1,0:T(8,128)} %bitcast.26, f32[48,128]{1,0:T(8,128)} %bitcast.27, f32[48,128]{1,0:T(8,128)} %bitcast.28, f32[2,48,128]{2,1,0:T(8,128)} %bitcast.24, f32[48,2,128]{2,1,0:T(2,128)} %bitcast.25, s32[48,4,128]{2,1,0:T(4,128)} %bitcast.23, bf16[4,512]{1,0:T(4,128)(2,1)} %one_hbm.1, ...), custom_call_target="tpu_custom_call" | custom-call | tf_op jit(solution)/shard_map/pack/pallas_call | solution.py:458
  3.2 20.3 %all_to_all.5.mine_ref = bf16[8,224,128]{2,1,0:T(8,128)(2,1)S(1)} all-to-all(bf16[8,224,128]{2,1,0:T(8,128)(2,1)S(1)} %pack.1), channel_id=1, replica_groups={{0,2,4,6,8,10,12,14},{1,3,5,7,9,11,13,15},{16,18,20,22,24,26,28,30},{17..., dimensions={0} | all-to-all | bytes 917504 | tf_op jit(solution)/shard_map/all_to_all | solution.py:451
  23.5 0.0 collective-permute-start
  23.5 0.0 copy-start
  23.5 0.0 copy-start.1
  23.5 0.0 copy-start.2
  23.5 0.6 %copy-done = s32[16]{0:T(128)S(1)} copy-done((s32[16]{0:T(128)S(1)}, s32[16]{0:T(128)}, u32[]{:S(2)}) %copy-start) | copy-done | bytes 88
  24.1 0.0 copy-done.1
  24.2 0.0 copy-done.2
  24.2 0.1 operators.1
  24.3 1.0 %collective-permute-done.other_ref = bf16[8,224,128]{2,1,0:T(8,128)(2,1)S(1)} collective-permute-done((bf16[8,224,128]{2,1,0:T(8,128)(2,1)S(1)}, bf16[8,224,128]{2,1,0:T(8,128)(2,1)S(1)}, u32[]{:S(2)}, u32[]{:S(2)}) %collective-permute-start) | collective-permute-done | bytes 458784 | tf_op jit(solution)/shard_map/ppermute | solution.py:468
  25.3 4.9 %column_step.1 = (bf16[184,128]{1,0:T(8,128)(2,1)S(1)}, bf16[184,128]{1,0:T(8,128)(2,1)S(1)}, bf16[184,128]{1,0:T(8,128)(2,1)S(1)}, bf16[184,128]{1,0:T(8,128)(2,1)S(1)}) custom-call(bf16[8,224,128]{2,1,0:T(8,128)(2,1)S(1)} %all_to_all.5.mine_ref, bf16[8,224,128]{2,1,0:T(8,128)(2,1)S(1)} %collective-permute-done.other_ref, ...), custom_call_target="tpu_custom_call" | custom-call | tf_op jit(solution)/shard_map/column_step/pallas_call | solution.py:470
  30.2 1.4 %collective-permute-start.1 = (bf16[184,128]{1,0:T(8,128)(2,1)S(1)}, bf16[184,128]{1,0:T(8,128)(2,1)S(1)}, u32[]{:S(2)}, u32[]{:S(2)}) collective-permute-start(bf16[184,128]{1,0:T(8,128)(2,1)S(1)} %get-tuple-element.23), channel_id=1, source_target_pairs={{0,2},{1,3},{2,0},{3,1},{4,6},{5,7},{6,4},{7,5},{8,10},{9,11},{10,... | collective-permute-start | bytes 141320 | tf_op jit(solution)/shard_map/ppermute | solution.py:482
  31.6 0.0 collective-permute-start.2
  31.7 2.1 %collective-permute-start.3 = (bf16[184,128]{1,0:T(8,128)(2,1)S(1)}, bf16[184,128]{1,0:T(8,128)(2,1)S(1)}, u32[]{:S(2)}, u32[]{:S(2)}) collective-permute-start(bf16[184,128]{1,0:T(8,128)(2,1)S(1)} %get-tuple-element.25), channel_id=1, source_target_pairs={{0,6},{1,7},{2,4},{3,5},{4,2},{5,3},{6,0},{7,1},{8,14},{9,15},{10,... | collective-permute-start | bytes 141320 | tf_op jit(solution)/shard_map/ppermute | solution.py:482
  33.8 0.6 %collective-permute-done.1.r1_ref = bf16[184,128]{1,0:T(8,128)(2,1)S(1)} collective-permute-done((bf16[184,128]{1,0:T(8,128)(2,1)S(1)}, bf16[184,128]{1,0:T(8,128)(2,1)S(1)}, u32[]{:S(2)}, u32[]{:S(2)}) %collective-permute-start.1) | collective-permute-done | bytes 47136 | tf_op jit(solution)/shard_map/ppermute | solution.py:482
  34.4 1.7 %collective-permute-done.2.r2_ref = bf16[184,128]{1,0:T(8,128)(2,1)S(1)} collective-permute-done((bf16[184,128]{1,0:T(8,128)(2,1)S(1)}, bf16[184,128]{1,0:T(8,128)(2,1)S(1)}, u32[]{:S(2)}, u32[]{:S(2)}) %collective-permute-start.2) | collective-permute-done | bytes 47136 | tf_op jit(solution)/shard_map/ppermute | solution.py:482
  36.0 0.6 %collective-permute-done.3.r3_ref = bf16[184,128]{1,0:T(8,128)(2,1)S(1)} collective-permute-done((bf16[184,128]{1,0:T(8,128)(2,1)S(1)}, bf16[184,128]{1,0:T(8,128)(2,1)S(1)}, u32[]{:S(2)}, u32[]{:S(2)}) %collective-permute-start.3) | collective-permute-done | bytes 47136 | tf_op jit(solution)/shard_map/ppermute | solution.py:482
  36.6 0.7 %finish.1 = (f32[48,128]{1,0:T(8,128)}, f32[48,128]{1,0:T(8,128)}, f32[48,128]{1,0:T(8,128)}, f32[4,512]{1,0:T(4,128)}, f32[32,512]{1,0:T(8,128)}, /*index=5*/f32[16,32]{1,0:T(8,128)}) custom-call(bf16[184,128]{1,0:T(8,128)(2,1)S(1)} %get-tuple-element.22.r0_ref, bf16[184,128]{1,0:T(8,128)(2,1)S(1)} %collective-permute-done.1.r1_ref, ...), custom_call_target="tpu_custom_call" | custom-call | tf_op jit(solution)/shard_map/finish/pallas_call | solution.py:484
Async XLA Ops:
  23.5 1.8 %collective-permute-start = (bf16[8,224,128]{2,1,0:T(8,128)(2,1)S(1)}, bf16[8,224,128]{2,1,0:T(8,128)(2,1)S(1)}, u32[]{:S(2)}, u32[]{:S(2)}) collective-permute-start(bf16[8,224,128]{2,1,0:T(8,128)(2,1)S(1)} %all_to_all.5.mine_ref), channel_id=1, source_target_pairs={{0,1},{1,0},{2,3},{3,2},{4,5},{5,4},{6,7},{7,6},{8,9},{9,8},{10,11... | collective-permute-start | bytes 1376264 | tf_op jit(solution)/shard_map/ppermute | solution.py:468
  23.5 0.7 %copy-start = (s32[16]{0:T(128)S(1)}, s32[16]{0:T(128)}, u32[]{:S(2)}) copy-start(s32[16]{0:T(128)} %param.20) | copy-start | bytes 196
  23.5 0.7 %copy-start.1 = (f32[16]{0:T(128)S(1)}, f32[16]{0:T(128)}, u32[]{:S(2)}) copy-start(f32[16]{0:T(128)} %param.21) | copy-start | bytes 196
  23.5 0.7 %copy-start.2 = (f32[16]{0:T(128)S(1)}, f32[16]{0:T(128)}, u32[]{:S(2)}) copy-start(f32[16]{0:T(128)} %param.22) | copy-start | bytes 196
  30.2 4.1 %collective-permute-start.1 = (bf16[184,128]{1,0:T(8,128)(2,1)S(1)}, bf16[184,128]{1,0:T(8,128)(2,1)S(1)}, u32[]{:S(2)}, u32[]{:S(2)}) collective-permute-start(bf16[184,128]{1,0:T(8,128)(2,1)S(1)} %get-tuple-element.23), channel_id=1, source_target_pairs={{0,2},{1,3},{2,0},{3,1},{4,6},{5,7},{6,4},{7,5},{8,10},{9,11},{10,... | collective-permute-start | bytes 141320 | tf_op jit(solution)/shard_map/ppermute | solution.py:482
  31.6 4.4 %collective-permute-start.2 = (bf16[184,128]{1,0:T(8,128)(2,1)S(1)}, bf16[184,128]{1,0:T(8,128)(2,1)S(1)}, u32[]{:S(2)}, u32[]{:S(2)}) collective-permute-start(bf16[184,128]{1,0:T(8,128)(2,1)S(1)} %get-tuple-element.24), channel_id=1, source_target_pairs={{0,4},{1,5},{2,6},{3,7},{4,0},{5,1},{6,2},{7,3},{8,12},{9,13},{10,... | collective-permute-start | bytes 141320 | tf_op jit(solution)/shard_map/ppermute | solution.py:482
  31.7 5.0 %collective-permute-start.3 = (bf16[184,128]{1,0:T(8,128)(2,1)S(1)}, bf16[184,128]{1,0:T(8,128)(2,1)S(1)}, u32[]{:S(2)}, u32[]{:S(2)}) collective-permute-start(bf16[184,128]{1,0:T(8,128)(2,1)S(1)} %get-tuple-element.25), channel_id=1, source_target_pairs={{0,6},{1,7},{2,4},{3,5},{4,2},{5,3},{6,0},{7,1},{8,14},{9,15},{10,... | collective-permute-start | bytes 141320 | tf_op jit(solution)/shard_map/ppermute | solution.py:482

commit v8 on v7

--- a/solution.py
+++ b/solution.py
@@ -145,6 +145,7 @@
 PIECE = 32
 HEAD = 4 * PIECE
 TAIL = HEAD + 16
+FRONT = TAIL + 8
 
 
 def call(kernel, name, outs, n_in, scratch=(), space=pltpu.VMEM):
@@ -196,8 +197,9 @@
 
 
 def pack_kernel(
-    p_hbm, d_hbm, w_hbm, u_hbm, m_hbm, n_hbm, one_hbm, two_hbm, three_hbm, pa_hbm, wa_hbm, out_ref,
-    p_ref, d_ref, w_ref, u_ref, m_ref, n_ref, one_ref, two_ref, three_ref, pa_ref, wa_ref, part_ref, f_ref, sems,
+    p_hbm, d_hbm, w_hbm, u_hbm, m_hbm, n_hbm, one_hbm, two_hbm, three_hbm, pa_hbm, wa_hbm,
+    whole_ref, out0_ref, out1_ref, out2_ref, out3_ref,
+    p_ref, d_ref, w_ref, u_ref, m_ref, n_ref, one_ref, two_ref, three_ref, pa_ref, wa_ref, part_ref, f_ref, g_ref, sems,
 ):
     pairs = (
         (n_hbm, n_ref), (u_hbm, u_ref), (m_hbm, m_ref), (p_hbm, p_ref), (d_hbm, d_ref), (w_hbm, w_ref),
@@ -207,7 +209,6 @@
     for copy in copies:
         copy.start()
     f32, bf16 = jnp.float32, jnp.bfloat16
-    chips = out_ref.shape[0]
     piece = f_ref.shape[0] // SUB
     blocks = p_ref.shape[0] // SUB
     for copy in copies:
@@ -236,17 +237,31 @@
     for q in range(4):
         part_ref[4 * q : 4 * q + 4, :] = one[:, LANE * q : LANE * (q + 1)]
     one = part_ref[...].astype(bf16)
-    for c in range(chips):
+    part_ref[0:4, :] = three
+    part_ref[4:8, :] = jnp.zeros((4, LANE), f32)
+    three = part_ref[0:8, :].astype(bf16)
+    for g in range(GROUPS):
+        both = [f_ref[piece * c : piece * (c + 1), :] for c in (g, g + GROUPS)]
+        g_ref[2 * piece * g : 2 * piece * (g + 1), :] = jnp.concatenate(both, axis=0)
+    group = lax.axis_index("slab") // 2 % GROUPS
+    outs = (out0_ref, out1_ref, out2_ref, out3_ref)
+    for ref in (whole_ref,) + outs:
         for q in range(4):
-            out_ref[c, PIECE * q : PIECE * (q + 1), :] = two_ref[:, LANE * q : LANE * (q + 1)]
-        out_ref[c, HEAD:TAIL, :] = one
-        f_ref[piece * c + 6 * blocks : piece * c + 6 * blocks + 4, :] = three
-        if piece > 6 * blocks + 4:
-            f_ref[piece * c + 6 * blocks + 4 : piece * (c + 1), :] = jnp.zeros((piece - 6 * blocks - 4, LANE), f32)
-    for g in range(GROUPS):
-        both = jnp.concatenate([f_ref[piece * c : piece * (c + 1), :] for c in (g, g + GROUPS)], axis=0).astype(bf16)
-        for c in range(g, chips, GROUPS):
-            out_ref[c, TAIL:, :] = both
+            ref[PIECE * q : PIECE * (q + 1), :] = two_ref[:, LANE * q : LANE * (q + 1)]
+        ref[HEAD:TAIL, :] = one
+        ref[TAIL:FRONT, :] = three
+    whole_ref[FRONT:, :] = g_ref[...].astype(bf16)
+    for k, ref in enumerate(outs):
+        ref[FRONT:, :] = g_ref[pl.ds(pl.multiple_of(2 * piece * (group ^ k), SUB), 2 * piece), :].astype(bf16)
+
+
+def relay_kernel(whole_ref, out0_ref, out1_ref, out2_ref, out3_ref, g_ref):
+    size = out0_ref.shape[0] - FRONT
+    group = lax.axis_index("slab") // 2 % GROUPS
+    g_ref[...] = whole_ref[FRONT:, :].astype(jnp.float32)
+    for k, ref in enumerate((out0_ref, out1_ref, out2_ref, out3_ref)):
+        ref[:FRONT, :] = whole_ref[:FRONT, :]
+        ref[FRONT:, :] = g_ref[pl.ds(pl.multiple_of(size * (group ^ k), SUB), size), :].astype(jnp.bfloat16)
 
 
 def shifted_up(field, rows):
@@ -286,36 +301,35 @@
     column_ref[...] = jnp.broadcast_to(couple, column_ref.shape)
 
 
-def column_kernel(
-    mine_ref, other_ref, place_ref, inverse_ref, column_ref, out0_ref, out1_ref, out2_ref, out3_ref,
-    a_ref, one_ref, w2_ref, w3_ref, act_ref, sel_ref, g_ref, h_ref, y_ref, t_ref, act2_ref, sel2_ref,
-):
+def column_kernel(*refs):
+    sources = refs[: 4 * GROUPS]
+    place_ref, inverse_ref, column_ref, out0_ref, out1_ref, out2_ref, out3_ref = refs[4 * GROUPS : 4 * GROUPS + 7]
+    (
+        a_ref, one_ref, w2_ref, w3_ref, act_ref, sel_ref, g_ref, h_ref, y_ref, t_ref, act2_ref, sel2_ref,
+    ) = refs[4 * GROUPS + 7 :]
     f32, bf16 = jnp.float32, jnp.bfloat16
     device = lax.axis_index("slab")
     core = device % 2
-    chips = mine_ref.shape[0]
-    devices = 2 * chips
+    devices = 4 * GROUPS
     levels = inverse_ref.shape[0]
     width = act_ref.shape[1]
     blocks = width // LANE
-    size = mine_ref.shape[1] - HEAD
+    half = blocks // 2
     stride = a_ref.shape[0] // devices
-    piece = (size - 16) // 2
-    half = blocks // 2
-    for ref, which in ((mine_ref, core), (other_ref, 1 - core)):
-        for c in range(chips):
-            for q in range(4):
-                rows = pl.ds(pl.multiple_of(2 * PIECE * c + PIECE * which, PIECE), PIECE)
-                w2_ref[rows, LANE * q : LANE * (q + 1)] = ref[c, PIECE * q : PIECE * (q + 1), :]
-            rows = pl.ds(pl.multiple_of(stride * (2 * c + which), SUB), size)
-            a_ref[rows, :] = ref[c, HEAD:, :].astype(f32)
+    size = sources[0].shape[0] - HEAD
+    for i, ref in enumerate(sources):
+        source = device ^ (2 * (i % GROUPS) + SUB * (i // GROUPS % 2) + i // (2 * GROUPS))
+        for q in range(4):
+            rows = pl.ds(pl.multiple_of(PIECE * source, PIECE), PIECE)
+            w2_ref[rows, LANE * q : LANE * (q + 1)] = ref[PIECE * q : PIECE * (q + 1), :]
+        a_ref[pl.ds(pl.multiple_of(stride * source, SUB), size), :] = ref[HEAD:, :].astype(f32)
     for q in range(4):
         for r in range(4):
             one_ref[pl.ds(4 * devices * q + r, devices, stride=4), :] = a_ref[pl.ds(4 * q + r, devices, stride=stride), :]
     one = jnp.concatenate([one_ref[4 * devices * q : 4 * devices * (q + 1), :] for q in range(4)], axis=1)
     lanes = lax.broadcasted_iota(jnp.int32, (4, LANE), 1)
     for t in range(devices // 4):
-        packed = [a_ref[pl.ds(stride * (4 * t + s) + 16 + 6 * half, 4), :] for s in range(4)]
+        packed = [a_ref[stride * (4 * t + s) + 16 : stride * (4 * t + s) + 20, :] for s in range(4)]
         for q in range(4):
             tile = jnp.zeros((4, LANE), f32)
             for s in range(4):
@@ -328,7 +342,7 @@
     w3t = w3_ref[...].astype(bf16)
     w3 = w3_ref[...].T.astype(bf16)
     place, inverse = place_ref[...], inverse_ref[...]
-    order = [16 + piece * b + half * f + j for f in range(6) for b in range(2) for j in range(half)]
+    order = [24 + 6 * half * b + half * f + j for f in range(6) for b in range(2) for j in range(half)]
     raw = jnp.concatenate([a_ref[pl.ds(k, levels, stride=stride), :] for k in order], axis=1)
     ordered = jnp.dot(place, raw.astype(bf16), preferred_element_type=f32)
     star, density, vertical, diverg, pressure_adjoint, wind_adjoint = (
@@ -431,12 +445,10 @@
     levels = devices = level_order.shape[0]
     columns = neighbors.shape[1]
     rows = columns // LANE
-    chips = devices // 2
     blocks = rows // GROUPS
     width = blocks * LANE
     hidden = weight_two.shape[1]
     f32, bf16 = jnp.float32, jnp.bfloat16
-    same_core = [list(range(core, devices, 2)) for core in range(2)]
 
     def pad(count):
         return -(-count // SUB) * SUB
@@ -447,28 +459,34 @@
     def lanes(table):
         return table.reshape(table.shape[0], rows, LANE).transpose(1, 0, 2)
 
-    def exchange(blocks_of_chips):
-        return lax.all_to_all(blocks_of_chips, "slab", split_axis=0, concat_axis=0, tiled=True, axis_index_groups=same_core)
+    def swap(array, bits):
+        return lax.ppermute(array, "slab", [(i, i ^ bits) for i in range(devices)])
+
+    def among_groups(outgoing):
+        return [outgoing[0]] + [swap(outgoing[k], 2 * k) for k in range(1, GROUPS)]
 
     sources = (
         view(pressure), view(density), view(vertical_wind), horizontal_wind.reshape(2, rows, LANE), lanes(metric_terms),
         lanes(neighbors), weight_one, weight_two, weight_three.T, view(pressure_adjoint), view(wind_adjoint),
     )
-    piece, back = pad(4 + 3 * blocks), pad(4 + 3 * blocks)
-    send = call(
-        pack_kernel, "pack", shape((chips, TAIL + 2 * piece, LANE), bf16), len(sources),
+    piece, back = 3 * blocks, pad(4 + 3 * blocks)
+    one_group = (shape((FRONT + 2 * piece, LANE), bf16),) * GROUPS
+    all_groups = pltpu.VMEM((GROUPS * 2 * piece, LANE), f32)
+    whole, *near = call(
+        pack_kernel, "pack", (shape((FRONT + GROUPS * 2 * piece, LANE), bf16),) + one_group, len(sources),
         [pltpu.VMEM(source.shape, source.dtype) for source in sources]
-        + [pltpu.VMEM((16, LANE), f32), pltpu.VMEM((SUB * piece, LANE), f32), pltpu.SemaphoreType.DMA((len(sources),))],
+        + [pltpu.VMEM((16, LANE), f32), pltpu.VMEM((SUB * piece, LANE), f32), all_groups, pltpu.SemaphoreType.DMA((len(sources),))],
         pltpu.HBM,
     )(*(pltpu.with_memory_space_constraint(source, pltpu.HBM) for source in sources))
+    far = call(relay_kernel, "relay", one_group, 1, [all_groups])(swap(whole, SUB))
+    same_core = among_groups(near) + among_groups(far)
+    other_core = [swap(block, 1) for block in same_core]
     operators = call(
         operator_kernel, "operators", (shape((levels, levels), bf16), shape((levels, levels), f32), shape((levels, LANE), f32)), 3
     )(level_order.reshape(1, levels), stiffness.reshape(1, levels), coupling.reshape(1, levels))
-    mine = exchange(send)
-    other = lax.ppermute(mine, "slab", [(i, i ^ 1) for i in range(devices)])
     block = shape((TAIL + back, LANE), bf16)
     send_back = call(
-        column_kernel, "column_step", (block,) * GROUPS, 5,
+        column_kernel, "column_step", (block,) * GROUPS, 4 * GROUPS + 3,
         [
             pltpu.VMEM((devices * STRIDE, LANE), f32), pltpu.VMEM((16 * devices, LANE), f32),
             pltpu.VMEM((hidden, hidden), bf16), pltpu.VMEM((levels, hidden), f32), pltpu.VMEM((hidden, width), bf16),
@@ -476,10 +494,8 @@
             pltpu.VMEM((devices * back, LANE), f32), pltpu.VMEM((levels, LANE), f32),
             pltpu.VMEM((hidden, width), bf16), pltpu.VMEM((GROUPS * PIECE, width), bf16),
         ],
-    )(mine, other, *operators)
-    received = [send_back[0]] * GROUPS
-    for k in range(GROUPS - 1, 0, -1):
-        received[k] = lax.ppermute(send_back[k], "slab", [(i, i ^ (2 * k)) for i in range(devices)])
+    )(*same_core, *other_core, *operators)
+    received = among_groups(send_back)
     field_out = shape((rows, LANE), f32)
     new_pressure, new_wind, grad, first_grad, second_grad, third_grad = call(
         functools.partial(finish_kernel, 1.0 / math.sqrt(columns)), "finish",
@@ -488,7 +504,7 @@
             shape(weight_three.shape[::-1], f32),
         ),
         GROUPS,
-        [pltpu.VMEM((GROUPS * back, LANE), f32)],
+        [pltpu.VMEM((SUB * back, LANE), f32)],
     )(*received)
     return (
         new_pressure.reshape(1, columns), new_wind.reshape(1, columns), grad.reshape(1, columns),

time: 37.5 us -> 35.1 us (0.936)
  blocking collectives: 20.3 us -> 0 us
  starting transfers between devices: 3.56 us -> 14.6 us
  waiting for transfers between devices: 3.86 us -> 10.7 us
    all_to_all x1 -> x0, blocking collectives: 20.3 us -> none  [exchange(): lax.all_to_all(blocks_of_chips, 'slab', split_axis=0, concat_axis=0, tile...]
    ppermute x4 -> x18, starting transfers between devices: 3.56 us -> 14.6 us  [swap(): return lax.ppermute(array, 'slab', [(i, i ^ bits) for i in range(devices)])]
    ppermute x4 -> x18, waiting for transfers between devices: 3.86 us -> 10.7 us  [swap(): return lax.ppermute(array, 'slab', [(i, i ^ bits) for i in range(devices)])]
    pallas_call x2 -> x3, Pallas kernels: 7.48 us -> 7.42 us  [the longest x1 4.82 us: fast_body(): call(column_kernel, 'column_step', (block,) * GROUPS, 4 * GROUPS + 3, [pl...]
  transfers between devices with their start and end apart: 4 -> 18, of which waited for: 4 -> 10; matrix products, arithmetic and copies ran while one was open for 0% -> 0% of each run, Pallas kernels for 0% -> 0%
where the time goes in v8:
time: 35.1 us; the launch traced here: 34.9 us
  starting transfers between devices  14.6 us (42%)
  waiting for transfers between devices  10.7 us (30%)
  Pallas kernels  8.25 us (24%)
  between operations  0.72 us (2%)
  local copies, waits for them, and re-layouts  0.68 us (2%)
    ppermute x18, starting transfers between devices, swap(): return lax.ppermute(array, 'slab', [(i, i ^ bits) for i in range(devices)])  14.6 us
    ppermute x18, waiting for transfers between devices, swap(): return lax.ppermute(array, 'slab', [(i, i ^ bits) for i in range(devices)])  10.7 us
    pallas_call x1, Pallas kernels, fast_body(): call(column_kernel, 'column_step', (block,) * GROUPS, 4 * GROUPS + 3, [pl...  4.82 us
    pallas_call x1, Pallas kernels, fast_body(): call(pack_kernel, 'pack', (shape((FRONT + GROUPS * 2 * piece, LANE), bf16...  2.56 us
  transfers between devices with their start and end apart: 18, of which 10 were waited for; matrix products, arithmetic and copies ran while one was open for 0% of the time, Pallas kernels for 0%

profile of v8, /device:TPU:0, one launch (start us, length us, event | category | flops | bytes accessed | tf_op | source)
XLA Modules:
  0.0 34.9 jit_solution(15735939598314012038)
XLA Ops:
  0.6 2.6 %pack.1 = (bf16[440,128]{1,0:T(8,128)(2,1)S(1)}, bf16[224,128]{1,0:T(8,128)(2,1)S(1)}, bf16[224,128]{1,0:T(8,128)(2,1)S(1)}, bf16[224,128]{1,0:T(8,128)(2,1)S(1)}, bf16[224,128]{1,0:T(8,128)(2,1)S(1)}) custom-call(f32[48,128]{1,0:T(8,128)} %bitcast.26, f32[48,128]{1,0:T(8,128)} %bitcast.27, f32[48,128]{1,0:T(8,128)} %bitcast.28, f32[2,48,128]{2,1,0:T(8,128)} %bitcast.24, ...), custom_call_target="tpu_custom_call" | custom-call | tf_op jit(solution)/shard_map/pack/pallas_call | solution.py:475
  3.2 4.1 %collective-permute-start.3 = (bf16[440,128]{1,0:T(8,128)(2,1)S(1)}, bf16[440,128]{1,0:T(8,128)(2,1)S(1)}, u32[]{:S(2)}, u32[]{:S(2)}) collective-permute-start(bf16[440,128]{1,0:T(8,128)(2,1)S(1)} %get-tuple-element.32), channel_id=1, source_target_pairs={{0,8},{1,9},{2,10},{3,11},{4,12},{5,13},{6,14},{7,15},{8,0},{9,1},... | collective-permute-start | bytes 337928 | tf_op jit(solution)/shard_map/ppermute | solution.py:463
  7.3 1.5 %collective-permute-start = (bf16[224,128]{1,0:T(8,128)(2,1)S(1)}, bf16[224,128]{1,0:T(8,128)(2,1)S(1)}, u32[]{:S(2)}, u32[]{:S(2)}) collective-permute-start(bf16[224,128]{1,0:T(8,128)(2,1)S(1)} %get-tuple-element.29), channel_id=1, source_target_pairs={{0,2},{1,3},{2,0},{3,1},{4,6},{5,7},{6,4},{7,5},{8,10},{9,11},{10,... | collective-permute-start | bytes 172040 | tf_op jit(solution)/shard_map/ppermute | solution.py:463
  8.8 1.6 %collective-permute-start.1 = (bf16[224,128]{1,0:T(8,128)(2,1)S(1)}, bf16[224,128]{1,0:T(8,128)(2,1)S(1)}, u32[]{:S(2)}, u32[]{:S(2)}) collective-permute-start(bf16[224,128]{1,0:T(8,128)(2,1)S(1)} %get-tuple-element.30), channel_id=1, source_target_pairs={{0,4},{1,5},{2,6},{3,7},{4,0},{5,1},{6,2},{7,3},{8,12},{9,13},{10,... | collective-permute-start | bytes 172040 | tf_op jit(solution)/shard_map/ppermute | solution.py:463
  10.4 0.4 %collective-permute-start.2 = (bf16[224,128]{1,0:T(8,128)(2,1)S(1)}, bf16[224,128]{1,0:T(8,128)(2,1)S(1)}, u32[]{:S(2)}, u32[]{:S(2)}) collective-permute-start(bf16[224,128]{1,0:T(8,128)(2,1)S(1)} %get-tuple-element.31), channel_id=1, source_target_pairs={{0,6},{1,7},{2,4},{3,5},{4,2},{5,3},{6,0},{7,1},{8,14},{9,15},{10,... | collective-permute-start | bytes 172040 | tf_op jit(solution)/shard_map/ppermute | solution.py:463
  10.8 0.0 collective-permute-start.7
  10.8 0.7 %collective-permute-done.refs_1_ = bf16[224,128]{1,0:T(8,128)(2,1)S(1)} collective-permute-done((bf16[224,128]{1,0:T(8,128)(2,1)S(1)}, bf16[224,128]{1,0:T(8,128)(2,1)S(1)}, u32[]{:S(2)}, u32[]{:S(2)}) %collective-permute-start) | collective-permute-done | bytes 57376 | tf_op jit(solution)/shard_map/ppermute | solution.py:463
  11.5 0.0 collective-permute-start.8
  11.5 2.3 %collective-permute-done.1.refs_2_ = bf16[224,128]{1,0:T(8,128)(2,1)S(1)} collective-permute-done((bf16[224,128]{1,0:T(8,128)(2,1)S(1)}, bf16[224,128]{1,0:T(8,128)(2,1)S(1)}, u32[]{:S(2)}, u32[]{:S(2)}) %collective-permute-start.1) | collective-permute-done | bytes 57376 | tf_op jit(solution)/shard_map/ppermute | solution.py:463
  13.8 0.0 collective-permute-start.9
  13.8 0.0 collective-permute-done.3.whole_ref
  13.8 0.9 %collective-permute-start.4 = (bf16[224,128]{1,0:T(8,128)(2,1)S(1)}, bf16[224,128]{1,0:T(8,128)(2,1)S(1)}, u32[]{:S(2)}, u32[]{:S(2)}) collective-permute-start(bf16[224,128]{1,0:T(8,128)(2,1)S(1)} %get-tuple-element.34), channel_id=1, source_target_pairs={{0,2},{1,3},{2,0},{3,1},{4,6},{5,7},{6,4},{7,5},{8,10},{9,11},{10,... | collective-permute-start | bytes 172040 | tf_op jit(solution)/shard_map/ppermute | solution.py:463
  14.8 0.7 %collective-permute-done.2.refs_3_ = bf16[224,128]{1,0:T(8,128)(2,1)S(1)} collective-permute-done((bf16[224,128]{1,0:T(8,128)(2,1)S(1)}, bf16[224,128]{1,0:T(8,128)(2,1)S(1)}, u32[]{:S(2)}, u32[]{:S(2)}) %collective-permute-start.2) | collective-permute-done | bytes 57376 | tf_op jit(solution)/shard_map/ppermute | solution.py:463
  15.5 0.4 %collective-permute-start.5 = (bf16[224,128]{1,0:T(8,128)(2,1)S(1)}, bf16[224,128]{1,0:T(8,128)(2,1)S(1)}, u32[]{:S(2)}, u32[]{:S(2)}) collective-permute-start(bf16[224,128]{1,0:T(8,128)(2,1)S(1)} %get-tuple-element.35), channel_id=1, source_target_pairs={{0,4},{1,5},{2,6},{3,7},{4,0},{5,1},{6,2},{7,3},{8,12},{9,13},{10,... | collective-permute-start | bytes 172040 | tf_op jit(solution)/shard_map/ppermute | solution.py:463
  15.9 1.5 %collective-permute-start.6 = (bf16[224,128]{1,0:T(8,128)(2,1)S(1)}, bf16[224,128]{1,0:T(8,128)(2,1)S(1)}, u32[]{:S(2)}, u32[]{:S(2)}) collective-permute-start(bf16[224,128]{1,0:T(8,128)(2,1)S(1)} %get-tuple-element.36), channel_id=1, source_target_pairs={{0,6},{1,7},{2,4},{3,5},{4,2},{5,3},{6,0},{7,1},{8,14},{9,15},{10,... | collective-permute-start | bytes 172040 | tf_op jit(solution)/shard_map/ppermute | solution.py:463
  17.5 0.5 %collective-permute-start.11 = (bf16[224,128]{1,0:T(8,128)(2,1)S(1)}, bf16[224,128]{1,0:T(8,128)(2,1)S(1)}, u32[]{:S(2)}, u32[]{:S(2)}) collective-permute-start(bf16[224,128]{1,0:T(8,128)(2,1)S(1)} %get-tuple-element.33.refs_4_), channel_id=1, source_target_pairs={{0,1},{1,0},{2,3},{3,2},{4,5},{5,4},{6,7},{7,6},{8,9},{9,8},{10,11... | collective-permute-start | bytes 172040 | tf_op jit(solution)/shard_map/ppermute | solution.py:463
  18.0 0.3 collective-permute-done.4.refs_5_
  18.2 1.7 %collective-permute-done.5.refs_6_ = bf16[224,128]{1,0:T(8,128)(2,1)S(1)} collective-permute-done((bf16[224,128]{1,0:T(8,128)(2,1)S(1)}, bf16[224,128]{1,0:T(8,128)(2,1)S(1)}, u32[]{:S(2)}, u32[]{:S(2)}) %collective-permute-start.5) | collective-permute-done | bytes 57376 | tf_op jit(solution)/shard_map/ppermute | solution.py:463
  19.9 1.1 %collective-permute-done.6.refs_7_ = bf16[224,128]{1,0:T(8,128)(2,1)S(1)} collective-permute-done((bf16[224,128]{1,0:T(8,128)(2,1)S(1)}, bf16[224,128]{1,0:T(8,128)(2,1)S(1)}, u32[]{:S(2)}, u32[]{:S(2)}) %collective-permute-start.6) | collective-permute-done | bytes 57376 | tf_op jit(solution)/shard_map/ppermute | solution.py:463
  21.0 0.6 %copy-done = s32[16]{0:T(128)S(1)} copy-done((s32[16]{0:T(128)S(1)}, s32[16]{0:T(128)}, u32[]{:S(2)}) %copy-start) | copy-done | bytes 88
  21.6 0.0 copy-done.1
  21.7 0.0 copy-done.2
  21.7 0.1 operators.1
  21.9 0.4 %collective-permute-done.14.refs_15_ = bf16[224,128]{1,0:T(8,128)(2,1)S(1)} collective-permute-done((bf16[224,128]{1,0:T(8,128)(2,1)S(1)}, bf16[224,128]{1,0:T(8,128)(2,1)S(1)}, u32[]{:S(2)}, u32[]{:S(2)}) %collective-permute-start.14) | collective-permute-done | bytes 57376 | tf_op jit(solution)/shard_map/ppermute | solution.py:463
  22.2 4.8 %column_step.1 = (bf16[184,128]{1,0:T(8,128)(2,1)S(1)}, bf16[184,128]{1,0:T(8,128)(2,1)S(1)}, bf16[184,128]{1,0:T(8,128)(2,1)S(1)}, bf16[184,128]{1,0:T(8,128)(2,1)S(1)}) custom-call(bf16[224,128]{1,0:T(8,128)(2,1)S(1)} %get-tuple-element.28.refs_0_, bf16[224,128]{1,0:T(8,128)(2,1)S(1)} %collective-permute-done.refs_1_, ...), custom_call_target="tpu_custom_call" | custom-call | tf_op jit(solution)/shard_map/column_step/pallas_call | solution.py:488
  27.1 1.1 %collective-permute-start.15 = (bf16[184,128]{1,0:T(8,128)(2,1)S(1)}, bf16[184,128]{1,0:T(8,128)(2,1)S(1)}, u32[]{:S(2)}, u32[]{:S(2)}) collective-permute-start(bf16[184,128]{1,0:T(8,128)(2,1)S(1)} %get-tuple-element.41), channel_id=1, source_target_pairs={{0,2},{1,3},{2,0},{3,1},{4,6},{5,7},{6,4},{7,5},{8,10},{9,11},{10,... | collective-permute-start | bytes 141320 | tf_op jit(solution)/shard_map/ppermute | solution.py:463
  28.1 1.1 %collective-permute-start.16 = (bf16[184,128]{1,0:T(8,128)(2,1)S(1)}, bf16[184,128]{1,0:T(8,128)(2,1)S(1)}, u32[]{:S(2)}, u32[]{:S(2)}) collective-permute-start(bf16[184,128]{1,0:T(8,128)(2,1)S(1)} %get-tuple-element.42), channel_id=1, source_target_pairs={{0,4},{1,5},{2,6},{3,7},{4,0},{5,1},{6,2},{7,3},{8,12},{9,13},{10,... | collective-permute-start | bytes 141320 | tf_op jit(solution)/shard_map/ppermute | solution.py:463
  29.2 1.4 %collective-permute-start.17 = (bf16[184,128]{1,0:T(8,128)(2,1)S(1)}, bf16[184,128]{1,0:T(8,128)(2,1)S(1)}, u32[]{:S(2)}, u32[]{:S(2)}) collective-permute-start(bf16[184,128]{1,0:T(8,128)(2,1)S(1)} %get-tuple-element.43), channel_id=1, source_target_pairs={{0,6},{1,7},{2,4},{3,5},{4,2},{5,3},{6,0},{7,1},{8,14},{9,15},{10,... | collective-permute-start | bytes 141320 | tf_op jit(solution)/shard_map/ppermute | solution.py:463
  30.6 0.6 %collective-permute-done.15.r1_ref = bf16[184,128]{1,0:T(8,128)(2,1)S(1)} collective-permute-done((bf16[184,128]{1,0:T(8,128)(2,1)S(1)}, bf16[184,128]{1,0:T(8,128)(2,1)S(1)}, u32[]{:S(2)}, u32[]{:S(2)}) %collective-permute-start.15) | collective-permute-done | bytes 47136 | tf_op jit(solution)/shard_map/ppermute | solution.py:463
  31.2 1.0 %collective-permute-done.16.r2_ref = bf16[184,128]{1,0:T(8,128)(2,1)S(1)} collective-permute-done((bf16[184,128]{1,0:T(8,128)(2,1)S(1)}, bf16[184,128]{1,0:T(8,128)(2,1)S(1)}, u32[]{:S(2)}, u32[]{:S(2)}) %collective-permute-start.16) | collective-permute-done | bytes 47136 | tf_op jit(solution)/shard_map/ppermute | solution.py:463
  32.2 2.0 %collective-permute-done.17.r3_ref = bf16[184,128]{1,0:T(8,128)(2,1)S(1)} collective-permute-done((bf16[184,128]{1,0:T(8,128)(2,1)S(1)}, bf16[184,128]{1,0:T(8,128)(2,1)S(1)}, u32[]{:S(2)}, u32[]{:S(2)}) %collective-permute-start.17) | collective-permute-done | bytes 47136 | tf_op jit(solution)/shard_map/ppermute | solution.py:463
  34.2 0.7 %finish.1 = (f32[48,128]{1,0:T(8,128)}, f32[48,128]{1,0:T(8,128)}, f32[48,128]{1,0:T(8,128)}, f32[4,512]{1,0:T(4,128)}, f32[32,512]{1,0:T(8,128)}, /*index=5*/f32[16,32]{1,0:T(8,128)}) custom-call(bf16[184,128]{1,0:T(8,128)(2,1)S(1)} %get-tuple-element.40.r0_ref, bf16[184,128]{1,0:T(8,128)(2,1)S(1)} %collective-permute-done.15.r1_ref, ...), custom_call_target="tpu_custom_call" | custom-call | tf_op jit(solution)/shard_map/finish/pallas_call | solution.py:500
  (15 shorter events, 0.1 us)
Async XLA Ops:
  3.2 10.6 %collective-permute-start.3 = (bf16[440,128]{1,0:T(8,128)(2,1)S(1)}, bf16[440,128]{1,0:T(8,128)(2,1)S(1)}, u32[]{:S(2)}, u32[]{:S(2)}) collective-permute-start(bf16[440,128]{1,0:T(8,128)(2,1)S(1)} %get-tuple-element.32), channel_id=1, source_target_pairs={{0,8},{1,9},{2,10},{3,11},{4,12},{5,13},{6,14},{7,15},{8,0},{9,1},... | collective-permute-start | bytes 337928 | tf_op jit(solution)/shard_map/ppermute | solution.py:463
  7.3 4.2 %collective-permute-start = (bf16[224,128]{1,0:T(8,128)(2,1)S(1)}, bf16[224,128]{1,0:T(8,128)(2,1)S(1)}, u32[]{:S(2)}, u32[]{:S(2)}) collective-permute-start(bf16[224,128]{1,0:T(8,128)(2,1)S(1)} %get-tuple-element.29), channel_id=1, source_target_pairs={{0,2},{1,3},{2,0},{3,1},{4,6},{5,7},{6,4},{7,5},{8,10},{9,11},{10,... | collective-permute-start | bytes 172040 | tf_op jit(solution)/shard_map/ppermute | solution.py:463
  8.8 5.0 %collective-permute-start.1 = (bf16[224,128]{1,0:T(8,128)(2,1)S(1)}, bf16[224,128]{1,0:T(8,128)(2,1)S(1)}, u32[]{:S(2)}, u32[]{:S(2)}) collective-permute-start(bf16[224,128]{1,0:T(8,128)(2,1)S(1)} %get-tuple-element.30), channel_id=1, source_target_pairs={{0,4},{1,5},{2,6},{3,7},{4,0},{5,1},{6,2},{7,3},{8,12},{9,13},{10,... | collective-permute-start | bytes 172040 | tf_op jit(solution)/shard_map/ppermute | solution.py:463
  10.4 5.1 %collective-permute-start.2 = (bf16[224,128]{1,0:T(8,128)(2,1)S(1)}, bf16[224,128]{1,0:T(8,128)(2,1)S(1)}, u32[]{:S(2)}, u32[]{:S(2)}) collective-permute-start(bf16[224,128]{1,0:T(8,128)(2,1)S(1)} %get-tuple-element.31), channel_id=1, source_target_pairs={{0,6},{1,7},{2,4},{3,5},{4,2},{5,3},{6,0},{7,1},{8,14},{9,15},{10,... | collective-permute-start | bytes 172040 | tf_op jit(solution)/shard_map/ppermute | solution.py:463
  10.8 5.1 %collective-permute-start.7 = (bf16[224,128]{1,0:T(8,128)(2,1)S(1)}, bf16[224,128]{1,0:T(8,128)(2,1)S(1)}, u32[]{:S(2)}, u32[]{:S(2)}) collective-permute-start(bf16[224,128]{1,0:T(8,128)(2,1)S(1)} %get-tuple-element.28.refs_0_), channel_id=1, source_target_pairs={{0,1},{1,0},{2,3},{3,2},{4,5},{5,4},{6,7},{7,6},{8,9},{9,8},{10,11... | collective-permute-start | bytes 172040 | tf_op jit(solution)/shard_map/ppermute | solution.py:463
  11.5 6.0 %collective-permute-start.8 = (bf16[224,128]{1,0:T(8,128)(2,1)S(1)}, bf16[224,128]{1,0:T(8,128)(2,1)S(1)}, u32[]{:S(2)}, u32[]{:S(2)}) collective-permute-start(bf16[224,128]{1,0:T(8,128)(2,1)S(1)} %collective-permute-done.refs_1_), channel_id=1, source_target_pairs={{0,1},{1,0},{2,3},{3,2},{4,5},{5,4},{6,7},{7,6},{8,9},{9,8},{10,11... | collective-permute-start | bytes 172040 | tf_op jit(solution)/shard_map/ppermute | solution.py:463
  13.8 3.7 %collective-permute-start.9 = (bf16[224,128]{1,0:T(8,128)(2,1)S(1)}, bf16[224,128]{1,0:T(8,128)(2,1)S(1)}, u32[]{:S(2)}, u32[]{:S(2)}) collective-permute-start(bf16[224,128]{1,0:T(8,128)(2,1)S(1)} %collective-permute-done.1.refs_2_), channel_id=1, source_target_pairs={{0,1},{1,0},{2,3},{3,2},{4,5},{5,4},{6,7},{7,6},{8,9},{9,8},{10,11... | collective-permute-start | bytes 172040 | tf_op jit(solution)/shard_map/ppermute | solution.py:463
  13.8 4.4 %collective-permute-start.4 = (bf16[224,128]{1,0:T(8,128)(2,1)S(1)}, bf16[224,128]{1,0:T(8,128)(2,1)S(1)}, u32[]{:S(2)}, u32[]{:S(2)}) collective-permute-start(bf16[224,128]{1,0:T(8,128)(2,1)S(1)} %get-tuple-element.34), channel_id=1, source_target_pairs={{0,2},{1,3},{2,0},{3,1},{4,6},{5,7},{6,4},{7,5},{8,10},{9,11},{10,... | collective-permute-start | bytes 172040 | tf_op jit(solution)/shard_map/ppermute | solution.py:463
  15.5 4.5 %collective-permute-start.5 = (bf16[224,128]{1,0:T(8,128)(2,1)S(1)}, bf16[224,128]{1,0:T(8,128)(2,1)S(1)}, u32[]{:S(2)}, u32[]{:S(2)}) collective-permute-start(bf16[224,128]{1,0:T(8,128)(2,1)S(1)} %get-tuple-element.35), channel_id=1, source_target_pairs={{0,4},{1,5},{2,6},{3,7},{4,0},{5,1},{6,2},{7,3},{8,12},{9,13},{10,... | collective-permute-start | bytes 172040 | tf_op jit(solution)/shard_map/ppermute | solution.py:463
  15.9 5.1 %collective-permute-start.6 = (bf16[224,128]{1,0:T(8,128)(2,1)S(1)}, bf16[224,128]{1,0:T(8,128)(2,1)S(1)}, u32[]{:S(2)}, u32[]{:S(2)}) collective-permute-start(bf16[224,128]{1,0:T(8,128)(2,1)S(1)} %get-tuple-element.36), channel_id=1, source_target_pairs={{0,6},{1,7},{2,4},{3,5},{4,2},{5,3},{6,0},{7,1},{8,14},{9,15},{10,... | collective-permute-start | bytes 172040 | tf_op jit(solution)/shard_map/ppermute | solution.py:463
  17.5 4.4 %collective-permute-start.10 = (bf16[224,128]{1,0:T(8,128)(2,1)S(1)}, bf16[224,128]{1,0:T(8,128)(2,1)S(1)}, u32[]{:S(2)}, u32[]{:S(2)}) collective-permute-start(bf16[224,128]{1,0:T(8,128)(2,1)S(1)} %collective-permute-done.2.refs_3_), channel_id=1, source_target_pairs={{0,1},{1,0},{2,3},{3,2},{4,5},{5,4},{6,7},{7,6},{8,9},{9,8},{10,11... | collective-permute-start | bytes 172040 | tf_op jit(solution)/shard_map/ppermute | solution.py:463
  17.5 4.4 %collective-permute-start.11 = (bf16[224,128]{1,0:T(8,128)(2,1)S(1)}, bf16[224,128]{1,0:T(8,128)(2,1)S(1)}, u32[]{:S(2)}, u32[]{:S(2)}) collective-permute-start(bf16[224,128]{1,0:T(8,128)(2,1)S(1)} %get-tuple-element.33.refs_4_), channel_id=1, source_target_pairs={{0,1},{1,0},{2,3},{3,2},{4,5},{5,4},{6,7},{7,6},{8,9},{9,8},{10,11... | collective-permute-start | bytes 172040 | tf_op jit(solution)/shard_map/ppermute | solution.py:463
  18.2 3.6 %collective-permute-start.12 = (bf16[224,128]{1,0:T(8,128)(2,1)S(1)}, bf16[224,128]{1,0:T(8,128)(2,1)S(1)}, u32[]{:S(2)}, u32[]{:S(2)}) collective-permute-start(bf16[224,128]{1,0:T(8,128)(2,1)S(1)} %collective-permute-done.4.refs_5_), channel_id=1, source_target_pairs={{0,1},{1,0},{2,3},{3,2},{4,5},{5,4},{6,7},{7,6},{8,9},{9,8},{10,11... | collective-permute-start | bytes 172040 | tf_op jit(solution)/shard_map/ppermute | solution.py:463
  19.9 1.9 %collective-permute-start.13 = (bf16[224,128]{1,0:T(8,128)(2,1)S(1)}, bf16[224,128]{1,0:T(8,128)(2,1)S(1)}, u32[]{:S(2)}, u32[]{:S(2)}) collective-permute-start(bf16[224,128]{1,0:T(8,128)(2,1)S(1)} %collective-permute-done.5.refs_6_), channel_id=1, source_target_pairs={{0,1},{1,0},{2,3},{3,2},{4,5},{5,4},{6,7},{7,6},{8,9},{9,8},{10,11... | collective-permute-start | bytes 172040 | tf_op jit(solution)/shard_map/ppermute | solution.py:463
  21.0 1.2 %collective-permute-start.14 = (bf16[224,128]{1,0:T(8,128)(2,1)S(1)}, bf16[224,128]{1,0:T(8,128)(2,1)S(1)}, u32[]{:S(2)}, u32[]{:S(2)}) collective-permute-start(bf16[224,128]{1,0:T(8,128)(2,1)S(1)} %collective-permute-done.6.refs_7_), channel_id=1, source_target_pairs={{0,1},{1,0},{2,3},{3,2},{4,5},{5,4},{6,7},{7,6},{8,9},{9,8},{10,11... | collective-permute-start | bytes 172040 | tf_op jit(solution)/shard_map/ppermute | solution.py:463
  21.0 0.7 %copy-start = (s32[16]{0:T(128)S(1)}, s32[16]{0:T(128)}, u32[]{:S(2)}) copy-start(s32[16]{0:T(128)} %param.20) | copy-start | bytes 196
  21.0 0.7 %copy-start.1 = (f32[16]{0:T(128)S(1)}, f32[16]{0:T(128)}, u32[]{:S(2)}) copy-start(f32[16]{0:T(128)} %param.21) | copy-start | bytes 196
  21.0 0.7 %copy-start.2 = (f32[16]{0:T(128)S(1)}, f32[16]{0:T(128)}, u32[]{:S(2)}) copy-start(f32[16]{0:T(128)} %param.22) | copy-start | bytes 196
  27.1 4.1 %collective-permute-start.15 = (bf16[184,128]{1,0:T(8,128)(2,1)S(1)}, bf16[184,128]{1,0:T(8,128)(2,1)S(1)}, u32[]{:S(2)}, u32[]{:S(2)}) collective-permute-start(bf16[184,128]{1,0:T(8,128)(2,1)S(1)} %get-tuple-element.41), channel_id=1, source_target_pairs={{0,2},{1,3},{2,0},{3,1},{4,6},{5,7},{6,4},{7,5},{8,10},{9,11},{10,... | collective-permute-start | bytes 141320 | tf_op jit(solution)/shard_map/ppermute | solution.py:463
  28.1 4.1 %collective-permute-start.16 = (bf16[184,128]{1,0:T(8,128)(2,1)S(1)}, bf16[184,128]{1,0:T(8,128)(2,1)S(1)}, u32[]{:S(2)}, u32[]{:S(2)}) collective-permute-start(bf16[184,128]{1,0:T(8,128)(2,1)S(1)} %get-tuple-element.42), channel_id=1, source_target_pairs={{0,4},{1,5},{2,6},{3,7},{4,0},{5,1},{6,2},{7,3},{8,12},{9,13},{10,... | collective-permute-start | bytes 141320 | tf_op jit(solution)/shard_map/ppermute | solution.py:463
  29.2 5.0 %collective-permute-start.17 = (bf16[184,128]{1,0:T(8,128)(2,1)S(1)}, bf16[184,128]{1,0:T(8,128)(2,1)S(1)}, u32[]{:S(2)}, u32[]{:S(2)}) collective-permute-start(bf16[184,128]{1,0:T(8,128)(2,1)S(1)} %get-tuple-element.43), channel_id=1, source_target_pairs={{0,6},{1,7},{2,4},{3,5},{4,2},{5,3},{6,0},{7,1},{8,14},{9,15},{10,... | collective-permute-start | bytes 141320 | tf_op jit(solution)/shard_map/ppermute | solution.py:463

commit v9 on v8

--- a/solution.py
+++ b/solution.py
@@ -141,6 +141,7 @@
 LANE = 128
 SUB = 8
 STRIDE = 104
+NEIGHBORS = (0, 3, 2, 1)
 GROUPS = 4
 PIECE = 32
 HEAD = 4 * PIECE
@@ -318,7 +319,7 @@
     stride = a_ref.shape[0] // devices
     size = sources[0].shape[0] - HEAD
     for i, ref in enumerate(sources):
-        source = device ^ (2 * (i % GROUPS) + SUB * (i // GROUPS % 2) + i // (2 * GROUPS))
+        source = device ^ (2 * NEIGHBORS[i % GROUPS] + SUB * (i // GROUPS % 2) + i // (2 * GROUPS))
         for q in range(4):
             rows = pl.ds(pl.multiple_of(PIECE * source, PIECE), PIECE)
             w2_ref[rows, LANE * q : LANE * (q + 1)] = ref[PIECE * q : PIECE * (q + 1), :]
@@ -412,7 +413,7 @@
         out_ref[TAIL:, :] = y_ref[pl.ds(start, back), :].astype(bf16)
 
 
-def finish_kernel(scale, r0_ref, r1_ref, r2_ref, r3_ref, p_ref, w_ref, g_ref, one_ref, two_ref, three_ref, y_ref):
+def finish_kernel(scale, r0_ref, r3_ref, r2_ref, r1_ref, p_ref, w_ref, g_ref, one_ref, two_ref, three_ref, y_ref):
     received = (r0_ref, r1_ref, r2_ref, r3_ref)
     back = r0_ref.shape[0] - TAIL
     half = p_ref.shape[0] // SUB
@@ -462,8 +463,8 @@
     def swap(array, bits):
         return lax.ppermute(array, "slab", [(i, i ^ bits) for i in range(devices)])
 
-    def among_groups(outgoing):
-        return [outgoing[0]] + [swap(outgoing[k], 2 * k) for k in range(1, GROUPS)]
+    def among_groups(outgoing, order=range(GROUPS)):
+        return [outgoing[0]] + [swap(outgoing[k], 2 * k) for k in order[1:]]
 
     sources = (
         view(pressure), view(density), view(vertical_wind), horizontal_wind.reshape(2, rows, LANE), lanes(metric_terms),
@@ -479,7 +480,10 @@
         pltpu.HBM,
     )(*(pltpu.with_memory_space_constraint(source, pltpu.HBM) for source in sources))
     far = call(relay_kernel, "relay", one_group, 1, [all_groups])(swap(whole, SUB))
-    same_core = among_groups(near) + among_groups(far)
+    near = among_groups(near, NEIGHBORS)
+    far = among_groups(far, NEIGHBORS)
+    *near, far[1] = lax.optimization_barrier((*near, far[1]))
+    same_core = near + far
     other_core = [swap(block, 1) for block in same_core]
     operators = call(
         operator_kernel, "operators", (shape((levels, levels), bf16), shape((levels, levels), f32), shape((levels, LANE), f32)), 3
@@ -495,7 +499,7 @@
             pltpu.VMEM((hidden, width), bf16), pltpu.VMEM((GROUPS * PIECE, width), bf16),
         ],
     )(*same_core, *other_core, *operators)
-    received = among_groups(send_back)
+    received = among_groups(send_back, (0, 3, 2, 1))
     field_out = shape((rows, LANE), f32)
     new_pressure, new_wind, grad, first_grad, second_grad, third_grad = call(
         functools.partial(finish_kernel, 1.0 / math.sqrt(columns)), "finish",

time: 35.1 us -> 33.9 us (0.966)
  waiting for transfers between devices: 10.7 us -> 7.87 us
  starting transfers between devices: 14.6 us -> 16.2 us
    ppermute x18, waiting for transfers between devices: 10.7 us -> 7.87 us  [swap(): return lax.ppermute(array, 'slab', [(i, i ^ bits) for i in range(devices)])]
    ppermute x18, starting transfers between devices: 14.6 us -> 16.2 us  [swap(): return lax.ppermute(array, 'slab', [(i, i ^ bits) for i in range(devices)])]
  transfers between devices with their start and end apart: 18 -> 18, of which waited for: 10 -> 6; matrix products, arithmetic and copies ran while one was open for 0% -> 0% of each run, Pallas kernels for 0% -> 0%
where the time goes in v9:
time: 33.9 us; the launch traced here: 33.7 us
  starting transfers between devices  16.2 us (48%)
  Pallas kernels  8.24 us (24%)
  waiting for transfers between devices  7.87 us (23%)
  between operations  0.71 us (2%)
  local copies, waits for them, and re-layouts  0.68 us (2%)
    ppermute x18, starting transfers between devices, swap(): return lax.ppermute(array, 'slab', [(i, i ^ bits) for i in range(devices)])  16.2 us
    ppermute x18, waiting for transfers between devices, swap(): return lax.ppermute(array, 'slab', [(i, i ^ bits) for i in range(devices)])  7.87 us
    pallas_call x1, Pallas kernels, fast_body(): call(column_kernel, 'column_step', (block,) * GROUPS, 4 * GROUPS + 3, [pl...  4.81 us
    pallas_call x1, Pallas kernels, fast_body(): call(pack_kernel, 'pack', (shape((FRONT + GROUPS * 2 * piece, LANE), bf16...  2.56 us
    pallas_call x1, Pallas kernels, fast_body(): call(functools.partial(finish_kernel, 1.0 / math.sqrt(columns)), 'finish'...  0.7 us
    unnamed x6, local copies, waits for them, and re-layouts  0.68 us
  transfers between devices with their start and end apart: 18, of which 6 were waited for; matrix products, arithmetic and copies ran while one was open for 0% of the time, Pallas kernels for 0%

profile of v9, /device:TPU:0, one launch (start us, length us, event | category | flops | bytes accessed | tf_op | source)
XLA Modules:
  0.0 33.7 jit_solution(7272826775439209091)
XLA Ops:
  0.6 2.6 %pack.1 = (bf16[440,128]{1,0:T(8,128)(2,1)S(1)}, bf16[224,128]{1,0:T(8,128)(2,1)S(1)}, bf16[224,128]{1,0:T(8,128)(2,1)S(1)}, bf16[224,128]{1,0:T(8,128)(2,1)S(1)}, bf16[224,128]{1,0:T(8,128)(2,1)S(1)}) custom-call(f32[48,128]{1,0:T(8,128)} %bitcast.26, f32[48,128]{1,0:T(8,128)} %bitcast.27, f32[48,128]{1,0:T(8,128)} %bitcast.28, f32[2,48,128]{2,1,0:T(8,128)} %bitcast.24, ...), custom_call_target="tpu_custom_call" | custom-call | tf_op jit(solution)/shard_map/pack/pallas_call | solution.py:476
  3.2 4.1 %collective-permute-start.3 = (bf16[440,128]{1,0:T(8,128)(2,1)S(1)}, bf16[440,128]{1,0:T(8,128)(2,1)S(1)}, u32[]{:S(2)}, u32[]{:S(2)}) collective-permute-start(bf16[440,128]{1,0:T(8,128)(2,1)S(1)} %get-tuple-element.37), channel_id=1, source_target_pairs={{0,8},{1,9},{2,10},{3,11},{4,12},{5,13},{6,14},{7,15},{8,0},{9,1},... | collective-permute-start | bytes 337928 | tf_op jit(solution)/shard_map/ppermute | solution.py:464
  7.3 2.5 %collective-permute-start = (bf16[224,128]{1,0:T(8,128)(2,1)S(1)}, bf16[224,128]{1,0:T(8,128)(2,1)S(1)}, u32[]{:S(2)}, u32[]{:S(2)}) collective-permute-start(bf16[224,128]{1,0:T(8,128)(2,1)S(1)} %get-tuple-element.34), channel_id=1, source_target_pairs={{0,6},{1,7},{2,4},{3,5},{4,2},{5,3},{6,0},{7,1},{8,14},{9,15},{10,... | collective-permute-start | bytes 172040 | tf_op jit(solution)/shard_map/ppermute | solution.py:464
  9.8 0.4 %collective-permute-start.1 = (bf16[224,128]{1,0:T(8,128)(2,1)S(1)}, bf16[224,128]{1,0:T(8,128)(2,1)S(1)}, u32[]{:S(2)}, u32[]{:S(2)}) collective-permute-start(bf16[224,128]{1,0:T(8,128)(2,1)S(1)} %get-tuple-element.35), channel_id=1, source_target_pairs={{0,4},{1,5},{2,6},{3,7},{4,0},{5,1},{6,2},{7,3},{8,12},{9,13},{10,... | collective-permute-start | bytes 172040 | tf_op jit(solution)/shard_map/ppermute | solution.py:464
  10.3 0.5 %collective-permute-start.2 = (bf16[224,128]{1,0:T(8,128)(2,1)S(1)}, bf16[224,128]{1,0:T(8,128)(2,1)S(1)}, u32[]{:S(2)}, u32[]{:S(2)}) collective-permute-start(bf16[224,128]{1,0:T(8,128)(2,1)S(1)} %get-tuple-element.36), channel_id=1, source_target_pairs={{0,2},{1,3},{2,0},{3,1},{4,6},{5,7},{6,4},{7,5},{8,10},{9,11},{10,... | collective-permute-start | bytes 172040 | tf_op jit(solution)/shard_map/ppermute | solution.py:464
  10.8 2.1 %collective-permute-done.3.whole_ref = bf16[440,128]{1,0:T(8,128)(2,1)S(1)} collective-permute-done((bf16[440,128]{1,0:T(8,128)(2,1)S(1)}, bf16[440,128]{1,0:T(8,128)(2,1)S(1)}, u32[]{:S(2)}, u32[]{:S(2)}) %collective-permute-start.3) | collective-permute-done | bytes 112672 | tf_op jit(solution)/shard_map/ppermute | solution.py:464
  13.0 1.6 %collective-permute-start.4 = (bf16[224,128]{1,0:T(8,128)(2,1)S(1)}, bf16[224,128]{1,0:T(8,128)(2,1)S(1)}, u32[]{:S(2)}, u32[]{:S(2)}) collective-permute-start(bf16[224,128]{1,0:T(8,128)(2,1)S(1)} %get-tuple-element.38), channel_id=1, source_target_pairs={{0,6},{1,7},{2,4},{3,5},{4,2},{5,3},{6,0},{7,1},{8,14},{9,15},{10,... | collective-permute-start | bytes 172040 | tf_op jit(solution)/shard_map/ppermute | solution.py:464
  14.6 1.5 %collective-permute-start.5 = (bf16[224,128]{1,0:T(8,128)(2,1)S(1)}, bf16[224,128]{1,0:T(8,128)(2,1)S(1)}, u32[]{:S(2)}, u32[]{:S(2)}) collective-permute-start(bf16[224,128]{1,0:T(8,128)(2,1)S(1)} %get-tuple-element.45), channel_id=1, source_target_pairs={{0,4},{1,5},{2,6},{3,7},{4,0},{5,1},{6,2},{7,3},{8,12},{9,13},{10,... | collective-permute-start | bytes 172040 | tf_op jit(solution)/shard_map/ppermute | solution.py:464
  16.0 0.0 collective-permute-done.refs_1_
  16.0 0.5 %collective-permute-start.6 = (bf16[224,128]{1,0:T(8,128)(2,1)S(1)}, bf16[224,128]{1,0:T(8,128)(2,1)S(1)}, u32[]{:S(2)}, u32[]{:S(2)}) collective-permute-start(bf16[224,128]{1,0:T(8,128)(2,1)S(1)} %get-tuple-element.46), channel_id=1, source_target_pairs={{0,2},{1,3},{2,0},{3,1},{4,6},{5,7},{6,4},{7,5},{8,10},{9,11},{10,... | collective-permute-start | bytes 172040 | tf_op jit(solution)/shard_map/ppermute | solution.py:464
  16.5 0.0 collective-permute-done.1.refs_2_
  16.5 0.0 collective-permute-start.11
  16.5 0.0 collective-permute-done.2.refs_3_
  16.5 1.6 %collective-permute-done.4.refs_5_ = bf16[224,128]{1,0:T(8,128)(2,1)S(1)} collective-permute-done((bf16[224,128]{1,0:T(8,128)(2,1)S(1)}, bf16[224,128]{1,0:T(8,128)(2,1)S(1)}, u32[]{:S(2)}, u32[]{:S(2)}) %collective-permute-start.4) | collective-permute-done | bytes 57376 | tf_op jit(solution)/shard_map/ppermute | solution.py:464
  18.2 0.5 %collective-permute-start.8 = (bf16[224,128]{1,0:T(8,128)(2,1)S(1)}, bf16[224,128]{1,0:T(8,128)(2,1)S(1)}, u32[]{:S(2)}, u32[]{:S(2)}) collective-permute-start(bf16[224,128]{1,0:T(8,128)(2,1)S(1)} %collective-permute-done.refs_1_), channel_id=1, source_target_pairs={{0,1},{1,0},{2,3},{3,2},{4,5},{5,4},{6,7},{7,6},{8,9},{9,8},{10,11... | collective-permute-start | bytes 172040 | tf_op jit(solution)/shard_map/ppermute | solution.py:464
  18.7 0.1 collective-permute-done.5.refs_6_
  18.8 1.4 %collective-permute-done.6.refs_7_ = bf16[224,128]{1,0:T(8,128)(2,1)S(1)} collective-permute-done((bf16[224,128]{1,0:T(8,128)(2,1)S(1)}, bf16[224,128]{1,0:T(8,128)(2,1)S(1)}, u32[]{:S(2)}, u32[]{:S(2)}) %collective-permute-start.6) | collective-permute-done | bytes 57376 | tf_op jit(solution)/shard_map/ppermute | solution.py:464
  20.2 0.5 %collective-permute-start.12 = (bf16[224,128]{1,0:T(8,128)(2,1)S(1)}, bf16[224,128]{1,0:T(8,128)(2,1)S(1)}, u32[]{:S(2)}, u32[]{:S(2)}) collective-permute-start(bf16[224,128]{1,0:T(8,128)(2,1)S(1)} %collective-permute-done.4.refs_5_), channel_id=1, source_target_pairs={{0,1},{1,0},{2,3},{3,2},{4,5},{5,4},{6,7},{7,6},{8,9},{9,8},{10,11... | collective-permute-start | bytes 172040 | tf_op jit(solution)/shard_map/ppermute | solution.py:464
  20.7 0.1 collective-permute-start.13
  20.8 0.4 %collective-permute-start.14 = (bf16[224,128]{1,0:T(8,128)(2,1)S(1)}, bf16[224,128]{1,0:T(8,128)(2,1)S(1)}, u32[]{:S(2)}, u32[]{:S(2)}) collective-permute-start(bf16[224,128]{1,0:T(8,128)(2,1)S(1)} %collective-permute-done.6.refs_7_), channel_id=1, source_target_pairs={{0,1},{1,0},{2,3},{3,2},{4,5},{5,4},{6,7},{7,6},{8,9},{9,8},{10,11... | collective-permute-start | bytes 172040 | tf_op jit(solution)/shard_map/ppermute | solution.py:464
  21.3 0.6 %copy-done = s32[16]{0:T(128)S(1)} copy-done((s32[16]{0:T(128)S(1)}, s32[16]{0:T(128)}, u32[]{:S(2)}) %copy-start) | copy-done | bytes 88
  21.9 0.0 copy-done.1
  21.9 0.0 copy-done.2
  21.9 0.1 operators.1
  22.1 0.0 collective-permute-done.14.refs_15_
  22.1 4.8 %column_step.1 = (bf16[184,128]{1,0:T(8,128)(2,1)S(1)}, bf16[184,128]{1,0:T(8,128)(2,1)S(1)}, bf16[184,128]{1,0:T(8,128)(2,1)S(1)}, bf16[184,128]{1,0:T(8,128)(2,1)S(1)}) custom-call(bf16[224,128]{1,0:T(8,128)(2,1)S(1)} %get-tuple-element.39.refs_0_, bf16[224,128]{1,0:T(8,128)(2,1)S(1)} %collective-permute-done.refs_1_, ...), custom_call_target="tpu_custom_call" | custom-call | tf_op jit(solution)/shard_map/column_step/pallas_call | solution.py:492
  27.0 0.7 %collective-permute-start.15 = (bf16[184,128]{1,0:T(8,128)(2,1)S(1)}, bf16[184,128]{1,0:T(8,128)(2,1)S(1)}, u32[]{:S(2)}, u32[]{:S(2)}) collective-permute-start(bf16[184,128]{1,0:T(8,128)(2,1)S(1)} %get-tuple-element.51), channel_id=1, source_target_pairs={{0,6},{1,7},{2,4},{3,5},{4,2},{5,3},{6,0},{7,1},{8,14},{9,15},{10,... | collective-permute-start | bytes 141320 | tf_op jit(solution)/shard_map/ppermute | solution.py:464
  27.6 1.4 %collective-permute-start.16 = (bf16[184,128]{1,0:T(8,128)(2,1)S(1)}, bf16[184,128]{1,0:T(8,128)(2,1)S(1)}, u32[]{:S(2)}, u32[]{:S(2)}) collective-permute-start(bf16[184,128]{1,0:T(8,128)(2,1)S(1)} %get-tuple-element.52), channel_id=1, source_target_pairs={{0,4},{1,5},{2,6},{3,7},{4,0},{5,1},{6,2},{7,3},{8,12},{9,13},{10,... | collective-permute-start | bytes 141320 | tf_op jit(solution)/shard_map/ppermute | solution.py:464
  29.0 1.5 %collective-permute-start.17 = (bf16[184,128]{1,0:T(8,128)(2,1)S(1)}, bf16[184,128]{1,0:T(8,128)(2,1)S(1)}, u32[]{:S(2)}, u32[]{:S(2)}) collective-permute-start(bf16[184,128]{1,0:T(8,128)(2,1)S(1)} %get-tuple-element.53), channel_id=1, source_target_pairs={{0,2},{1,3},{2,0},{3,1},{4,6},{5,7},{6,4},{7,5},{8,10},{9,11},{10,... | collective-permute-start | bytes 141320 | tf_op jit(solution)/shard_map/ppermute | solution.py:464
  30.5 1.9 %collective-permute-done.15.r3_ref = bf16[184,128]{1,0:T(8,128)(2,1)S(1)} collective-permute-done((bf16[184,128]{1,0:T(8,128)(2,1)S(1)}, bf16[184,128]{1,0:T(8,128)(2,1)S(1)}, u32[]{:S(2)}, u32[]{:S(2)}) %collective-permute-start.15) | collective-permute-done | bytes 47136 | tf_op jit(solution)/shard_map/ppermute | solution.py:464
  32.4 0.7 %collective-permute-done.17.r1_ref = bf16[184,128]{1,0:T(8,128)(2,1)S(1)} collective-permute-done((bf16[184,128]{1,0:T(8,128)(2,1)S(1)}, bf16[184,128]{1,0:T(8,128)(2,1)S(1)}, u32[]{:S(2)}, u32[]{:S(2)}) %collective-permute-start.17) | collective-permute-done | bytes 47136 | tf_op jit(solution)/shard_map/ppermute | solution.py:464
  33.0 0.7 %finish.1 = (f32[48,128]{1,0:T(8,128)}, f32[48,128]{1,0:T(8,128)}, f32[48,128]{1,0:T(8,128)}, f32[4,512]{1,0:T(4,128)}, f32[32,512]{1,0:T(8,128)}, /*index=5*/f32[16,32]{1,0:T(8,128)}) custom-call(bf16[184,128]{1,0:T(8,128)(2,1)S(1)} %get-tuple-element.50.r0_ref, bf16[184,128]{1,0:T(8,128)(2,1)S(1)} %collective-permute-done.15.r3_ref, ...), custom_call_target="tpu_custom_call" | custom-call | tf_op jit(solution)/shard_map/finish/pallas_call | solution.py:504
  (15 shorter events, 0.1 us)
Async XLA Ops:
  3.2 9.7 %collective-permute-start.3 = (bf16[440,128]{1,0:T(8,128)(2,1)S(1)}, bf16[440,128]{1,0:T(8,128)(2,1)S(1)}, u32[]{:S(2)}, u32[]{:S(2)}) collective-permute-start(bf16[440,128]{1,0:T(8,128)(2,1)S(1)} %get-tuple-element.37), channel_id=1, source_target_pairs={{0,8},{1,9},{2,10},{3,11},{4,12},{5,13},{6,14},{7,15},{8,0},{9,1},... | collective-permute-start | bytes 337928 | tf_op jit(solution)/shard_map/ppermute | solution.py:464
  7.3 8.7 %collective-permute-start = (bf16[224,128]{1,0:T(8,128)(2,1)S(1)}, bf16[224,128]{1,0:T(8,128)(2,1)S(1)}, u32[]{:S(2)}, u32[]{:S(2)}) collective-permute-start(bf16[224,128]{1,0:T(8,128)(2,1)S(1)} %get-tuple-element.34), channel_id=1, source_target_pairs={{0,6},{1,7},{2,4},{3,5},{4,2},{5,3},{6,0},{7,1},{8,14},{9,15},{10,... | collective-permute-start | bytes 172040 | tf_op jit(solution)/shard_map/ppermute | solution.py:464
  9.8 6.7 %collective-permute-start.1 = (bf16[224,128]{1,0:T(8,128)(2,1)S(1)}, bf16[224,128]{1,0:T(8,128)(2,1)S(1)}, u32[]{:S(2)}, u32[]{:S(2)}) collective-permute-start(bf16[224,128]{1,0:T(8,128)(2,1)S(1)} %get-tuple-element.35), channel_id=1, source_target_pairs={{0,4},{1,5},{2,6},{3,7},{4,0},{5,1},{6,2},{7,3},{8,12},{9,13},{10,... | collective-permute-start | bytes 172040 | tf_op jit(solution)/shard_map/ppermute | solution.py:464
  10.3 6.3 %collective-permute-start.2 = (bf16[224,128]{1,0:T(8,128)(2,1)S(1)}, bf16[224,128]{1,0:T(8,128)(2,1)S(1)}, u32[]{:S(2)}, u32[]{:S(2)}) collective-permute-start(bf16[224,128]{1,0:T(8,128)(2,1)S(1)} %get-tuple-element.36), channel_id=1, source_target_pairs={{0,2},{1,3},{2,0},{3,1},{4,6},{5,7},{6,4},{7,5},{8,10},{9,11},{10,... | collective-permute-start | bytes 172040 | tf_op jit(solution)/shard_map/ppermute | solution.py:464
  13.0 5.2 %collective-permute-start.4 = (bf16[224,128]{1,0:T(8,128)(2,1)S(1)}, bf16[224,128]{1,0:T(8,128)(2,1)S(1)}, u32[]{:S(2)}, u32[]{:S(2)}) collective-permute-start(bf16[224,128]{1,0:T(8,128)(2,1)S(1)} %get-tuple-element.38), channel_id=1, source_target_pairs={{0,6},{1,7},{2,4},{3,5},{4,2},{5,3},{6,0},{7,1},{8,14},{9,15},{10,... | collective-permute-start | bytes 172040 | tf_op jit(solution)/shard_map/ppermute | solution.py:464
  14.6 4.2 %collective-permute-start.5 = (bf16[224,128]{1,0:T(8,128)(2,1)S(1)}, bf16[224,128]{1,0:T(8,128)(2,1)S(1)}, u32[]{:S(2)}, u32[]{:S(2)}) collective-permute-start(bf16[224,128]{1,0:T(8,128)(2,1)S(1)} %get-tuple-element.45), channel_id=1, source_target_pairs={{0,4},{1,5},{2,6},{3,7},{4,0},{5,1},{6,2},{7,3},{8,12},{9,13},{10,... | collective-permute-start | bytes 172040 | tf_op jit(solution)/shard_map/ppermute | solution.py:464
  16.0 4.2 %collective-permute-start.6 = (bf16[224,128]{1,0:T(8,128)(2,1)S(1)}, bf16[224,128]{1,0:T(8,128)(2,1)S(1)}, u32[]{:S(2)}, u32[]{:S(2)}) collective-permute-start(bf16[224,128]{1,0:T(8,128)(2,1)S(1)} %get-tuple-element.46), channel_id=1, source_target_pairs={{0,2},{1,3},{2,0},{3,1},{4,6},{5,7},{6,4},{7,5},{8,10},{9,11},{10,... | collective-permute-start | bytes 172040 | tf_op jit(solution)/shard_map/ppermute | solution.py:464
  16.5 3.7 %collective-permute-start.11 = (bf16[224,128]{1,0:T(8,128)(2,1)S(1)}, bf16[224,128]{1,0:T(8,128)(2,1)S(1)}, u32[]{:S(2)}, u32[]{:S(2)}) collective-permute-start(bf16[224,128]{1,0:T(8,128)(2,1)S(1)} %get-tuple-element.43.refs_4_), channel_id=1, source_target_pairs={{0,1},{1,0},{2,3},{3,2},{4,5},{5,4},{6,7},{7,6},{8,9},{9,8},{10,11... | collective-permute-start | bytes 172040 | tf_op jit(solution)/shard_map/ppermute | solution.py:464
  18.2 2.6 %collective-permute-start.7 = (bf16[224,128]{1,0:T(8,128)(2,1)S(1)}, bf16[224,128]{1,0:T(8,128)(2,1)S(1)}, u32[]{:S(2)}, u32[]{:S(2)}) collective-permute-start(bf16[224,128]{1,0:T(8,128)(2,1)S(1)} %get-tuple-element.39.refs_0_), channel_id=1, source_target_pairs={{0,1},{1,0},{2,3},{3,2},{4,5},{5,4},{6,7},{7,6},{8,9},{9,8},{10,11... | collective-permute-start | bytes 172040 | tf_op jit(solution)/shard_map/ppermute | solution.py:464
  18.2 2.6 %collective-permute-start.8 = (bf16[224,128]{1,0:T(8,128)(2,1)S(1)}, bf16[224,128]{1,0:T(8,128)(2,1)S(1)}, u32[]{:S(2)}, u32[]{:S(2)}) collective-permute-start(bf16[224,128]{1,0:T(8,128)(2,1)S(1)} %collective-permute-done.refs_1_), channel_id=1, source_target_pairs={{0,1},{1,0},{2,3},{3,2},{4,5},{5,4},{6,7},{7,6},{8,9},{9,8},{10,11... | collective-permute-start | bytes 172040 | tf_op jit(solution)/shard_map/ppermute | solution.py:464
  18.8 3.3 %collective-permute-start.9 = (bf16[224,128]{1,0:T(8,128)(2,1)S(1)}, bf16[224,128]{1,0:T(8,128)(2,1)S(1)}, u32[]{:S(2)}, u32[]{:S(2)}) collective-permute-start(bf16[224,128]{1,0:T(8,128)(2,1)S(1)} %collective-permute-done.1.refs_2_), channel_id=1, source_target_pairs={{0,1},{1,0},{2,3},{3,2},{4,5},{5,4},{6,7},{7,6},{8,9},{9,8},{10,11... | collective-permute-start | bytes 172040 | tf_op jit(solution)/shard_map/ppermute | solution.py:464
  20.2 1.9 %collective-permute-start.10 = (bf16[224,128]{1,0:T(8,128)(2,1)S(1)}, bf16[224,128]{1,0:T(8,128)(2,1)S(1)}, u32[]{:S(2)}, u32[]{:S(2)}) collective-permute-start(bf16[224,128]{1,0:T(8,128)(2,1)S(1)} %collective-permute-done.2.refs_3_), channel_id=1, source_target_pairs={{0,1},{1,0},{2,3},{3,2},{4,5},{5,4},{6,7},{7,6},{8,9},{9,8},{10,11... | collective-permute-start | bytes 172040 | tf_op jit(solution)/shard_map/ppermute | solution.py:464
  20.2 1.9 %collective-permute-start.12 = (bf16[224,128]{1,0:T(8,128)(2,1)S(1)}, bf16[224,128]{1,0:T(8,128)(2,1)S(1)}, u32[]{:S(2)}, u32[]{:S(2)}) collective-permute-start(bf16[224,128]{1,0:T(8,128)(2,1)S(1)} %collective-permute-done.4.refs_5_), channel_id=1, source_target_pairs={{0,1},{1,0},{2,3},{3,2},{4,5},{5,4},{6,7},{7,6},{8,9},{9,8},{10,11... | collective-permute-start | bytes 172040 | tf_op jit(solution)/shard_map/ppermute | solution.py:464
  20.7 1.4 %collective-permute-start.13 = (bf16[224,128]{1,0:T(8,128)(2,1)S(1)}, bf16[224,128]{1,0:T(8,128)(2,1)S(1)}, u32[]{:S(2)}, u32[]{:S(2)}) collective-permute-start(bf16[224,128]{1,0:T(8,128)(2,1)S(1)} %collective-permute-done.5.refs_6_), channel_id=1, source_target_pairs={{0,1},{1,0},{2,3},{3,2},{4,5},{5,4},{6,7},{7,6},{8,9},{9,8},{10,11... | collective-permute-start | bytes 172040 | tf_op jit(solution)/shard_map/ppermute | solution.py:464
  20.8 1.3 %collective-permute-start.14 = (bf16[224,128]{1,0:T(8,128)(2,1)S(1)}, bf16[224,128]{1,0:T(8,128)(2,1)S(1)}, u32[]{:S(2)}, u32[]{:S(2)}) collective-permute-start(bf16[224,128]{1,0:T(8,128)(2,1)S(1)} %collective-permute-done.6.refs_7_), channel_id=1, source_target_pairs={{0,1},{1,0},{2,3},{3,2},{4,5},{5,4},{6,7},{7,6},{8,9},{9,8},{10,11... | collective-permute-start | bytes 172040 | tf_op jit(solution)/shard_map/ppermute | solution.py:464
  21.3 0.7 %copy-start = (s32[16]{0:T(128)S(1)}, s32[16]{0:T(128)}, u32[]{:S(2)}) copy-start(s32[16]{0:T(128)} %param.20) | copy-start | bytes 196
  21.3 0.7 %copy-start.1 = (f32[16]{0:T(128)S(1)}, f32[16]{0:T(128)}, u32[]{:S(2)}) copy-start(f32[16]{0:T(128)} %param.21) | copy-start | bytes 196
  21.3 0.7 %copy-start.2 = (f32[16]{0:T(128)S(1)}, f32[16]{0:T(128)}, u32[]{:S(2)}) copy-start(f32[16]{0:T(128)} %param.22) | copy-start | bytes 196
  27.0 5.4 %collective-permute-start.15 = (bf16[184,128]{1,0:T(8,128)(2,1)S(1)}, bf16[184,128]{1,0:T(8,128)(2,1)S(1)}, u32[]{:S(2)}, u32[]{:S(2)}) collective-permute-start(bf16[184,128]{1,0:T(8,128)(2,1)S(1)} %get-tuple-element.51), channel_id=1, source_target_pairs={{0,6},{1,7},{2,4},{3,5},{4,2},{5,3},{6,0},{7,1},{8,14},{9,15},{10,... | collective-permute-start | bytes 141320 | tf_op jit(solution)/shard_map/ppermute | solution.py:464
  27.6 4.8 %collective-permute-start.16 = (bf16[184,128]{1,0:T(8,128)(2,1)S(1)}, bf16[184,128]{1,0:T(8,128)(2,1)S(1)}, u32[]{:S(2)}, u32[]{:S(2)}) collective-permute-start(bf16[184,128]{1,0:T(8,128)(2,1)S(1)} %get-tuple-element.52), channel_id=1, source_target_pairs={{0,4},{1,5},{2,6},{3,7},{4,0},{5,1},{6,2},{7,3},{8,12},{9,13},{10,... | collective-permute-start | bytes 141320 | tf_op jit(solution)/shard_map/ppermute | solution.py:464
  29.0 4.1 %collective-permute-start.17 = (bf16[184,128]{1,0:T(8,128)(2,1)S(1)}, bf16[184,128]{1,0:T(8,128)(2,1)S(1)}, u32[]{:S(2)}, u32[]{:S(2)}) collective-permute-start(bf16[184,128]{1,0:T(8,128)(2,1)S(1)} %get-tuple-element.53), channel_id=1, source_target_pairs={{0,2},{1,3},{2,0},{3,1},{4,6},{5,7},{6,4},{7,5},{8,10},{9,11},{10,... | collective-permute-start | bytes 141320 | tf_op jit(solution)/shard_map/ppermute | solution.py:464

commit v10 on v9

--- a/solution.py
+++ b/solution.py
@@ -479,15 +479,16 @@
         + [pltpu.VMEM((16, LANE), f32), pltpu.VMEM((SUB * piece, LANE), f32), all_groups, pltpu.SemaphoreType.DMA((len(sources),))],
         pltpu.HBM,
     )(*(pltpu.with_memory_space_constraint(source, pltpu.HBM) for source in sources))
-    far = call(relay_kernel, "relay", one_group, 1, [all_groups])(swap(whole, SUB))
+    operators = call(
+        operator_kernel, "operators", (shape((levels, levels), bf16), shape((levels, levels), f32), shape((levels, LANE), f32)), 3
+    )(level_order.reshape(1, levels), stiffness.reshape(1, levels), coupling.reshape(1, levels))
+    whole, *operators = lax.optimization_barrier((swap(whole, SUB), *operators))
+    far = call(relay_kernel, "relay", one_group, 1, [all_groups])(whole)
     near = among_groups(near, NEIGHBORS)
     far = among_groups(far, NEIGHBORS)
     *near, far[1] = lax.optimization_barrier((*near, far[1]))
     same_core = near + far
     other_core = [swap(block, 1) for block in same_core]
-    operators = call(
-        operator_kernel, "operators", (shape((levels, levels), bf16), shape((levels, levels), f32), shape((levels, LANE), f32)), 3
-    )(level_order.reshape(1, levels), stiffness.reshape(1, levels), coupling.reshape(1, levels))
     block = shape((TAIL + back, LANE), bf16)
     send_back = call(
         column_kernel, "column_step", (block,) * GROUPS, 4 * GROUPS + 3,

time: 33.9 us -> 33.9 us (level)
  transfers between devices with their start and end apart: 18 -> 18, of which waited for: 6 -> 10; matrix products, arithmetic and copies ran while one was open for 0% -> 0% of each run, Pallas kernels for 0% -> 0%
where the time goes in v10:
time: 33.9 us; the launch traced here: 33.7 us
  starting transfers between devices  16.2 us (48%)
  Pallas kernels  8.24 us (24%)
  waiting for transfers between devices  7.9 us (23%)
  local copies, waits for them, and re-layouts  0.68 us (2%)
  between operations  0.68 us (2%)
    ppermute x18, starting transfers between devices, swap(): return lax.ppermute(array, 'slab', [(i, i ^ bits) for i in range(devices)])  16.2 us
    ppermute x18, waiting for transfers between devices, swap(): return lax.ppermute(array, 'slab', [(i, i ^ bits) for i in range(devices)])  7.9 us
    pallas_call x1, Pallas kernels, fast_body(): call(column_kernel, 'column_step', (block,) * GROUPS, 4 * GROUPS + 3, [pl...  4.81 us
    pallas_call x1, Pallas kernels, fast_body(): call(pack_kernel, 'pack', (shape((FRONT + GROUPS * 2 * piece, LANE), bf16...  2.56 us
    pallas_call x1, Pallas kernels, fast_body(): call(functools.partial(finish_kernel, 1.0 / math.sqrt(columns)), 'finish'...  0.7 us
    unnamed x6, local copies, waits for them, and re-layouts  0.68 us
  transfers between devices with their start and end apart: 18, of which 10 were waited for; matrix products, arithmetic and copies ran while one was open for 0% of the time, Pallas kernels for 0%

profile of v10, /device:TPU:0, one launch (start us, length us, event | category | flops | bytes accessed | tf_op | source)
XLA Modules:
  0.0 33.7 jit_solution(16169952264877399695)
XLA Ops:
  0.6 2.6 %pack.1 = (bf16[440,128]{1,0:T(8,128)(2,1)S(1)}, bf16[224,128]{1,0:T(8,128)(2,1)S(1)}, bf16[224,128]{1,0:T(8,128)(2,1)S(1)}, bf16[224,128]{1,0:T(8,128)(2,1)S(1)}, bf16[224,128]{1,0:T(8,128)(2,1)S(1)}) custom-call(f32[48,128]{1,0:T(8,128)} %bitcast.26, f32[48,128]{1,0:T(8,128)} %bitcast.27, f32[48,128]{1,0:T(8,128)} %bitcast.28, f32[2,48,128]{2,1,0:T(8,128)} %bitcast.24, ...), custom_call_target="tpu_custom_call" | custom-call | tf_op jit(solution)/shard_map/pack/pallas_call | solution.py:476
  3.2 4.1 %collective-permute-start.3 = (bf16[440,128]{1,0:T(8,128)(2,1)S(1)}, bf16[440,128]{1,0:T(8,128)(2,1)S(1)}, u32[]{:S(2)}, u32[]{:S(2)}) collective-permute-start(bf16[440,128]{1,0:T(8,128)(2,1)S(1)} %get-tuple-element.41), channel_id=1, source_target_pairs={{0,8},{1,9},{2,10},{3,11},{4,12},{5,13},{6,14},{7,15},{8,0},{9,1},... | collective-permute-start | bytes 337928 | tf_op jit(solution)/shard_map/ppermute | solution.py:464
  7.3 2.5 %collective-permute-start = (bf16[224,128]{1,0:T(8,128)(2,1)S(1)}, bf16[224,128]{1,0:T(8,128)(2,1)S(1)}, u32[]{:S(2)}, u32[]{:S(2)}) collective-permute-start(bf16[224,128]{1,0:T(8,128)(2,1)S(1)} %get-tuple-element.38), channel_id=1, source_target_pairs={{0,6},{1,7},{2,4},{3,5},{4,2},{5,3},{6,0},{7,1},{8,14},{9,15},{10,... | collective-permute-start | bytes 172040 | tf_op jit(solution)/shard_map/ppermute | solution.py:464
  9.8 0.4 %collective-permute-start.1 = (bf16[224,128]{1,0:T(8,128)(2,1)S(1)}, bf16[224,128]{1,0:T(8,128)(2,1)S(1)}, u32[]{:S(2)}, u32[]{:S(2)}) collective-permute-start(bf16[224,128]{1,0:T(8,128)(2,1)S(1)} %get-tuple-element.39), channel_id=1, source_target_pairs={{0,4},{1,5},{2,6},{3,7},{4,0},{5,1},{6,2},{7,3},{8,12},{9,13},{10,... | collective-permute-start | bytes 172040 | tf_op jit(solution)/shard_map/ppermute | solution.py:464
  10.3 0.5 %collective-permute-start.2 = (bf16[224,128]{1,0:T(8,128)(2,1)S(1)}, bf16[224,128]{1,0:T(8,128)(2,1)S(1)}, u32[]{:S(2)}, u32[]{:S(2)}) collective-permute-start(bf16[224,128]{1,0:T(8,128)(2,1)S(1)} %get-tuple-element.40), channel_id=1, source_target_pairs={{0,2},{1,3},{2,0},{3,1},{4,6},{5,7},{6,4},{7,5},{8,10},{9,11},{10,... | collective-permute-start | bytes 172040 | tf_op jit(solution)/shard_map/ppermute | solution.py:464
  10.8 0.6 %copy-done = s32[16]{0:T(128)S(1)} copy-done((s32[16]{0:T(128)S(1)}, s32[16]{0:T(128)}, u32[]{:S(2)}) %copy-start) | copy-done | bytes 88
  11.5 0.0 copy-done.1
  11.5 0.0 copy-done.2
  11.5 0.1 operators.1
  11.6 1.3 %collective-permute-done.3.whole_ref = bf16[440,128]{1,0:T(8,128)(2,1)S(1)} collective-permute-done((bf16[440,128]{1,0:T(8,128)(2,1)S(1)}, bf16[440,128]{1,0:T(8,128)(2,1)S(1)}, u32[]{:S(2)}, u32[]{:S(2)}) %collective-permute-start.3) | collective-permute-done | bytes 112672 | tf_op jit(solution)/shard_map/ppermute | solution.py:464
  13.0 1.6 %collective-permute-start.4 = (bf16[224,128]{1,0:T(8,128)(2,1)S(1)}, bf16[224,128]{1,0:T(8,128)(2,1)S(1)}, u32[]{:S(2)}, u32[]{:S(2)}) collective-permute-start(bf16[224,128]{1,0:T(8,128)(2,1)S(1)} %get-tuple-element.46), channel_id=1, source_target_pairs={{0,6},{1,7},{2,4},{3,5},{4,2},{5,3},{6,0},{7,1},{8,14},{9,15},{10,... | collective-permute-start | bytes 172040 | tf_op jit(solution)/shard_map/ppermute | solution.py:464
  14.6 1.5 %collective-permute-start.5 = (bf16[224,128]{1,0:T(8,128)(2,1)S(1)}, bf16[224,128]{1,0:T(8,128)(2,1)S(1)}, u32[]{:S(2)}, u32[]{:S(2)}) collective-permute-start(bf16[224,128]{1,0:T(8,128)(2,1)S(1)} %get-tuple-element.53), channel_id=1, source_target_pairs={{0,4},{1,5},{2,6},{3,7},{4,0},{5,1},{6,2},{7,3},{8,12},{9,13},{10,... | collective-permute-start | bytes 172040 | tf_op jit(solution)/shard_map/ppermute | solution.py:464
  16.0 0.5 %collective-permute-start.6 = (bf16[224,128]{1,0:T(8,128)(2,1)S(1)}, bf16[224,128]{1,0:T(8,128)(2,1)S(1)}, u32[]{:S(2)}, u32[]{:S(2)}) collective-permute-start(bf16[224,128]{1,0:T(8,128)(2,1)S(1)} %get-tuple-element.54), channel_id=1, source_target_pairs={{0,2},{1,3},{2,0},{3,1},{4,6},{5,7},{6,4},{7,5},{8,10},{9,11},{10,... | collective-permute-start | bytes 172040 | tf_op jit(solution)/shard_map/ppermute | solution.py:464
  16.5 1.6 %collective-permute-done.4.refs_5_ = bf16[224,128]{1,0:T(8,128)(2,1)S(1)} collective-permute-done((bf16[224,128]{1,0:T(8,128)(2,1)S(1)}, bf16[224,128]{1,0:T(8,128)(2,1)S(1)}, u32[]{:S(2)}, u32[]{:S(2)}) %collective-permute-start.4) | collective-permute-done | bytes 57376 | tf_op jit(solution)/shard_map/ppermute | solution.py:464
  18.2 0.0 collective-permute-start.7
  18.2 0.5 %collective-permute-start.8 = (bf16[224,128]{1,0:T(8,128)(2,1)S(1)}, bf16[224,128]{1,0:T(8,128)(2,1)S(1)}, u32[]{:S(2)}, u32[]{:S(2)}) collective-permute-start(bf16[224,128]{1,0:T(8,128)(2,1)S(1)} %collective-permute-done.refs_1_), channel_id=1, source_target_pairs={{0,1},{1,0},{2,3},{3,2},{4,5},{5,4},{6,7},{7,6},{8,9},{9,8},{10,11... | collective-permute-start | bytes 172040 | tf_op jit(solution)/shard_map/ppermute | solution.py:464
  18.7 0.1 collective-permute-done.5.refs_6_
  18.8 1.4 %collective-permute-done.6.refs_7_ = bf16[224,128]{1,0:T(8,128)(2,1)S(1)} collective-permute-done((bf16[224,128]{1,0:T(8,128)(2,1)S(1)}, bf16[224,128]{1,0:T(8,128)(2,1)S(1)}, u32[]{:S(2)}, u32[]{:S(2)}) %collective-permute-start.6) | collective-permute-done | bytes 57376 | tf_op jit(solution)/shard_map/ppermute | solution.py:464
  20.2 0.5 %collective-permute-start.12 = (bf16[224,128]{1,0:T(8,128)(2,1)S(1)}, bf16[224,128]{1,0:T(8,128)(2,1)S(1)}, u32[]{:S(2)}, u32[]{:S(2)}) collective-permute-start(bf16[224,128]{1,0:T(8,128)(2,1)S(1)} %collective-permute-done.4.refs_5_), channel_id=1, source_target_pairs={{0,1},{1,0},{2,3},{3,2},{4,5},{5,4},{6,7},{7,6},{8,9},{9,8},{10,11... | collective-permute-start | bytes 172040 | tf_op jit(solution)/shard_map/ppermute | solution.py:464
  20.7 0.1 collective-permute-start.13
  20.8 0.4 %collective-permute-start.14 = (bf16[224,128]{1,0:T(8,128)(2,1)S(1)}, bf16[224,128]{1,0:T(8,128)(2,1)S(1)}, u32[]{:S(2)}, u32[]{:S(2)}) collective-permute-start(bf16[224,128]{1,0:T(8,128)(2,1)S(1)} %collective-permute-done.6.refs_7_), channel_id=1, source_target_pairs={{0,1},{1,0},{2,3},{3,2},{4,5},{5,4},{6,7},{7,6},{8,9},{9,8},{10,11... | collective-permute-start | bytes 172040 | tf_op jit(solution)/shard_map/ppermute | solution.py:464
  21.3 0.2 collective-permute-done.10.refs_11_
  21.5 0.2 collective-permute-done.12.refs_13_
  21.6 0.4 %collective-permute-done.13.refs_14_ = bf16[224,128]{1,0:T(8,128)(2,1)S(1)} collective-permute-done((bf16[224,128]{1,0:T(8,128)(2,1)S(1)}, bf16[224,128]{1,0:T(8,128)(2,1)S(1)}, u32[]{:S(2)}, u32[]{:S(2)}) %collective-permute-start.13) | collective-permute-done | bytes 57376 | tf_op jit(solution)/shard_map/ppermute | solution.py:464
  22.0 0.2 collective-permute-done.14.refs_15_
  22.1 4.8 %column_step.1 = (bf16[184,128]{1,0:T(8,128)(2,1)S(1)}, bf16[184,128]{1,0:T(8,128)(2,1)S(1)}, bf16[184,128]{1,0:T(8,128)(2,1)S(1)}, bf16[184,128]{1,0:T(8,128)(2,1)S(1)}) custom-call(bf16[224,128]{1,0:T(8,128)(2,1)S(1)} %get-tuple-element.47.refs_0_, bf16[224,128]{1,0:T(8,128)(2,1)S(1)} %collective-permute-done.refs_1_, ...), custom_call_target="tpu_custom_call" | custom-call | tf_op jit(solution)/shard_map/column_step/pallas_call | solution.py:493
  27.0 0.7 %collective-permute-start.15 = (bf16[184,128]{1,0:T(8,128)(2,1)S(1)}, bf16[184,128]{1,0:T(8,128)(2,1)S(1)}, u32[]{:S(2)}, u32[]{:S(2)}) collective-permute-start(bf16[184,128]{1,0:T(8,128)(2,1)S(1)} %get-tuple-element.59), channel_id=1, source_target_pairs={{0,6},{1,7},{2,4},{3,5},{4,2},{5,3},{6,0},{7,1},{8,14},{9,15},{10,... | collective-permute-start | bytes 141320 | tf_op jit(solution)/shard_map/ppermute | solution.py:464
  27.6 1.4 %collective-permute-start.16 = (bf16[184,128]{1,0:T(8,128)(2,1)S(1)}, bf16[184,128]{1,0:T(8,128)(2,1)S(1)}, u32[]{:S(2)}, u32[]{:S(2)}) collective-permute-start(bf16[184,128]{1,0:T(8,128)(2,1)S(1)} %get-tuple-element.60), channel_id=1, source_target_pairs={{0,4},{1,5},{2,6},{3,7},{4,0},{5,1},{6,2},{7,3},{8,12},{9,13},{10,... | collective-permute-start | bytes 141320 | tf_op jit(solution)/shard_map/ppermute | solution.py:464
  29.0 1.5 %collective-permute-start.17 = (bf16[184,128]{1,0:T(8,128)(2,1)S(1)}, bf16[184,128]{1,0:T(8,128)(2,1)S(1)}, u32[]{:S(2)}, u32[]{:S(2)}) collective-permute-start(bf16[184,128]{1,0:T(8,128)(2,1)S(1)} %get-tuple-element.61), channel_id=1, source_target_pairs={{0,2},{1,3},{2,0},{3,1},{4,6},{5,7},{6,4},{7,5},{8,10},{9,11},{10,... | collective-permute-start | bytes 141320 | tf_op jit(solution)/shard_map/ppermute | solution.py:464
  30.5 1.9 %collective-permute-done.15.r3_ref = bf16[184,128]{1,0:T(8,128)(2,1)S(1)} collective-permute-done((bf16[184,128]{1,0:T(8,128)(2,1)S(1)}, bf16[184,128]{1,0:T(8,128)(2,1)S(1)}, u32[]{:S(2)}, u32[]{:S(2)}) %collective-permute-start.15) | collective-permute-done | bytes 47136 | tf_op jit(solution)/shard_map/ppermute | solution.py:464
  32.4 0.7 %collective-permute-done.17.r1_ref = bf16[184,128]{1,0:T(8,128)(2,1)S(1)} collective-permute-done((bf16[184,128]{1,0:T(8,128)(2,1)S(1)}, bf16[184,128]{1,0:T(8,128)(2,1)S(1)}, u32[]{:S(2)}, u32[]{:S(2)}) %collective-permute-start.17) | collective-permute-done | bytes 47136 | tf_op jit(solution)/shard_map/ppermute | solution.py:464
  33.0 0.7 %finish.1 = (f32[48,128]{1,0:T(8,128)}, f32[48,128]{1,0:T(8,128)}, f32[48,128]{1,0:T(8,128)}, f32[4,512]{1,0:T(4,128)}, f32[32,512]{1,0:T(8,128)}, /*index=5*/f32[16,32]{1,0:T(8,128)}) custom-call(bf16[184,128]{1,0:T(8,128)(2,1)S(1)} %get-tuple-element.58.r0_ref, bf16[184,128]{1,0:T(8,128)(2,1)S(1)} %collective-permute-done.15.r3_ref, ...), custom_call_target="tpu_custom_call" | custom-call | tf_op jit(solution)/shard_map/finish/pallas_call | solution.py:505
  (15 shorter events, 0.1 us)
Async XLA Ops:
  3.2 9.7 %collective-permute-start.3 = (bf16[440,128]{1,0:T(8,128)(2,1)S(1)}, bf16[440,128]{1,0:T(8,128)(2,1)S(1)}, u32[]{:S(2)}, u32[]{:S(2)}) collective-permute-start(bf16[440,128]{1,0:T(8,128)(2,1)S(1)} %get-tuple-element.41), channel_id=1, source_target_pairs={{0,8},{1,9},{2,10},{3,11},{4,12},{5,13},{6,14},{7,15},{8,0},{9,1},... | collective-permute-start | bytes 337928 | tf_op jit(solution)/shard_map/ppermute | solution.py:464
  7.3 8.7 %collective-permute-start = (bf16[224,128]{1,0:T(8,128)(2,1)S(1)}, bf16[224,128]{1,0:T(8,128)(2,1)S(1)}, u32[]{:S(2)}, u32[]{:S(2)}) collective-permute-start(bf16[224,128]{1,0:T(8,128)(2,1)S(1)} %get-tuple-element.38), channel_id=1, source_target_pairs={{0,6},{1,7},{2,4},{3,5},{4,2},{5,3},{6,0},{7,1},{8,14},{9,15},{10,... | collective-permute-start | bytes 172040 | tf_op jit(solution)/shard_map/ppermute | solution.py:464
  9.8 6.7 %collective-permute-start.1 = (bf16[224,128]{1,0:T(8,128)(2,1)S(1)}, bf16[224,128]{1,0:T(8,128)(2,1)S(1)}, u32[]{:S(2)}, u32[]{:S(2)}) collective-permute-start(bf16[224,128]{1,0:T(8,128)(2,1)S(1)} %get-tuple-element.39), channel_id=1, source_target_pairs={{0,4},{1,5},{2,6},{3,7},{4,0},{5,1},{6,2},{7,3},{8,12},{9,13},{10,... | collective-permute-start | bytes 172040 | tf_op jit(solution)/shard_map/ppermute | solution.py:464
  10.3 6.3 %collective-permute-start.2 = (bf16[224,128]{1,0:T(8,128)(2,1)S(1)}, bf16[224,128]{1,0:T(8,128)(2,1)S(1)}, u32[]{:S(2)}, u32[]{:S(2)}) collective-permute-start(bf16[224,128]{1,0:T(8,128)(2,1)S(1)} %get-tuple-element.40), channel_id=1, source_target_pairs={{0,2},{1,3},{2,0},{3,1},{4,6},{5,7},{6,4},{7,5},{8,10},{9,11},{10,... | collective-permute-start | bytes 172040 | tf_op jit(solution)/shard_map/ppermute | solution.py:464
  10.8 0.7 %copy-start = (s32[16]{0:T(128)S(1)}, s32[16]{0:T(128)}, u32[]{:S(2)}) copy-start(s32[16]{0:T(128)} %param.20) | copy-start | bytes 196
  10.8 0.7 %copy-start.1 = (f32[16]{0:T(128)S(1)}, f32[16]{0:T(128)}, u32[]{:S(2)}) copy-start(f32[16]{0:T(128)} %param.21) | copy-start | bytes 196
  10.8 0.7 %copy-start.2 = (f32[16]{0:T(128)S(1)}, f32[16]{0:T(128)}, u32[]{:S(2)}) copy-start(f32[16]{0:T(128)} %param.22) | copy-start | bytes 196
  13.0 5.2 %collective-permute-start.4 = (bf16[224,128]{1,0:T(8,128)(2,1)S(1)}, bf16[224,128]{1,0:T(8,128)(2,1)S(1)}, u32[]{:S(2)}, u32[]{:S(2)}) collective-permute-start(bf16[224,128]{1,0:T(8,128)(2,1)S(1)} %get-tuple-element.46), channel_id=1, source_target_pairs={{0,6},{1,7},{2,4},{3,5},{4,2},{5,3},{6,0},{7,1},{8,14},{9,15},{10,... | collective-permute-start | bytes 172040 | tf_op jit(solution)/shard_map/ppermute | solution.py:464
  14.6 4.2 %collective-permute-start.5 = (bf16[224,128]{1,0:T(8,128)(2,1)S(1)}, bf16[224,128]{1,0:T(8,128)(2,1)S(1)}, u32[]{:S(2)}, u32[]{:S(2)}) collective-permute-start(bf16[224,128]{1,0:T(8,128)(2,1)S(1)} %get-tuple-element.53), channel_id=1, source_target_pairs={{0,4},{1,5},{2,6},{3,7},{4,0},{5,1},{6,2},{7,3},{8,12},{9,13},{10,... | collective-permute-start | bytes 172040 | tf_op jit(solution)/shard_map/ppermute | solution.py:464
  16.0 4.2 %collective-permute-start.6 = (bf16[224,128]{1,0:T(8,128)(2,1)S(1)}, bf16[224,128]{1,0:T(8,128)(2,1)S(1)}, u32[]{:S(2)}, u32[]{:S(2)}) collective-permute-start(bf16[224,128]{1,0:T(8,128)(2,1)S(1)} %get-tuple-element.54), channel_id=1, source_target_pairs={{0,2},{1,3},{2,0},{3,1},{4,6},{5,7},{6,4},{7,5},{8,10},{9,11},{10,... | collective-permute-start | bytes 172040 | tf_op jit(solution)/shard_map/ppermute | solution.py:464
  16.5 3.7 %collective-permute-start.11 = (bf16[224,128]{1,0:T(8,128)(2,1)S(1)}, bf16[224,128]{1,0:T(8,128)(2,1)S(1)}, u32[]{:S(2)}, u32[]{:S(2)}) collective-permute-start(bf16[224,128]{1,0:T(8,128)(2,1)S(1)} %get-tuple-element.51.refs_4_), channel_id=1, source_target_pairs={{0,1},{1,0},{2,3},{3,2},{4,5},{5,4},{6,7},{7,6},{8,9},{9,8},{10,11... | collective-permute-start | bytes 172040 | tf_op jit(solution)/shard_map/ppermute | solution.py:464
  18.2 2.6 %collective-permute-start.7 = (bf16[224,128]{1,0:T(8,128)(2,1)S(1)}, bf16[224,128]{1,0:T(8,128)(2,1)S(1)}, u32[]{:S(2)}, u32[]{:S(2)}) collective-permute-start(bf16[224,128]{1,0:T(8,128)(2,1)S(1)} %get-tuple-element.47.refs_0_), channel_id=1, source_target_pairs={{0,1},{1,0},{2,3},{3,2},{4,5},{5,4},{6,7},{7,6},{8,9},{9,8},{10,11... | collective-permute-start | bytes 172040 | tf_op jit(solution)/shard_map/ppermute | solution.py:464
  18.2 2.6 %collective-permute-start.8 = (bf16[224,128]{1,0:T(8,128)(2,1)S(1)}, bf16[224,128]{1,0:T(8,128)(2,1)S(1)}, u32[]{:S(2)}, u32[]{:S(2)}) collective-permute-start(bf16[224,128]{1,0:T(8,128)(2,1)S(1)} %collective-permute-done.refs_1_), channel_id=1, source_target_pairs={{0,1},{1,0},{2,3},{3,2},{4,5},{5,4},{6,7},{7,6},{8,9},{9,8},{10,11... | collective-permute-start | bytes 172040 | tf_op jit(solution)/shard_map/ppermute | solution.py:464
  18.8 2.5 %collective-permute-start.9 = (bf16[224,128]{1,0:T(8,128)(2,1)S(1)}, bf16[224,128]{1,0:T(8,128)(2,1)S(1)}, u32[]{:S(2)}, u32[]{:S(2)}) collective-permute-start(bf16[224,128]{1,0:T(8,128)(2,1)S(1)} %collective-permute-done.1.refs_2_), channel_id=1, source_target_pairs={{0,1},{1,0},{2,3},{3,2},{4,5},{5,4},{6,7},{7,6},{8,9},{9,8},{10,11... | collective-permute-start | bytes 172040 | tf_op jit(solution)/shard_map/ppermute | solution.py:464
  20.2 1.2 %collective-permute-start.10 = (bf16[224,128]{1,0:T(8,128)(2,1)S(1)}, bf16[224,128]{1,0:T(8,128)(2,1)S(1)}, u32[]{:S(2)}, u32[]{:S(2)}) collective-permute-start(bf16[224,128]{1,0:T(8,128)(2,1)S(1)} %collective-permute-done.2.refs_3_), channel_id=1, source_target_pairs={{0,1},{1,0},{2,3},{3,2},{4,5},{5,4},{6,7},{7,6},{8,9},{9,8},{10,11... | collective-permute-start | bytes 172040 | tf_op jit(solution)/shard_map/ppermute | solution.py:464
  20.2 1.4 %collective-permute-start.12 = (bf16[224,128]{1,0:T(8,128)(2,1)S(1)}, bf16[224,128]{1,0:T(8,128)(2,1)S(1)}, u32[]{:S(2)}, u32[]{:S(2)}) collective-permute-start(bf16[224,128]{1,0:T(8,128)(2,1)S(1)} %collective-permute-done.4.refs_5_), channel_id=1, source_target_pairs={{0,1},{1,0},{2,3},{3,2},{4,5},{5,4},{6,7},{7,6},{8,9},{9,8},{10,11... | collective-permute-start | bytes 172040 | tf_op jit(solution)/shard_map/ppermute | solution.py:464
  20.7 1.2 %collective-permute-start.13 = (bf16[224,128]{1,0:T(8,128)(2,1)S(1)}, bf16[224,128]{1,0:T(8,128)(2,1)S(1)}, u32[]{:S(2)}, u32[]{:S(2)}) collective-permute-start(bf16[224,128]{1,0:T(8,128)(2,1)S(1)} %collective-permute-done.5.refs_6_), channel_id=1, source_target_pairs={{0,1},{1,0},{2,3},{3,2},{4,5},{5,4},{6,7},{7,6},{8,9},{9,8},{10,11... | collective-permute-start | bytes 172040 | tf_op jit(solution)/shard_map/ppermute | solution.py:464
  20.8 1.3 %collective-permute-start.14 = (bf16[224,128]{1,0:T(8,128)(2,1)S(1)}, bf16[224,128]{1,0:T(8,128)(2,1)S(1)}, u32[]{:S(2)}, u32[]{:S(2)}) collective-permute-start(bf16[224,128]{1,0:T(8,128)(2,1)S(1)} %collective-permute-done.6.refs_7_), channel_id=1, source_target_pairs={{0,1},{1,0},{2,3},{3,2},{4,5},{5,4},{6,7},{7,6},{8,9},{9,8},{10,11... | collective-permute-start | bytes 172040 | tf_op jit(solution)/shard_map/ppermute | solution.py:464
  27.0 5.4 %collective-permute-start.15 = (bf16[184,128]{1,0:T(8,128)(2,1)S(1)}, bf16[184,128]{1,0:T(8,128)(2,1)S(1)}, u32[]{:S(2)}, u32[]{:S(2)}) collective-permute-start(bf16[184,128]{1,0:T(8,128)(2,1)S(1)} %get-tuple-element.59), channel_id=1, source_target_pairs={{0,6},{1,7},{2,4},{3,5},{4,2},{5,3},{6,0},{7,1},{8,14},{9,15},{10,... | collective-permute-start | bytes 141320 | tf_op jit(solution)/shard_map/ppermute | solution.py:464
  27.6 4.8 %collective-permute-start.16 = (bf16[184,128]{1,0:T(8,128)(2,1)S(1)}, bf16[184,128]{1,0:T(8,128)(2,1)S(1)}, u32[]{:S(2)}, u32[]{:S(2)}) collective-permute-start(bf16[184,128]{1,0:T(8,128)(2,1)S(1)} %get-tuple-element.60), channel_id=1, source_target_pairs={{0,4},{1,5},{2,6},{3,7},{4,0},{5,1},{6,2},{7,3},{8,12},{9,13},{10,... | collective-permute-start | bytes 141320 | tf_op jit(solution)/shard_map/ppermute | solution.py:464
  29.0 4.1 %collective-permute-start.17 = (bf16[184,128]{1,0:T(8,128)(2,1)S(1)}, bf16[184,128]{1,0:T(8,128)(2,1)S(1)}, u32[]{:S(2)}, u32[]{:S(2)}) collective-permute-start(bf16[184,128]{1,0:T(8,128)(2,1)S(1)} %get-tuple-element.61), channel_id=1, source_target_pairs={{0,2},{1,3},{2,0},{3,1},{4,6},{5,7},{6,4},{7,5},{8,10},{9,11},{10,... | collective-permute-start | bytes 141320 | tf_op jit(solution)/shard_map/ppermute | solution.py:464
